TPU v7x, 32 devices: a whole 2x2x4 slice. The times are simulated.
32 devices in a mesh: fsdp: 8 (over z, x), seq: 4 (over y, core).
Axes of the slice: x: 2, y: 2, z: 4, core: 2. Of those that a mesh axis runs over, the one named last changes fastest.
Arguments:
- tokens: bfloat16 [8192, 768], P(('fsdp', 'seq')), may hold values from -6 to 6
- norm_gains: float32 [2, 2, 768], P(None, None, ('fsdp', 'seq')), may hold values from 0.25 to 1.75
- norm_shifts: float32 [2, 2, 768], P(None, None, ('fsdp', 'seq')), may hold values from -1.5 to 1.5
- w_qkv: float32 [2, 768, 2304], P(None, ('fsdp', 'seq')), may hold values from -0.3125 to 0.3125
- w_out: float32 [2, 768, 768], P(None, ('fsdp', 'seq')), may hold values from -0.875 to 0.875
- w_up: float32 [2, 768, 3072], P(None, ('fsdp', 'seq')), may hold values from -0.21875 to 0.21875
- w_down: float32 [2, 3072, 768], P(None, ('fsdp', 'seq')), may hold values from -0.109375 to 0.109375
- out_grad: bfloat16 [8192, 768], P(('fsdp', 'seq')), may hold values from -6 to 6
- doc_lengths: int32 [8, 8], P('fsdp'), may hold values from 1 to 512, 1024 in all within a row
Outputs:
- outputs: bfloat16 [8192, 768], P(('fsdp', 'seq'))
- grad_tokens: bfloat16 [8192, 768], P(('fsdp', 'seq'))
- grad_norm_gains: float32 [2, 2, 768], P(None, None, ('fsdp', 'seq'))
- grad_attn_shifts: float32 [2, 768], P(None, ('fsdp', 'seq'))
- grad_ffn_shifts: float32 [2, 768], P(None, ('fsdp', 'seq'))
- grad_w_qkv: float32 [2, 768, 2304], P(None, ('fsdp', 'seq'))
- grad_w_out: float32 [2, 768, 768], P(None, ('fsdp', 'seq'))
- grad_w_up: float32 [2, 768, 3072], P(None, ('fsdp', 'seq'))
- grad_w_down: float32 [2, 3072, 768], P(None, ('fsdp', 'seq'))
Inputs may be any that keep to these rules, and one draw needn't show every extreme that they name: `doc_lengths`: the lengths of each stream add up to 1024; documents may cross from one device's tokens to the next.
All inputs are finite; a program needn't handle non-finite values.
Results may differ from a plain program's by a relative error of at most 0.023.
The roundings to bfloat16 on the way count: a program that leaves them out, or rounds other values in their place, can miss the bound.
Values may be sent and summed in bfloat16 or wider, within the bound.
No kernel may reach another device: no remote copies, remote signals or barrier semaphores. Data moves between devices by JAX's collectives and lax.ppermute only.
A program may use at most 256 MiB of HBM per device.

v0:
```python
import jax
import jax.numpy as jnp
from jax import lax
from jax.sharding import PartitionSpec as P

H = 12
HD = 64
LAYERS = 2


NORM_EPS = 1e-05
BRANCH_SCALE = 0.7071067811865476
MASKED = -1e30


def layer_norm(values, gain_row, shift_row):
    center = values - jnp.mean(values, axis=-1, keepdims=True)
    spread = jnp.mean(center * center, axis=-1, keepdims=True)
    return center * lax.rsqrt(spread + NORM_EPS) * gain_row + shift_row


def gelu_tanh(values):
    return (
        0.5
        * values
        * (1.0 + jnp.tanh(0.7978845608028654 * (values + 0.044715 * values * values * values)))
    )


def contract_rows(left_side, right_side):
    return lax.dot_general(
        left_side, right_side, (((0,), (0,)), ((), ())), preferred_element_type=jnp.float32
    )


def contract_cols(left_side, right_side):
    return lax.dot_general(
        left_side, right_side, (((1,), (1,)), ((), ())), preferred_element_type=jnp.float32
    )


def fetch_forward(norm_gains, norm_shifts, w_qkv, w_out, w_up, w_down, layer_index):
    return (
        lax.all_gather(
            norm_gains[layer_index].T.astype(jnp.bfloat16), ("fsdp", "seq"), axis=0, tiled=True
        ),
        lax.all_gather(
            norm_shifts[layer_index].T.astype(jnp.bfloat16), ("fsdp", "seq"), axis=0, tiled=True
        ),
        lax.all_gather(
            w_qkv[layer_index].astype(jnp.bfloat16), ("fsdp", "seq"), axis=0, tiled=True
        ),
        lax.all_gather(
            w_out[layer_index].astype(jnp.bfloat16), ("fsdp", "seq"), axis=0, tiled=True
        ),
        lax.all_gather(w_up[layer_index].astype(jnp.bfloat16), ("fsdp", "seq"), axis=0, tiled=True),
        lax.all_gather(
            w_down[layer_index].astype(jnp.bfloat16), ("fsdp", "seq"), axis=0, tiled=True
        ),
    )


def block_scores(
    query_block, keys_all, segment, query_seg, query_pos, key_index, block_rows, score_scale
):
    key_start = key_index * block_rows
    key_block = lax.dynamic_slice_in_dim(keys_all, key_start, block_rows, 0)
    scores = (
        jnp.einsum("qhd,khd->hqk", query_block, key_block, preferred_element_type=jnp.float32)
        * score_scale
    )
    key_pos = key_start + lax.iota(jnp.int32, block_rows)
    key_seg = lax.dynamic_slice_in_dim(segment, key_start, block_rows, 0)
    allowed = (query_pos[:, None] >= key_pos[None, :]) & (query_seg[:, None] == key_seg[None, :])
    return (scores, allowed[None])


def probabilities(scores, allowed, log_total):
    return jnp.exp(jnp.where(allowed, scores - log_total[:, :, None], MASKED))


def first_key():
    return 0


def attend_forward(queries, keys_all, values_all, segment, block_rows):
    length, local_heads, head_dim = queries.shape
    score_scale = head_dim ** (-0.5)
    outputs = []
    log_totals = []
    for block_index in range(length // block_rows):
        row_start = block_index * block_rows
        query_block = queries[row_start : row_start + block_rows]
        query_pos = row_start + lax.iota(jnp.int32, block_rows)
        query_seg = segment[row_start : row_start + block_rows]
        lowest = first_key()

        def stats_step(key_index, state_pair):
            running_max, running_sum = state_pair
            scores, allowed = block_scores(
                query_block,
                keys_all,
                segment,
                query_seg,
                query_pos,
                key_index,
                block_rows,
                score_scale,
            )
            masked = jnp.where(allowed, scores, MASKED)
            new_max = jnp.maximum(running_max, jnp.max(masked, axis=2))
            weights = jnp.where(allowed, jnp.exp(masked - new_max[:, :, None]), 0.0)
            new_sum = running_sum * jnp.exp(running_max - new_max) + jnp.sum(weights, axis=2)
            return (new_max, new_sum)

        start_state = (
            jnp.full((local_heads, block_rows), MASKED, jnp.float32),
            jnp.zeros((local_heads, block_rows), jnp.float32),
        )
        running_max, running_sum = lax.fori_loop(lowest, block_index + 1, stats_step, start_state)
        log_total = running_max + jnp.log(running_sum)

        def value_step(key_index, gathered):
            scores, allowed = block_scores(
                query_block,
                keys_all,
                segment,
                query_seg,
                query_pos,
                key_index,
                block_rows,
                score_scale,
            )
            weights_low = probabilities(scores, allowed, log_total).astype(jnp.bfloat16)
            value_block = lax.dynamic_slice_in_dim(
                values_all, key_index * block_rows, block_rows, 0
            )
            return gathered + jnp.einsum(
                "hqk,khd->qhd", weights_low, value_block, preferred_element_type=jnp.float32
            )

        result = lax.fori_loop(
            lowest,
            block_index + 1,
            value_step,
            jnp.zeros((block_rows, local_heads, head_dim), jnp.float32),
        )
        outputs.append(result)
        log_totals.append(log_total)
    return (jnp.concatenate(outputs, axis=0), log_totals)


def attend_backward(queries, keys_all, values_all, grad_out, segment, log_totals, block_rows):
    length, local_heads, head_dim = queries.shape
    score_scale = head_dim ** (-0.5)
    grad_queries = []
    grad_keys = jnp.zeros((length, local_heads, head_dim), jnp.float32)
    grad_values = jnp.zeros((length, local_heads, head_dim), jnp.float32)
    for block_index in range(length // block_rows):
        row_start = block_index * block_rows
        query_block = queries[row_start : row_start + block_rows]
        grad_block = grad_out[row_start : row_start + block_rows]
        query_pos = row_start + lax.iota(jnp.int32, block_rows)
        query_seg = segment[row_start : row_start + block_rows]
        log_total = log_totals[block_index]
        lowest = first_key()

        def delta_step(key_index, running):
            scores, allowed = block_scores(
                query_block,
                keys_all,
                segment,
                query_seg,
                query_pos,
                key_index,
                block_rows,
                score_scale,
            )
            weights = probabilities(scores, allowed, log_total)
            value_block = lax.dynamic_slice_in_dim(
                values_all, key_index * block_rows, block_rows, 0
            )
            grad_probs = jnp.einsum(
                "qhd,khd->hqk", grad_block, value_block, preferred_element_type=jnp.float32
            )
            return running + jnp.sum(weights * grad_probs, axis=2)

        delta_sum = lax.fori_loop(
            lowest, block_index + 1, delta_step, jnp.zeros((local_heads, block_rows), jnp.float32)
        )

        def grad_step(key_index, state_triple):
            grad_query, key_grads, value_grads = state_triple
            key_start = key_index * block_rows
            scores, allowed = block_scores(
                query_block,
                keys_all,
                segment,
                query_seg,
                query_pos,
                key_index,
                block_rows,
                score_scale,
            )
            weights = probabilities(scores, allowed, log_total)
            key_block = lax.dynamic_slice_in_dim(keys_all, key_start, block_rows, 0)
            value_block = lax.dynamic_slice_in_dim(values_all, key_start, block_rows, 0)
            grad_probs = jnp.einsum(
                "qhd,khd->hqk", grad_block, value_block, preferred_element_type=jnp.float32
            )
            grad_scores = (weights * (grad_probs - delta_sum[:, :, None])).astype(jnp.bfloat16)
            grad_query = (
                grad_query
                + jnp.einsum(
                    "hqk,khd->qhd", grad_scores, key_block, preferred_element_type=jnp.float32
                )
                * score_scale
            )
            key_part = (
                jnp.einsum(
                    "hqk,qhd->khd", grad_scores, query_block, preferred_element_type=jnp.float32
                )
                * score_scale
            )
            value_part = jnp.einsum(
                "hqk,qhd->khd",
                weights.astype(jnp.bfloat16),
                grad_block,
                preferred_element_type=jnp.float32,
            )
            key_grads = lax.dynamic_update_slice_in_dim(
                key_grads,
                lax.dynamic_slice_in_dim(key_grads, key_start, block_rows, 0) + key_part,
                key_start,
                0,
            )
            value_grads = lax.dynamic_update_slice_in_dim(
                value_grads,
                lax.dynamic_slice_in_dim(value_grads, key_start, block_rows, 0) + value_part,
                key_start,
                0,
            )
            return (grad_query, key_grads, value_grads)

        grad_query, grad_keys, grad_values = lax.fori_loop(
            lowest,
            block_index + 1,
            grad_step,
            (jnp.zeros((block_rows, local_heads, head_dim), jnp.float32), grad_keys, grad_values),
        )
        grad_queries.append(grad_query)
    return (jnp.concatenate(grad_queries, axis=0), grad_keys, grad_values)


def shards(tokens, norm_gains, norm_shifts, w_qkv, w_out, w_up, w_down, out_grad, doc_lengths):
    tok_rows, model_width = tokens.shape
    seq_count = lax.axis_size("seq")
    length = tok_rows * seq_count
    local_heads = H // seq_count
    group_cols = local_heads * HD
    block_rows = min(512, length)
    lengths_row = doc_lengths[0]
    starts = jnp.cumsum(lengths_row) - lengths_row
    positions = lax.iota(jnp.int32, length)
    segment = jnp.sum((positions[:, None] >= starts[None, :]).astype(jnp.int32), axis=1)
    hidden = tokens.astype(jnp.float32)
    saved_layers = []
    for layer_index in range(LAYERS):
        weights_low = fetch_forward(
            norm_gains, norm_shifts, w_qkv, w_out, w_up, w_down, layer_index
        )
        gain_rows = weights_low[0].T.astype(jnp.float32)
        shift_rows = weights_low[1].T.astype(jnp.float32)
        normed, first_pull = jax.vjp(layer_norm, hidden, gain_rows[0], shift_rows[0])
        normed_low = normed.astype(jnp.bfloat16)
        mixed_low = jnp.dot(normed_low, weights_low[2], preferred_element_type=jnp.float32).astype(
            jnp.bfloat16
        )
        head_rows = lax.all_to_all(
            mixed_low.reshape(tok_rows, 3, seq_count, group_cols),
            "seq",
            split_axis=2,
            concat_axis=0,
            tiled=True,
        )
        queries = head_rows[:, 0, 0].reshape(length, local_heads, HD)
        keys_all = head_rows[:, 1, 0].reshape(length, local_heads, HD)
        values_all = head_rows[:, 2, 0].reshape(length, local_heads, HD)
        attended, log_totals = attend_forward(queries, keys_all, values_all, segment, block_rows)
        attended_low = attended.reshape(length, 1, group_cols).astype(jnp.bfloat16)
        attended_tok = lax.all_to_all(
            attended_low, "seq", split_axis=0, concat_axis=1, tiled=True
        ).reshape(tok_rows, model_width)
        hidden = hidden + BRANCH_SCALE * jnp.dot(
            attended_tok, weights_low[3], preferred_element_type=jnp.float32
        )
        second, second_pull = jax.vjp(layer_norm, hidden, gain_rows[1], shift_rows[1])
        second_low = second.astype(jnp.bfloat16)
        upper_rows = jnp.dot(second_low, weights_low[4], preferred_element_type=jnp.float32)
        active, gelu_pull = jax.vjp(gelu_tanh, upper_rows)
        active_low = active.astype(jnp.bfloat16)
        hidden = hidden + BRANCH_SCALE * jnp.dot(
            active_low, weights_low[5], preferred_element_type=jnp.float32
        )
        kept_weights = weights_low
        saved_layers.append(
            (
                kept_weights,
                first_pull,
                normed_low,
                queries,
                keys_all,
                values_all,
                log_totals,
                attended_tok,
                second_pull,
                second_low,
                gelu_pull,
                active_low,
            )
        )
    outputs = hidden.astype(jnp.bfloat16)
    grad_hidden = out_grad.astype(jnp.float32)
    grad_layers = []
    for layer_index in reversed(range(LAYERS)):
        (
            kept_weights,
            first_pull,
            normed_low,
            queries,
            keys_all,
            values_all,
            log_totals,
            attended_tok,
            second_pull,
            second_low,
            gelu_pull,
            active_low,
        ) = saved_layers[layer_index]
        weights_low = kept_weights
        down_cot = (BRANCH_SCALE * grad_hidden).astype(jnp.bfloat16)
        grad_down = contract_rows(active_low, down_cot)
        grad_active = contract_cols(down_cot, weights_low[5])
        upper_cot = gelu_pull(grad_active)[0].astype(jnp.bfloat16)
        grad_up = contract_rows(second_low, upper_cot)
        second_cot = contract_cols(upper_cot, weights_low[4])
        back_hidden, gain_grad_b, shift_grad_b = second_pull(second_cot)
        grad_hidden = grad_hidden + back_hidden
        attn_cot = (BRANCH_SCALE * grad_hidden).astype(jnp.bfloat16)
        grad_proj = contract_rows(attended_tok, attn_cot)
        attended_cot = contract_cols(attn_cot, weights_low[3]).astype(jnp.bfloat16)
        grad_heads = lax.all_to_all(
            attended_cot.reshape(tok_rows, seq_count, group_cols),
            "seq",
            split_axis=1,
            concat_axis=0,
            tiled=True,
        ).reshape(length, local_heads, HD)
        grad_queries, grad_keys, grad_values = attend_backward(
            queries, keys_all, values_all, grad_heads, segment, log_totals, block_rows
        )
        stacked_cot = jnp.stack((grad_queries, grad_keys, grad_values), axis=1).reshape(
            length, 3, 1, group_cols
        )
        mixed_cot = lax.all_to_all(
            stacked_cot.astype(jnp.bfloat16), "seq", split_axis=0, concat_axis=2, tiled=True
        ).reshape(tok_rows, 3 * model_width)
        grad_mixed = contract_rows(normed_low, mixed_cot)
        normed_cot = contract_cols(mixed_cot, weights_low[2])
        back_hidden, gain_grad_a, shift_grad_a = first_pull(normed_cot)
        grad_hidden = grad_hidden + back_hidden
        grad_gains = jnp.stack((gain_grad_a, gain_grad_b), axis=1)
        grad_shifts = jnp.stack((shift_grad_a, shift_grad_b), axis=1)
        layer_grads = (
            lax.psum_scatter(grad_gains, ("fsdp", "seq"), scatter_dimension=0, tiled=True),
            lax.psum_scatter(grad_shifts, ("fsdp", "seq"), scatter_dimension=0, tiled=True),
            lax.psum_scatter(grad_mixed, ("fsdp", "seq"), scatter_dimension=0, tiled=True),
            lax.psum_scatter(grad_proj, ("fsdp", "seq"), scatter_dimension=0, tiled=True),
            lax.psum_scatter(grad_up, ("fsdp", "seq"), scatter_dimension=0, tiled=True),
            lax.psum_scatter(grad_down, ("fsdp", "seq"), scatter_dimension=0, tiled=True),
        )
        grad_layers.append(layer_grads)
    grad_layers = grad_layers[::-1]
    stacked_grads = tuple(
        (jnp.stack([layer_grads[member] for layer_grads in grad_layers]) for member in range(6))
    )
    gains_out = jnp.transpose(stacked_grads[0], (0, 2, 1))
    attn_shifts_out = stacked_grads[1][:, :, 0]
    ffn_shifts_out = stacked_grads[1][:, :, 1]
    return (
        outputs,
        grad_hidden.astype(jnp.bfloat16),
        gains_out,
        attn_shifts_out,
        ffn_shifts_out,
        stacked_grads[2],
        stacked_grads[3],
        stacked_grads[4],
        stacked_grads[5],
    )


def solution(mesh):
    placed = (
        P(("fsdp", "seq"), None),
        P(None, None, ("fsdp", "seq")),
        P(None, None, ("fsdp", "seq")),
        P(None, ("fsdp", "seq"), None),
        P(None, ("fsdp", "seq"), None),
        P(None, ("fsdp", "seq"), None),
        P(None, ("fsdp", "seq"), None),
        P(("fsdp", "seq"), None),
        P("fsdp", None),
    )
    return jax.shard_map(
        shards,
        mesh=mesh,
        in_specs=placed,
        out_specs=(
            P(("fsdp", "seq"), None),
            P(("fsdp", "seq"), None),
            P(None, None, ("fsdp", "seq")),
            P(None, ("fsdp", "seq")),
            P(None, ("fsdp", "seq")),
            P(None, ("fsdp", "seq"), None),
            P(None, ("fsdp", "seq"), None),
            P(None, ("fsdp", "seq"), None),
            P(None, ("fsdp", "seq"), None),
        ),
        check_vma=False,
    )
```

profile of v0, /device:TPU:0, one launch (start us, length us, event | category | flops | bytes accessed | tf_op | source)
XLA Modules:
  0.0 1610.6 jit_solution(1654424393687251802)
XLA Ops:
  15.5 43.4 %all-gather.9 = bf16[32,24,2]{1,2,0:T(2,128)(2,1)S(1)} all-gather(bf16[1,24,2]{1,2,0:T(2,128)(2,1)S(1)} %get-tuple-element.2159), channel_id=1, replica_groups=mesh['fsdp'=8,'seq'=4] {'fsdp','seq'}, dimensions={0}, use_global_device_ids=true | all-gather | bytes 3168 | tf_op jit(solution)/shard_map/all_gather | solution.py:47
  59.2 36.7 %all-gather.8 = bf16[32,24,2]{1,2,0:T(2,128)(2,1)S(1)} all-gather(bf16[1,24,2]{1,2,0:T(2,128)(2,1)S(1)} %get-tuple-element.2157), channel_id=1, replica_groups=mesh['fsdp'=8,'seq'=4] {'fsdp','seq'}, dimensions={0}, use_global_device_ids=true | all-gather | bytes 3168 | tf_op jit(solution)/shard_map/all_gather | solution.py:44
  106.5 16.7 %all-to-all-done = bf16[256,3,4,192]{0,3,1,2:T(8,128)(2,1)S(1)} async-done(((bf16[256,3,4,192]{0,3,1,2:T(8,128)(2,1)}), bf16[256,3,4,192]{0,3,1,2:T(8,128)(2,1)S(1)}, u32[]{:S(2)}, u32[]{:S(2)}) %all-to-all-start) | async-done | bytes 1179680 | tf_op jit(solution)/shard_map/all_to_all | solution.py:279
  125.1 9.2 while.78
  152.4 38.5 %all-gather.11 = bf16[32,24,2]{1,2,0:T(2,128)(2,1)S(1)} all-gather(bf16[1,24,2]{1,2,0:T(2,128)(2,1)S(1)} %get-tuple-element.2158), channel_id=1, replica_groups=mesh['fsdp'=8,'seq'=4] {'fsdp','seq'}, dimensions={0}, use_global_device_ids=true | all-gather | bytes 3168 | tf_op jit(solution)/shard_map/all_gather | solution.py:47
  191.1 36.9 %all-gather.10 = bf16[32,24,2]{1,2,0:T(2,128)(2,1)S(1)} all-gather(bf16[1,24,2]{1,2,0:T(2,128)(2,1)S(1)} %get-tuple-element.2156), channel_id=1, replica_groups=mesh['fsdp'=8,'seq'=4] {'fsdp','seq'}, dimensions={0}, use_global_device_ids=true | all-gather | bytes 3168 | tf_op jit(solution)/shard_map/all_gather | solution.py:44
  238.6 22.3 %all-gather.27.cloned.1.call-done = bf16[1,3072,768]{2,1,0:T(8,128)(2,1)} async-done(((bf16[1,96,768]{2,1,0:T(8,128)(2,1)}), bf16[1,3072,768]{2,1,0:T(8,128)(2,1)}) %all-gather.27.cloned.1.call-update) | async-done | bytes 4718608 | tf_op jit(solution)/shard_map/all_gather | solution.py:57
  266.5 55.5 %all-gather.29.cloned.1.call-done = bf16[1,768,2304]{2,1,0:T(8,128)(2,1)} async-done(((bf16[1,24,2304]{2,1,0:T(8,128)(2,1)}), bf16[1,768,2304]{2,1,0:T(8,128)(2,1)}) %all-gather.29.cloned.1.call-update) | async-done | bytes 3538960 | tf_op jit(solution)/shard_map/all_gather | solution.py:50
  330.7 16.0 all-to-all-done.2
  348.7 12.9 while.80
  382.0 13.1 all_to_all.126
  410.4 33.4 %all-gather.33.cloned.1.call-done = bf16[1,768,3072]{2,1,0:T(8,128)(2,1)} async-done(((bf16[1,24,3072]{2,1,0:T(8,128)(2,1)}), bf16[1,768,3072]{2,1,0:T(8,128)(2,1)}) %all-gather.33.cloned.1.call-update) | async-done | bytes 4718608 | tf_op jit(solution)/shard_map/all_gather | solution.py:56
  449.5 59.6 %all-gather.35.cloned.1.call-done = bf16[1,3072,768]{2,1,0:T(8,128)(2,1)} async-done(((bf16[1,96,768]{2,1,0:T(8,128)(2,1)}), bf16[1,3072,768]{2,1,0:T(8,128)(2,1)}) %all-gather.35.cloned.1.call-update) | async-done | bytes 4718608 | tf_op jit(solution)/shard_map/all_gather | solution.py:57
  553.6 16.9 %while.83 = (s32[]{:T(128)}, f32[512,3,64]{0,2,1:T(8,128)S(1)}, f32[1024,3,64]{0,2,1:T(8,128)S(1)}, f32[1024,3,64]{0,2,1:T(8,128)}, bf16[1024,3,64]{0,2,1:T(8,12...) while((s32[]{:T(128)}, f32[512,3,64]{0,2,1:T(8,128)S(1)}, ...), condition=%wide.region_33.34_spmd.clone, body=%wide.region_32.33_spmd.clone.sunk | while | flops 512558080 | bytes 55468580 | solution.py:245
  581.5 23.3 %all-to-all-done.5 = bf16[1024,3,1,192]{3,1,2,0:T(4,128)(2,1)S(1)} async-done(((bf16[1024,3,1,192]{3,1,2,0:T(4,128)(2,1)}), bf16[1024,3,1,192]{3,1,2,0:T(4,128)(2,1)S(1)}, u32[]{:S(2)}, u32[]{:S(2)}) %all-to-all-start.5) | async-done | bytes 1179680 | tf_op jit(solution)/shard_map/all_to_all | solution.py:365
  657.7 19.3 %while.85 = (s32[]{:T(128)}, f32[512,3,64]{0,2,1:T(8,128)S(1)}, f32[1024,3,64]{0,2,1:T(8,128)S(1)}, f32[1024,3,64]{0,2,1:T(8,128)}, bf16[1024,3,64]{0,2,1:T(8,12...) while((s32[]{:T(128)}, f32[512,3,64]{0,2,1:T(8,128)S(1)}, ...), condition=%wide.region_43.44_spmd.clone, body=%wide.region_42.43_spmd.clone.sunk | while | flops 512558080 | bytes 57041472 | solution.py:245
  680.6 29.1 %all_to_all.127 = bf16[1024,3,1,192]{3,1,2,0:T(4,128)(2,1)} all-to-all(bf16[1024,3,1,192]{3,1,2,0:T(4,128)(2,1)S(1)} %copy.291), channel_id=1, replica_groups=mesh['fsdp'=8,'seq'=4] {'seq'}, dimensions={0} | all-to-all | bytes 2359296 | tf_op jit(solution)/shard_map/all_to_all | solution.py:365
  760.1 39.7 %all-reduce.8 = (f32[768,2]{0,1:T(2,128)S(1)}, f32[768,2]{0,1:T(2,128)S(1)}, f32[768,2]{0,1:T(2,128)S(1)}, f32[768,2]{0,1:T(2,128)S(1)}) all-reduce(f32[768,2]{0,1:T(2,128)S(1)} %pad_maximum_fusion.11, f32[768,2]{0,1:T(2,128)S(1)} %pad_maximum_fusion.10, ...), channel_id=11, replica_groups=mesh['fsdp'=8,'seq'=4] {'fsdp','seq'}, use_global_device_ids=true, to_apply=%region_51.52.clone | all-reduce | flops 6144 | bytes 49152
  803.9 110.0 %reduce-scatter.15.cloned.1.call-done = f32[24,2304]{1,0:T(8,128)} async-done(((f32[768,2304]{1,0:T(8,128)}), f32[24,2304]{1,0:T(8,128)}) %reduce-scatter.15.cloned.1.call-update) | async-done | bytes 221200 | tf_op jit(solution)/shard_map/reduce_scatter | solution.py:377
  913.9 124.1 %reduce-scatter.13.cloned.1.call-done = f32[24,2304]{1,0:T(8,128)} async-done(((f32[768,2304]{1,0:T(8,128)}), f32[24,2304]{1,0:T(8,128)}) %reduce-scatter.13.cloned.1.call-update) | async-done | bytes 221200 | tf_op jit(solution)/shard_map/reduce_scatter | solution.py:377
  1039.8 139.2 %reduce-scatter.23.cloned.1.call-done = f32[24,3072]{1,0:T(8,128)} async-done(((f32[768,3072]{1,0:T(8,128)}), f32[24,3072]{1,0:T(8,128)}) %reduce-scatter.23.cloned.1.call-update) | async-done | bytes 294928 | tf_op jit(solution)/shard_map/reduce_scatter | solution.py:379
  1179.0 140.9 %reduce-scatter.21.cloned.1.call-done = f32[24,3072]{1,0:T(8,128)} async-done(((f32[768,3072]{1,0:T(8,128)}), f32[24,3072]{1,0:T(8,128)}) %reduce-scatter.21.cloned.1.call-update) | async-done | bytes 294928 | tf_op jit(solution)/shard_map/reduce_scatter | solution.py:379
  1321.8 139.0 %reduce-scatter.27.cloned.1.call-done = f32[96,768]{1,0:T(8,128)} async-done(((f32[3072,768]{1,0:T(8,128)}), f32[96,768]{1,0:T(8,128)}) %reduce-scatter.27.cloned.1.call-update) | async-done | bytes 294928 | tf_op jit(solution)/shard_map/reduce_scatter | solution.py:380
  1460.8 141.2 %reduce-scatter.25.cloned.1.call-done = f32[96,768]{1,0:T(8,128)} async-done(((f32[3072,768]{1,0:T(8,128)}), f32[96,768]{1,0:T(8,128)}) %reduce-scatter.25.cloned.1.call-update) | async-done | bytes 294928 | tf_op jit(solution)/shard_map/reduce_scatter | solution.py:380
  (718 shorter events, 361.7 us)
Async XLA Ops:
  7.2 89.4 %all-gather.21.cloned.1.call-start = ((), (), s32[]{:S(2)}) async-start(), calls=%async_computation.24 | async-start | bytes 3649536 | tf_op jit(solution)/shard_map/all_gather | solution.py:50
  9.1 221.6 %all-gather.23.cloned.1.call-start = ((), (), s32[]{:S(2)}) async-start(), calls=%async_computation.25 | async-start | bytes 1216512 | tf_op jit(solution)/shard_map/all_gather | solution.py:53
  10.7 222.2 %all-gather.25.cloned.1.call-start = ((), (), s32[]{:S(2)}) async-start(), calls=%async_computation.26 | async-start | bytes 4866048 | tf_op jit(solution)/shard_map/all_gather | solution.py:56
  12.7 248.2 %all-gather.27.cloned.1.call-start = ((), (), s32[]{:S(2)}) async-start(), calls=%async_computation.27 | async-start | bytes 4866048 | tf_op jit(solution)/shard_map/all_gather | solution.py:57
  13.5 308.4 %all-gather.29.cloned.1.call-start = ((), (), s32[]{:S(2)}) async-start(), calls=%async_computation.28 | async-start | bytes 3649536 | tf_op jit(solution)/shard_map/all_gather | solution.py:50
  14.1 391.8 %all-gather.31.cloned.1.call-start = ((), (), s32[]{:S(2)}) async-start(), calls=%async_computation.29 | async-start | bytes 1216512 | tf_op jit(solution)/shard_map/all_gather | solution.py:53
  14.7 429.0 %all-gather.33.cloned.1.call-start = ((), (), s32[]{:S(2)}) async-start(), calls=%async_computation.30 | async-start | bytes 4866048 | tf_op jit(solution)/shard_map/all_gather | solution.py:56
  96.2 136.8 %copy-start.82 = (f32[768]{0:T(1024)}, f32[768]{0:T(1024)S(1)}, u32[]{:S(2)}) copy-start(f32[768]{0:T(1024)S(1)} %get-tuple-element.2179) | copy-start | bytes 9220
  96.2 136.8 %copy-start.89 = (f32[768]{0:T(1024)}, f32[768]{0:T(1024)S(1)}, u32[]{:S(2)}) copy-start(f32[768]{0:T(1024)S(1)} %get-tuple-element.1952) | copy-start | bytes 9220
  101.7 21.4 %all-to-all-start = ((bf16[256,3,4,192]{0,3,1,2:T(8,128)(2,1)}), bf16[256,3,4,192]{0,3,1,2:T(8,128)(2,1)S(1)}, u32[]{:S(2)}, u32[]{:S(2)}) async-start(bf16[256,3,4,192]{0,3,1,2:T(8,128)(2,1)} %copy.259), calls=%async_computation | async-start | bytes 2359296 | tf_op jit(solution)/shard_map/all_to_all | solution.py:279
  148.2 80.8 %all-to-all-start.1 = ((bf16[4,2,24576]{2,1,0:T(2,128)(2,1)}), bf16[4,2,24576]{2,1,0:T(2,128)(2,1)S(1)}, u32[]{:S(2)}, u32[]{:S(2)}) async-start(bf16[4,2,24576]{2,1,0:T(2,128)(2,1)} %reshape.952), calls=%async_computation.1 | async-start | bytes 786432 | tf_op jit(solution)/shard_map/all_to_all | solution.py:291
  151.6 357.5 %all-gather.35.cloned.1.call-start = ((), (), s32[]{:S(2)}) async-start(), calls=%async_computation.31 | async-start | bytes 4866048 | tf_op jit(solution)/shard_map/all_gather | solution.py:57
  326.9 19.8 %all-to-all-start.2 = ((bf16[256,3,4,192]{0,3,1,2:T(8,128)(2,1)}), bf16[256,3,4,192]{0,3,1,2:T(8,128)(2,1)S(1)}, u32[]{:S(2)}, u32[]{:S(2)}) async-start(bf16[256,3,4,192]{0,3,1,2:T(8,128)(2,1)} %copy.270), calls=%async_computation.2 | async-start | bytes 2359296 | tf_op jit(solution)/shard_map/all_to_all | solution.py:279
  523.7 11.7 all-to-all-start.4
  575.5 29.4 %all-to-all-start.5 = ((bf16[1024,3,1,192]{3,1,2,0:T(4,128)(2,1)}), bf16[1024,3,1,192]{3,1,2,0:T(4,128)(2,1)S(1)}, u32[]{:S(2)}, u32[]{:S(2)}) async-start(bf16[1024,3,1,192]{3,1,2,0:T(4,128)(2,1)} %copy.282), calls=%async_computation.5 | async-start | bytes 4194304 | tf_op jit(solution)/shard_map/all_to_all | solution.py:365
  579.2 223.0 %reduce-scatter.19.cloned.1.call-start = ((), (), s32[]{:S(2)}) async-start(), calls=%async_computation.19 | async-start | bytes 2433024 | tf_op jit(solution)/shard_map/reduce_scatter | solution.py:378
  581.3 221.0 %reduce-scatter.17.cloned.1.call-start = ((), (), s32[]{:S(2)}) async-start(), calls=%async_computation.18 | async-start | bytes 2433024 | tf_op jit(solution)/shard_map/reduce_scatter | solution.py:378
  626.3 14.7 all-to-all-start.6
  630.4 283.5 %reduce-scatter.15.cloned.1.call-start = ((), (), s32[]{:S(2)}) async-start(), calls=%async_computation.17 | async-start | bytes 7299072 | tf_op jit(solution)/shard_map/reduce_scatter | solution.py:377
  635.9 402.1 %reduce-scatter.13.cloned.1.call-start = ((), (), s32[]{:S(2)}) async-start(), calls=%async_computation.16 | async-start | bytes 7299072 | tf_op jit(solution)/shard_map/reduce_scatter | solution.py:377
  718.1 460.9 %reduce-scatter.23.cloned.1.call-start = ((), (), s32[]{:S(2)}) async-start(), calls=%async_computation.21 | async-start | bytes 9732096 | tf_op jit(solution)/shard_map/reduce_scatter | solution.py:379
  726.0 594.0 %reduce-scatter.21.cloned.1.call-start = ((), (), s32[]{:S(2)}) async-start(), calls=%async_computation.20 | async-start | bytes 9732096 | tf_op jit(solution)/shard_map/reduce_scatter | solution.py:379
  733.7 727.2 %reduce-scatter.27.cloned.1.call-start = ((), (), s32[]{:S(2)}) async-start(), calls=%async_computation.23 | async-start | bytes 9732096 | tf_op jit(solution)/shard_map/reduce_scatter | solution.py:380
  742.4 859.6 %reduce-scatter.25.cloned.1.call-start = ((), (), s32[]{:S(2)}) async-start(), calls=%async_computation.22 | async-start | bytes 9732096 | tf_op jit(solution)/shard_map/reduce_scatter | solution.py:380
  (179 other events, 1476.3 us)
Sparse Core Ops, SparseCore 0:
  11.5 62.8 all-gather.20
  77.3 53.1 all-gather.22
  133.4 62.0 all-gather.24
  198.8 62.0 all-gather.26
  263.6 58.2 all-gather.28
  324.7 52.7 all-gather.30
  380.4 63.2 all-gather.32
  447.2 61.8 all-gather.34
  585.3 100.4 reduce-scatter.18
  691.0 98.6 reduce-scatter.16
  795.3 118.5 reduce-scatter.14
  919.4 118.5 reduce-scatter.12
  1043.9 135.0 reduce-scatter.22
  1184.8 135.1 reduce-scatter.20
  1325.7 135.0 reduce-scatter.26
  1466.6 135.3 reduce-scatter.24
where the time goes:
time: 1620 us; the launch traced here: 1610 us
  waiting for transfers between devices  1040 us (64%)
  blocking collectives  237 us (15%)
  matrix products  169 us (10%)
  local copies, waits for them, and re-layouts  81 us (5%)
  other arithmetic  45.2 us (3%)
  starting transfers between devices  24.4 us (2%)
  between operations  16.3 us (1%)
    reduce_scatter x2, waiting for transfers between devices, shards(): lax.psum_scatter(grad_down, ('fsdp', 'seq'), scatter_dimension=0, tiled=T...  280 us
    reduce_scatter x2, waiting for transfers between devices, shards(): lax.psum_scatter(grad_up, ('fsdp', 'seq'), scatter_dimension=0, tiled=True)  280 us
    reduce_scatter x2, waiting for transfers between devices, shards(): lax.psum_scatter(grad_mixed, ('fsdp', 'seq'), scatter_dimension=0, tiled=...  234 us
    all_gather x2, waiting for transfers between devices, fetch_forward(): lax.all_gather(w_down[layer_index].astype(jnp.bfloat16), ('fsdp', 'seq'),...  81.9 us
    all_gather x2, blocking collectives, fetch_forward(): lax.all_gather(norm_shifts[layer_index].T.astype(jnp.bfloat16), ('fsdp',...  81.8 us
    all_gather x2, blocking collectives, fetch_forward(): lax.all_gather(norm_gains[layer_index].T.astype(jnp.bfloat16), ('fsdp', '...  73.6 us
    all_gather x2, waiting for transfers between devices, fetch_forward(): lax.all_gather(w_qkv[layer_index].astype(jnp.bfloat16), ('fsdp', 'seq'),...  55.5 us
    dot_general x8, matrix products, contract_rows(): lax.dot_general(left_side, right_side, (((0,), (0,)), ((), ())), preferre...  42.1 us
  transfers between devices with their start and end apart: 22, of which 15 were waited for; matrix products, arithmetic and copies ran while one was open for 14% of the time, Pallas kernels for 0%

commit v1 on v0

v1 whole, which is shorter than its diff:
```python
import jax
import jax.numpy as jnp
from jax import lax
from jax.experimental import pallas as pl
from jax.experimental.pallas import tpu as pltpu
from jax.sharding import PartitionSpec as P

H = 12
HD = 64
LAYERS = 2
MAX_DOC = 512

NORM_EPS = 1e-05
BRANCH_SCALE = 0.7071067811865476
MASKED = -1e30
BF = jnp.bfloat16
F32 = jnp.float32
BOTH = ("fsdp", "seq")

RING_NEXT = (1, 3, 0, 2)
RING_PREV = (2, 0, 3, 1)


def pick(table, index):
    return jnp.array(table, jnp.int32)[index]


def swap_seq(values, bit):
    return lax.ppermute(values, "seq", [(s, s ^ bit) for s in range(4)])


def by_bit(bit, own, other):
    zero = bit == 0
    return jnp.where(zero, own, other), jnp.where(zero, other, own)


def gather_seq(rows):
    place = lax.axis_index("seq")
    far = swap_seq(rows, 2)
    pair = jnp.stack(by_bit(place // 2, rows, far))
    near = swap_seq(pair, 1)
    return jnp.stack(by_bit(place % 2, pair, near), axis=1).reshape(-1, rows.shape[-1])


def scatter_seq(partial):
    place = lax.axis_index("seq")
    y_bit, c_bit = place // 2, place % 2
    width = partial.shape[-1]
    parts = partial.reshape(2, 2, -1, width)
    sent = lax.dynamic_index_in_dim(parts, 1 - c_bit, 1, keepdims=False).astype(BF)
    kept = lax.dynamic_index_in_dim(parts, c_bit, 1, keepdims=False).astype(F32)
    half = kept + swap_seq(sent, 1).astype(F32)
    sent = lax.dynamic_index_in_dim(half, 1 - y_bit, 0, keepdims=False).astype(BF)
    kept = lax.dynamic_index_in_dim(half, y_bit, 0, keepdims=False)
    return kept + swap_seq(sent, 2).astype(F32)


def exchange_seq(parts):
    place = lax.axis_index("seq")
    y_bit, c_bit = place // 2, place % 2
    grid = parts.reshape((2, 2) + parts.shape[1:])
    kept, sent = by_bit(c_bit, grid[:, 0], grid[:, 1])
    half = jnp.stack(by_bit(c_bit, kept, swap_seq(sent, 1)), axis=1)
    kept, sent = by_bit(y_bit, half[0], half[1])
    return jnp.stack(by_bit(y_bit, kept, swap_seq(sent, 2))).reshape(parts.shape)


def gather_fsdp(block):
    count = lax.axis_size("fsdp")
    if count != 8:
        return lax.all_gather(block, "fsdp", axis=0, tiled=False)
    place = lax.axis_index("fsdp")
    line, side = place // 2, place % 2
    ring = [(f, 2 * RING_NEXT[f // 2] + f % 2) for f in range(8)]
    gathered = jnp.zeros((4,) + block.shape, block.dtype)
    source = line
    for step in range(4):
        gathered = lax.dynamic_update_index_in_dim(gathered, block, source, 0)
        if step < 3:
            block = lax.ppermute(block, "fsdp", ring)
            source = pick(RING_PREV, source)
    other = lax.ppermute(gathered, "fsdp", [(f, f ^ 1) for f in range(8)])
    return jnp.stack(by_bit(side, gathered, other), axis=1).reshape((8,) + block.shape)


def scatter_fsdp(blocks):
    count = lax.axis_size("fsdp")
    if count != 8:
        return lax.psum_scatter(blocks.astype(BF), "fsdp", scatter_dimension=0, tiled=False).astype(F32)
    place = lax.axis_index("fsdp")
    line, side = place // 2, place % 2
    ring = [(f, 2 * RING_NEXT[f // 2] + f % 2) for f in range(8)]
    grid = blocks.reshape((4, 2) + blocks.shape[1:])
    sent = lax.dynamic_index_in_dim(grid, 1 - side, 1, keepdims=False).astype(BF)
    kept = lax.dynamic_index_in_dim(grid, side, 1, keepdims=False).astype(F32)
    kept = kept + lax.ppermute(sent, "fsdp", [(f, f ^ 1) for f in range(8)]).astype(F32)
    owner = pick(RING_PREV, line)
    running = lax.dynamic_index_in_dim(kept, owner, 0, keepdims=False)
    for _ in range(3):
        running = lax.ppermute(running.astype(BF), "fsdp", ring).astype(F32)
        owner = pick(RING_PREV, owner)
        running = running + lax.dynamic_index_in_dim(kept, owner, 0, keepdims=False)
    return running


def turn(rows):
    moves = []
    for f in range(8):
        for s in range(4):
            moves.append((f * 4 + s, (2 * s + f % 2) * 4 + f // 2))
    return lax.ppermute(rows, BOTH, moves)


ROWS = 256


def allowed_pairs(first_ref, row_start, key_start, width):
    key_pos = key_start + lax.broadcasted_iota(jnp.int32, (ROWS, width), 1)
    query_pos = row_start + lax.broadcasted_iota(jnp.int32, (ROWS, width), 0)
    first = first_ref[pl.ds(row_start, ROWS), :]
    return (key_pos <= query_pos) & (key_pos >= first)


def key_window(row_start):
    key_start = max(0, row_start - (MAX_DOC + ROWS - 1) // ROWS * ROWS)
    return key_start, row_start + ROWS - key_start


def dot_t(left, right):
    return lax.dot_general(left, right, (((1,), (1,)), ((), ())), preferred_element_type=F32)


def t_dot(left, right):
    return lax.dot_general(left, right, (((0,), (0,)), ((), ())), preferred_element_type=F32)


def attend_kernel(first_ref, mixed_ref, out_ref, total_ref):
    length, group = out_ref.shape
    heads = group // HD
    scale = HD ** (-0.5)
    for row_start in range(0, length, ROWS):
        key_start, width = key_window(row_start)
        allowed = allowed_pairs(first_ref, row_start, key_start, width)
        outs = []
        totals = []
        for head in range(heads):
            at = head * HD
            query = mixed_ref[pl.ds(row_start, ROWS), pl.ds(at, HD)]
            keys = mixed_ref[pl.ds(key_start, width), pl.ds(group + at, HD)]
            values = mixed_ref[pl.ds(key_start, width), pl.ds(2 * group + at, HD)]
            scores = jnp.where(allowed, dot_t(query, keys) * scale, MASKED)
            top = jnp.max(scores, axis=1, keepdims=True)
            weights = jnp.exp(scores - top)
            total = jnp.sum(weights, axis=1, keepdims=True)
            low = (weights * (1.0 / total)).astype(BF)
            outs.append(jnp.dot(low, values, preferred_element_type=F32))
            totals.append(top + jnp.log(total))
        out_ref[pl.ds(row_start, ROWS), :] = jnp.concatenate(outs, axis=1).astype(BF)
        total_ref[pl.ds(row_start, ROWS), :] = jnp.concatenate(totals, axis=1)


def attend(first, mixed):
    length, wide = mixed.shape
    group = wide // 3
    return pl.pallas_call(
        attend_kernel,
        out_shape=(
            jax.ShapeDtypeStruct((length, group), BF),
            jax.ShapeDtypeStruct((length, group // HD), F32),
        ),
        compiler_params=pltpu.CompilerParams(vmem_limit_bytes=48 << 20),
        name="attend",
    )(first, mixed)


def attend_back_kernel(first_ref, mixed_ref, total_ref, cot_ref, out_ref, key_acc, value_acc):
    length, group = cot_ref.shape
    heads = group // HD
    scale = HD ** (-0.5)
    key_acc[...] = jnp.zeros_like(key_acc)
    value_acc[...] = jnp.zeros_like(value_acc)
    for row_start in range(0, length, ROWS):
        key_start, width = key_window(row_start)
        allowed = allowed_pairs(first_ref, row_start, key_start, width)
        query_grads = []
        key_grads = []
        value_grads = []
        for head in range(heads):
            at = head * HD
            query = mixed_ref[pl.ds(row_start, ROWS), pl.ds(at, HD)]
            keys = mixed_ref[pl.ds(key_start, width), pl.ds(group + at, HD)]
            values = mixed_ref[pl.ds(key_start, width), pl.ds(2 * group + at, HD)]
            cot = cot_ref[pl.ds(row_start, ROWS), pl.ds(at, HD)]
            total = total_ref[pl.ds(row_start, ROWS), pl.ds(head, 1)]
            scores = jnp.where(allowed, dot_t(query, keys) * scale - total, MASKED)
            probs = jnp.exp(scores)
            prob_cot = dot_t(cot, values)
            delta = jnp.sum(probs * prob_cot, axis=1, keepdims=True)
            score_cot = (probs * (prob_cot - delta)).astype(BF)
            query_grads.append(jnp.dot(score_cot, keys, preferred_element_type=F32) * scale)
            key_grads.append(t_dot(score_cot, query) * scale)
            value_grads.append(t_dot(probs.astype(BF), cot))
        out_ref[pl.ds(row_start, ROWS), pl.ds(0, group)] = jnp.concatenate(query_grads, axis=1).astype(BF)
        window = pl.ds(key_start, width)
        key_acc[window, :] += jnp.concatenate(key_grads, axis=1)
        value_acc[window, :] += jnp.concatenate(value_grads, axis=1)
    out_ref[:, pl.ds(group, group)] = key_acc[...].astype(BF)
    out_ref[:, pl.ds(2 * group, group)] = value_acc[...].astype(BF)


def attend_back(first, mixed, totals, cot):
    length, wide = mixed.shape
    group = wide // 3
    return pl.pallas_call(
        attend_back_kernel,
        out_shape=jax.ShapeDtypeStruct((length, wide), BF),
        scratch_shapes=[pltpu.VMEM((length, group), F32), pltpu.VMEM((length, group), F32)],
        compiler_params=pltpu.CompilerParams(vmem_limit_bytes=48 << 20),
        name="attend_back",
    )(first, mixed, totals, cot)


def norm_parts(values):
    center = values - jnp.mean(values, axis=-1, keepdims=True)
    inverse = lax.rsqrt(jnp.mean(center * center, axis=-1, keepdims=True) + NORM_EPS)
    return center * inverse, inverse


def norm_back(unit, inverse, gain, cot):
    scaled = cot * gain
    inner = scaled - jnp.mean(scaled, axis=-1, keepdims=True)
    inner = inner - unit * jnp.mean(scaled * unit, axis=-1, keepdims=True)
    return inner * inverse, jnp.sum(cot * unit, axis=0), jnp.sum(cot, axis=0)


def gelu_tanh(values):
    return 0.5 * values * (1.0 + jnp.tanh(0.7978845608028654 * (values + 0.044715 * values * values * values)))


def gelu_slope(values):
    square = values * values
    bent = jnp.tanh(0.7978845608028654 * (values + 0.044715 * values * square))
    inner = 0.7978845608028654 * (1.0 + 3.0 * 0.044715 * square)
    return 0.5 * (1.0 + bent) + 0.5 * values * (1.0 - bent * bent) * inner


def mul(left, right):
    return jnp.dot(left, right, preferred_element_type=F32)


def shards(tokens, norm_gains, norm_shifts, w_qkv, w_out, w_up, w_down, out_grad, doc_lengths):
    tok_rows, width = tokens.shape
    fsdp, seq = lax.axis_size("fsdp"), lax.axis_size("seq")
    ruled = fsdp == 8
    length = tok_rows * seq
    group = (H // seq) * HD
    piece = w_qkv.shape[1]
    inner = w_up.shape[2] // seq
    place = lax.axis_index("seq")

    ends = jnp.cumsum(doc_lengths[0])
    starts = ends - doc_lengths[0]
    positions = lax.iota(jnp.int32, length)
    first = jnp.max(jnp.where(positions[:, None] >= starts[None, :], starts[None, :], 0), axis=1, keepdims=True)

    def column_parts(layer):
        qkv = w_qkv[layer].astype(BF).reshape(piece, 3, seq, group).transpose(2, 0, 1, 3)
        up = w_up[layer].astype(BF).reshape(piece, seq, inner).transpose(1, 0, 2)
        return qkv.reshape(seq, piece, 3 * group), up

    def pad_cols(values, cols):
        return jnp.pad(values, [(0, 0)] * (values.ndim - 1) + [(0, cols - values.shape[-1])])

    norms = jnp.stack([norm_gains, norm_shifts]).astype(BF).reshape(1, 1, 8 * piece)
    qkv_parts = [None, None]
    up_parts = [None, None]
    for layer in range(LAYERS):
        qkv_parts[layer], up_parts[layer] = column_parts(layer)
    sent = jnp.concatenate([qkv_parts[0], jnp.broadcast_to(pad_cols(norms, 3 * group), (seq, 8, 3 * group))], axis=1)
    early = exchange_seq(sent).reshape(seq, piece + 8, 3 * group)
    early = gather_fsdp(early)
    qkv_low = [early[:, :, :piece].reshape(width, 3 * group), None]
    norm_low = early[:, :, piece, : 8 * piece].reshape(fsdp * seq, 2, LAYERS, 2, piece)
    norm_low = norm_low.transpose(1, 2, 3, 0, 4).reshape(2, LAYERS, 2, width).astype(F32)
    gains, shifts = norm_low[0], norm_low[1]

    later = jnp.concatenate([up_parts[0], pad_cols(qkv_parts[1], inner), up_parts[1]], axis=1)
    later = exchange_seq(later)
    rows_of = piece + w_down.shape[1]
    if ruled:
        turned = jnp.concatenate([w_out[0], w_down[0], w_out[1], w_down[1]]).astype(BF)
        turned = turn(turned)
        turned = [turned[:rows_of], turned[rows_of:]]

        def unturn(gathered):
            rest = gathered.shape[1:]
            return gathered.reshape((4, 2) + rest).transpose((1, 0) + tuple(range(2, 2 + len(rest)))).reshape(-1, rest[-1])

    out_low = [None, None]
    up_low = [None, None]
    down_low = [None, None]
    for layer in range(LAYERS):
        if layer == 0:
            cols = later[:, :piece].reshape(seq * piece, inner)
        else:
            cols = later[:, piece:].reshape(seq * 2 * piece, inner)
        taken = cols.shape[0]
        if ruled:
            cols = jnp.concatenate([cols, turned[layer]])
        cols = gather_fsdp(cols)
        if layer == 0:
            up_low[0] = cols[:, :taken].reshape(width, inner)
        else:
            both = cols[:, :taken].reshape(fsdp, seq, 2, piece, inner)
            qkv_low[1] = both[:, :, 0, :, : 3 * group].reshape(width, 3 * group)
            up_low[1] = both[:, :, 1].reshape(width, inner)
        if ruled:
            rows = cols[:, taken:]
            out_low[layer] = unturn(rows[:, :piece])
            down_low[layer] = unturn(rows[:, piece:])
        else:
            whole = lax.all_gather(w_out[layer].astype(BF), BOTH, axis=0, tiled=True)
            out_low[layer] = lax.dynamic_slice_in_dim(whole, place * group, group, 0)
            whole = lax.all_gather(w_down[layer].astype(BF), BOTH, axis=0, tiled=True)
            down_low[layer] = lax.dynamic_slice_in_dim(whole, place * inner, inner, 0)

    hidden = tokens.astype(F32)
    saved = []
    for layer in range(LAYERS):
        unit_a, inverse_a = norm_parts(hidden)
        normed_a = gather_seq((unit_a * gains[layer, 0] + shifts[layer, 0]).astype(BF))
        mixed = mul(normed_a, qkv_low[layer]).astype(BF)
        attended, totals = attend(first, mixed)
        hidden = hidden + BRANCH_SCALE * scatter_seq(mul(attended, out_low[layer]))
        unit_b, inverse_b = norm_parts(hidden)
        normed_b = gather_seq((unit_b * gains[layer, 1] + shifts[layer, 1]).astype(BF))
        upper = mul(normed_b, up_low[layer])
        active = gelu_tanh(upper).astype(BF)
        hidden = hidden + BRANCH_SCALE * scatter_seq(mul(active, down_low[layer]))
        saved.append((unit_a, inverse_a, normed_a, mixed, attended, totals, unit_b, inverse_b, normed_b, upper, active))
    outputs = hidden.astype(BF)

    cot = out_grad.astype(F32)
    norm_sums = []
    qkv_grads = [None, None]
    out_grads = [None, None]
    up_grads = [None, None]
    down_grads = [None, None]

    def cols_blocks(grad):
        return grad.reshape(fsdp, seq * piece, -1)

    def rows_blocks(grad):
        if not ruled:
            return None
        each = grad.shape[0] // 8
        return grad.reshape(2, 4, each, -1).transpose(1, 0, 2, 3).reshape(8, each, -1)

    def rows_whole(grad):
        spread = jnp.zeros((seq,) + grad.shape, BF)
        spread = lax.dynamic_update_index_in_dim(spread, grad.astype(BF), place, 0).reshape(seq * grad.shape[0], -1)
        return lax.psum_scatter(spread, BOTH, scatter_dimension=0, tiled=True).astype(F32)

    def reduce_blocks(parts):
        joined = scatter_fsdp(jnp.concatenate(parts, axis=1))
        taken = []
        at = 0
        for part in parts:
            taken.append(joined[at : at + part.shape[1]])
            at += part.shape[1]
        return taken

    pending = {}
    for layer in reversed(range(LAYERS)):
        unit_a, inverse_a, normed_a, mixed, attended, totals, unit_b, inverse_b, normed_b, upper, active = saved[layer]
        down_cot = gather_seq((BRANCH_SCALE * cot).astype(BF))
        grad_down = t_dot(active, down_cot)
        upper_cot = (gelu_slope(upper) * dot_t(down_cot, down_low[layer])).astype(BF)
        grad_up = t_dot(normed_b, upper_cot)
        second_cot = scatter_seq(dot_t(upper_cot, up_low[layer]))
        back, gain_sum_b, shift_sum_b = norm_back(unit_b, inverse_b, gains[layer, 1], second_cot)
        cot = cot + back
        attn_cot = gather_seq((BRANCH_SCALE * cot).astype(BF))
        grad_out = t_dot(attended, attn_cot)
        attended_cot = dot_t(attn_cot, out_low[layer]).astype(BF)
        mixed_cot = attend_back(first, mixed, totals, attended_cot)
        grad_qkv = t_dot(normed_a, mixed_cot)
        normed_cot = scatter_seq(dot_t(mixed_cot, qkv_low[layer]))
        back, gain_sum_a, shift_sum_a = norm_back(unit_a, inverse_a, gains[layer, 0], normed_cot)
        cot = cot + back
        norm_sums.append(jnp.stack([gain_sum_a, gain_sum_b, shift_sum_a, shift_sum_b]))
        pending[layer] = (grad_qkv, grad_out, grad_up, grad_down)

    turned_back = {}
    column_back = {}
    qkv1, out1, up1, down1 = pending[1]
    qkv0, out0, up0, down0 = pending[0]
    if ruled:
        column_back["up1"], down1_t, out1_t = reduce_blocks([cols_blocks(up1), rows_blocks(down1), rows_blocks(out1)])
        qkv1_p, column_back["up0"], down0_t = reduce_blocks(
            [pad_cols(cols_blocks(qkv1), inner), cols_blocks(up0), rows_blocks(down0)]
        )
        column_back["qkv1"] = qkv1_p[:, : 3 * group]
        (out0_t,) = reduce_blocks([rows_blocks(out0)])
        (column_back["qkv0"],) = reduce_blocks([cols_blocks(qkv0)])
        back = turn(jnp.concatenate([out1_t, down1_t]).astype(BF)).astype(F32)
        out_grads[1], down_grads[1] = back[:piece], back[piece:]
        back = turn(down0_t.astype(BF)).astype(F32)
        down_grads[0] = back
        out_grads[0] = turn(out0_t.astype(BF)).astype(F32)
    else:
        for name, grad in (("up1", up1), ("qkv1", qkv1), ("up0", up0), ("qkv0", qkv0)):
            (column_back[name],) = reduce_blocks([cols_blocks(grad)])
        out_grads = [rows_whole(out0), rows_whole(out1)]
        down_grads = [rows_whole(down0), rows_whole(down1)]

    def column_home(grad):
        return exchange_seq(grad.astype(BF).reshape(seq, piece, -1)).astype(F32)

    for layer in range(LAYERS):
        up_grads[layer] = column_home(column_back["up%d" % layer]).transpose(1, 0, 2).reshape(piece, -1)
        qkv_home = column_home(column_back["qkv%d" % layer]).reshape(seq, piece, 3, group)
        qkv_grads[layer] = qkv_home.transpose(1, 2, 0, 3).reshape(piece, -1)

    sums = jnp.concatenate(norm_sums[::-1])
    if ruled:
        for bit in (1, 2):
            sums = sums + swap_seq(sums, bit)
        for bit in (1, 2, 4):
            sums = sums + lax.ppermute(sums, "fsdp", [(f, f ^ bit) for f in range(8)])
    else:
        sums = lax.psum(sums, BOTH)
    whose = lax.axis_index("fsdp") * seq + place
    sums = lax.dynamic_slice_in_dim(sums, whose * piece, piece, 1).reshape(LAYERS, 4, piece)
    return (
        outputs,
        cot.astype(BF),
        sums[:, :2],
        sums[:, 2],
        sums[:, 3],
        jnp.stack(qkv_grads),
        jnp.stack(out_grads),
        jnp.stack(up_grads),
        jnp.stack(down_grads),
    )


def solution(mesh):
    rows = P(BOTH, None)
    thirds = P(None, None, BOTH)
    middle = P(None, BOTH, None)
    return jax.shard_map(
        shards,
        mesh=mesh,
        in_specs=(rows, thirds, thirds, middle, middle, middle, middle, rows, P("fsdp", None)),
        out_specs=(rows, rows, thirds, P(None, BOTH), P(None, BOTH), middle, middle, middle, middle),
        check_vma=False,
    )
```

time: 1620 us -> 598 us (0.37)
  waiting for transfers between devices: 1040 us -> 313 us
  blocking collectives: 237 us -> 0 us
  matrix products: 169 us -> 41.6 us
  starting transfers between devices: 24.4 us -> 67.6 us
  Pallas kernels: 0 us -> 29.4 us
    reduce_scatter x8 -> x0, waiting for transfers between devices: 794 us -> none  [the longest x2 280 us: shards(): lax.psum_scatter(grad_down, ('fsdp', 'seq'), scatter_dimension=0, tiled=T...]
    ppermute x0 -> x81, waiting for transfers between devices: none -> 313 us  [the longest x46 105 us: swap_seq(): return lax.ppermute(values, 'seq', [(s, s ^ bit) for s in range(4)])]
    all_gather x8 -> x0, waiting for transfers between devices: 171 us -> none  [the longest x2 81.9 us: fetch_forward(): lax.all_gather(w_down[layer_index].astype(jnp.bfloat16), ('fsdp', 'seq'),...]
    all_gather x4 -> x0, blocking collectives: 155 us -> none  [the longest x2 81.8 us: fetch_forward(): lax.all_gather(norm_shifts[layer_index].T.astype(jnp.bfloat16), ('fsdp',...]
    dot_general x72 -> x24, matrix products: 169 us -> 41.6 us  [the longest x8 15.3 us: dot_t(): lax.dot_general(left, right, (((1,), (1,)), ((), ())), preferred_element_...]
    all_to_all x6 -> x0, waiting for transfers between devices: 68.2 us -> none  [the longest x2 32.7 us: shards(): lax.all_to_all(mixed_low.reshape(tok_rows, 3, seq_count, group_cols), 'se...]
    ppermute x0 -> x81, starting transfers between devices: none -> 67.6 us  [the longest x46 43.4 us: swap_seq(): return lax.ppermute(values, 'seq', [(s, s ^ bit) for s in range(4)])]
    all_to_all x2 -> x0, blocking collectives: 42.2 us -> none  [the longest x1 29.1 us: shards(): lax.all_to_all(stacked_cot.astype(jnp.bfloat16), 'seq', split_axis=0, con...]
  transfers between devices with their start and end apart: 22 -> 81, of which waited for: 15 -> 47; matrix products, arithmetic and copies ran while one was open for 14% -> 20% of each run, Pallas kernels for 0% -> 2%
where the time goes in v1:
time: 598 us; the launch traced here: 592 us
  waiting for transfers between devices  313 us (52%)
  local copies, waits for them, and re-layouts  69.7 us (12%)
  starting transfers between devices  67.6 us (11%)
  other arithmetic  58.4 us (10%)
  matrix products  41.6 us (7%)
  Pallas kernels  29.4 us (5%)
  between operations  11.7 us (2%)
    ppermute x46, waiting for transfers between devices, swap_seq(): return lax.ppermute(values, 'seq', [(s, s ^ bit) for s in range(4)])  105 us
    ppermute x9, waiting for transfers between devices, gather_fsdp(): block = lax.ppermute(block, 'fsdp', ring)  63.9 us
    ppermute x12, waiting for transfers between devices, scatter_fsdp(): running = lax.ppermute(running.astype(BF), 'fsdp', ring).astype(F32)  55.4 us
    ppermute x3, waiting for transfers between devices, gather_fsdp(): other = lax.ppermute(gathered, 'fsdp', [(f, f ^ 1) for f in range(8)])  44 us
    ppermute x46, starting transfers between devices, swap_seq(): return lax.ppermute(values, 'seq', [(s, s ^ bit) for s in range(4)])  43.4 us
    ppermute x4, waiting for transfers between devices, scatter_fsdp(): lax.ppermute(sent, 'fsdp', [(f, f ^ 1) for f in range(8)]).astype(F32)  36 us
    unnamed x216, local copies, waits for them, and re-layouts  19.8 us
    pallas_call x2, Pallas kernels, attend_back(): pl.pallas_call(attend_back_kernel, out_shape=jax.ShapeDtypeStruct((length...  17.8 us
  transfers between devices with their start and end apart: 81, of which 47 were waited for; matrix products, arithmetic and copies ran while one was open for 20% of the time, Pallas kernels for 2%

profile of v1, /device:TPU:0, one launch (start us, length us, event | category | flops | bytes accessed | tf_op | source)
XLA Modules:
  0.0 591.6 jit_solution(18211366515154643778)
XLA Ops:
  47.3 9.8 %collective-permute-done.11 = bf16[216,768]{1,0:T(8,128)(2,1)} collective-permute-done((bf16[216,768]{1,0:T(8,128)(2,1)S(1)}, bf16[216,768]{1,0:T(8,128)(2,1)}, u32[]{:S(2)}, u32[]{:S(2)}) %collective-permute-start.11) | collective-permute-done | bytes 331808 | tf_op jit(solution)/shard_map/ppermute | solution.py:80
  89.7 12.7 %collective-permute-done.14 = bf16[4,216,768]{2,1,0:T(8,128)(2,1)} collective-permute-done((bf16[4,216,768]{2,1,0:T(8,128)(2,1)S(1)}, bf16[4,216,768]{2,1,0:T(8,128)(2,1)}, u32[]{:S(2)}, u32[]{:S(2)}) %collective-permute-start.14) | collective-permute-done | bytes 1327136 | tf_op jit(solution)/shard_map/ppermute | solution.py:82
  114.3 9.9 %collective-permute-done.16 = bf16[256,768]{1,0:T(8,128)(2,1)S(1)} collective-permute-done((bf16[256,768]{1,0:T(8,128)(2,1)S(1)}, bf16[256,768]{1,0:T(8,128)(2,1)S(1)}, u32[]{:S(2)}, u32[]{:S(2)}) %collective-permute-start.16) | collective-permute-done | bytes 393248 | tf_op jit(solution)/shard_map/ppermute | solution.py:29
  127.3 9.1 %collective-permute-done.17 = bf16[256,768]{1,0:T(8,128)(2,1)S(1)} collective-permute-done((bf16[256,768]{1,0:T(8,128)(2,1)S(1)}, bf16[256,768]{1,0:T(8,128)(2,1)S(1)}, u32[]{:S(2)}, u32[]{:S(2)}) %collective-permute-start.17) | collective-permute-done | bytes 393248 | tf_op jit(solution)/shard_map/ppermute | solution.py:29
  145.4 6.2 %collective-permute-done.23 = bf16[312,768]{1,0:T(8,128)(2,1)S(1)} collective-permute-done((bf16[312,768]{1,0:T(8,128)(2,1)S(1)}, bf16[312,768]{1,0:T(8,128)(2,1)S(1)}, u32[]{:S(2)}, u32[]{:S(2)}) %collective-permute-start.23) | collective-permute-done | bytes 479264 | tf_op jit(solution)/shard_map/ppermute | solution.py:80
  152.3 12.6 %collective-permute-done.24 = bf16[312,768]{1,0:T(8,128)(2,1)S(1)} collective-permute-done((bf16[312,768]{1,0:T(8,128)(2,1)S(1)}, bf16[312,768]{1,0:T(8,128)(2,1)S(1)}, u32[]{:S(2)}, u32[]{:S(2)}) %collective-permute-start.24) | collective-permute-done | bytes 479264 | tf_op jit(solution)/shard_map/ppermute | solution.py:80
  166.6 10.9 %collective-permute-done.25 = bf16[312,768]{1,0:T(8,128)(2,1)S(1)} collective-permute-done((bf16[312,768]{1,0:T(8,128)(2,1)S(1)}, bf16[312,768]{1,0:T(8,128)(2,1)S(1)}, u32[]{:S(2)}, u32[]{:S(2)}) %collective-permute-start.25) | collective-permute-done | bytes 479264 | tf_op jit(solution)/shard_map/ppermute | solution.py:80
  180.2 7.1 %collective-permute-done.21 = bf16[256,768]{1,0:T(8,128)(2,1)S(1)} collective-permute-done((bf16[256,768]{1,0:T(8,128)(2,1)S(1)}, bf16[256,768]{1,0:T(8,128)(2,1)S(1)}, u32[]{:S(2)}, u32[]{:S(2)}) %collective-permute-start.21) | collective-permute-done | bytes 393248 | tf_op jit(solution)/shard_map/ppermute | solution.py:29
  187.8 31.3 %collective-permute-done.26 = bf16[4,312,768]{2,1,0:T(8,128)(2,1)S(1)} collective-permute-done((bf16[4,312,768]{2,1,0:T(8,128)(2,1)S(1)}, bf16[4,312,768]{2,1,0:T(8,128)(2,1)S(1)}, u32[]{:S(2)}, u32[]{:S(2)}) %collective-permute-start.26) | collective-permute-done | bytes 1916960 | tf_op jit(solution)/shard_map/ppermute | solution.py:82
  234.1 9.8 %collective-permute-done.28 = bf16[256,768]{1,0:T(8,128)(2,1)S(1)} collective-permute-done((bf16[256,768]{1,0:T(8,128)(2,1)S(1)}, bf16[256,768]{1,0:T(8,128)(2,1)S(1)}, u32[]{:S(2)}, u32[]{:S(2)}) %collective-permute-start.28) | collective-permute-done | bytes 393248 | tf_op jit(solution)/shard_map/ppermute | solution.py:29
  245.9 6.5 %collective-permute-done.33 = bf16[256,768]{1,0:T(8,128)(2,1)S(1)} collective-permute-done((bf16[256,768]{1,0:T(8,128)(2,1)S(1)}, bf16[256,768]{1,0:T(8,128)(2,1)S(1)}, u32[]{:S(2)}, u32[]{:S(2)}) %collective-permute-start.33) | collective-permute-done | bytes 393248 | tf_op jit(solution)/shard_map/ppermute | solution.py:29
  252.6 7.3 %collective-permute-done.29 = bf16[256,768]{1,0:T(8,128)(2,1)S(1)} collective-permute-done((bf16[256,768]{1,0:T(8,128)(2,1)S(1)}, bf16[256,768]{1,0:T(8,128)(2,1)S(1)}, u32[]{:S(2)}, u32[]{:S(2)}) %collective-permute-start.29) | collective-permute-done | bytes 393248 | tf_op jit(solution)/shard_map/ppermute | solution.py:29
  275.6 9.0 %collective-permute-done.36 = bf16[256,768]{1,0:T(8,128)(2,1)S(1)} collective-permute-done((bf16[256,768]{1,0:T(8,128)(2,1)S(1)}, bf16[256,768]{1,0:T(8,128)(2,1)S(1)}, u32[]{:S(2)}, u32[]{:S(2)}) %collective-permute-start.36) | collective-permute-done | bytes 393248 | tf_op jit(solution)/shard_map/ppermute | solution.py:29
  285.7 6.6 %collective-permute-done.32 = bf16[256,768]{1,0:T(8,128)(2,1)S(1)} collective-permute-done((bf16[256,768]{1,0:T(8,128)(2,1)S(1)}, bf16[256,768]{1,0:T(8,128)(2,1)S(1)}, u32[]{:S(2)}, u32[]{:S(2)}) %collective-permute-start.32) | collective-permute-done | bytes 393248 | tf_op jit(solution)/shard_map/ppermute | solution.py:29
  325.3 8.9 %attend_back.2 = bf16[1024,576]{1,0:T(8,128)(2,1)S(1)} custom-call(s32[1024,1]{1,0:T(8,128)S(1)} %copy.474.first_ref, bf16[1024,576]{1,0:T(8,128)(2,1)S(1)} %convolution_convert_fusion.mixed_ref, f32[1024,3]{1,0:T(8,128)S(1)} %copy-done.9, bf16[1024,192]{1,0:T(8,128)(2,1)S(1)} %copy-done.3), custom_call_target="tpu_custom_call" | custom-call | tf_op jit(solution)/shard_map/attend_back/pallas_call | solution.py:214
  358.0 18.6 %collective-permute-done.71 = bf16[4,216,768]{2,1,0:T(8,128)(2,1)} collective-permute-done((bf16[4,216,768]{2,1,0:T(8,128)(2,1)}, bf16[4,216,768]{2,1,0:T(8,128)(2,1)}, u32[]{:S(2)}, u32[]{:S(2)}) %collective-permute-start.71) | collective-permute-done | bytes 1327136 | tf_op jit(solution)/shard_map/ppermute | solution.py:96
  392.0 9.1 %collective-permute-done.73 = bf16[216,768]{1,0:T(8,128)(2,1)S(1)} collective-permute-done((bf16[216,768]{1,0:T(8,128)(2,1)S(1)}, bf16[216,768]{1,0:T(8,128)(2,1)S(1)}, u32[]{:S(2)}, u32[]{:S(2)}) %collective-permute-start.73) | collective-permute-done | bytes 331808 | tf_op jit(solution)/shard_map/ppermute | solution.py:100
  404.1 6.6 %collective-permute-done.74 = bf16[216,768]{1,0:T(8,128)(2,1)S(1)} collective-permute-done((bf16[216,768]{1,0:T(8,128)(2,1)S(1)}, bf16[216,768]{1,0:T(8,128)(2,1)S(1)}, u32[]{:S(2)}, u32[]{:S(2)}) %collective-permute-start.74) | collective-permute-done | bytes 331808 | tf_op jit(solution)/shard_map/ppermute | solution.py:100
  428.2 7.5 %collective-permute-done.44 = bf16[256,768]{1,0:T(8,128)(2,1)S(1)} collective-permute-done((bf16[256,768]{1,0:T(8,128)(2,1)S(1)}, bf16[256,768]{1,0:T(8,128)(2,1)S(1)}, u32[]{:S(2)}, u32[]{:S(2)}) %collective-permute-start.44) | collective-permute-done | bytes 393248 | tf_op jit(solution)/shard_map/ppermute | solution.py:29
  450.1 17.4 %collective-permute-done.60 = bf16[4,288,768]{2,1,0:T(8,128)(2,1)} collective-permute-done((bf16[4,288,768]{2,1,0:T(8,128)(2,1)}, bf16[4,288,768]{2,1,0:T(8,128)(2,1)}, u32[]{:S(2)}, u32[]{:S(2)}) %collective-permute-start.60) | collective-permute-done | bytes 1769504 | tf_op jit(solution)/shard_map/ppermute | solution.py:96
  473.0 9.6 %collective-permute-done.61 = bf16[288,768]{1,0:T(8,128)(2,1)S(1)} collective-permute-done((bf16[288,768]{1,0:T(8,128)(2,1)S(1)}, bf16[288,768]{1,0:T(8,128)(2,1)S(1)}, u32[]{:S(2)}, u32[]{:S(2)}) %collective-permute-start.61) | collective-permute-done | bytes 442400 | tf_op jit(solution)/shard_map/ppermute | solution.py:100
  490.2 8.9 %attend_back.3 = bf16[1024,576]{1,0:T(8,128)(2,1)S(1)} custom-call(s32[1024,1]{1,0:T(8,128)S(1)} %copy.474.first_ref, bf16[1024,576]{1,0:T(8,128)(2,1)S(1)} %convolution_convert_fusion.1.mixed_ref, f32[1024,3]{1,0:T(8,128)S(1)} %copy-done.7, bf16[1024,192]{1,0:T(8,128)(2,1)S(1)} %copy.507.cot_ref), custom_call_target="tpu_custom_call" | custom-call | tf_op jit(solution)/shard_map/attend_back/pallas_call | solution.py:214
  521.1 12.6 %collective-permute-done.55 = bf16[96,576]{1,0:T(8,128)(2,1)S(1)} collective-permute-done((bf16[96,576]{1,0:T(8,128)(2,1)S(1)}, bf16[96,576]{1,0:T(8,128)(2,1)S(1)}, u32[]{:S(2)}, u32[]{:S(2)}) %collective-permute-start.55) | collective-permute-done | bytes 110624 | tf_op jit(solution)/shard_map/ppermute | solution.py:100
  553.6 9.3 %collective-permute-done.65 = bf16[2,24,576]{2,1,0:T(8,128)(2,1)S(1)} collective-permute-done((bf16[2,24,576]{2,1,0:T(8,128)(2,1)S(1)}, bf16[2,24,576]{2,1,0:T(8,128)(2,1)S(1)}, u32[]{:S(2)}, u32[]{:S(2)}) %collective-permute-start.65) | collective-permute-done | bytes 55328 | tf_op jit(solution)/shard_map/ppermute | solution.py:29
  (675 shorter events, 322.6 us)
Async XLA Ops:
  3.1 15.2 %collective-permute-start = (bf16[2,32,576]{2,1,0:T(8,128)(2,1)S(1)}, bf16[2,32,576]{2,1,0:T(8,128)(2,1)S(1)}, u32[]{:S(2)}, u32[]{:S(2)}) collective-permute-start(bf16[2,32,576]{2,1,0:T(8,128)(2,1)S(1)} %fusion.101), channel_id=1, source_target_pairs={{0,1},{1,0},{2,3},{3,2},{4,5},{5,4},{6,7},{7,6},{8,9},{9,8},{10,11... | collective-permute-start | bytes 221192 | tf_op jit(solution)/shard_map/ppermute | solution.py:29
  3.8 28.2 %collective-permute-start.10 = (bf16[240,768]{1,0:T(8,128)(2,1)S(1)}, bf16[240,768]{1,0:T(8,128)(2,1)S(1)}, u32[]{:S(2)}, u32[]{:S(2)}) collective-permute-start(bf16[240,768]{1,0:T(8,128)(2,1)S(1)} %pad_maximum_fusion.24), channel_id=1, source_target_pairs={{0,0},{1,8},{2,16},{3,24},{4,4},{5,12},{6,20},{7,28},{8,1},{9,9},{... | collective-permute-start | bytes 1105928 | tf_op jit(solution)/shard_map/ppermute | solution.py:111
  6.5 20.0 %collective-permute-start.8 = (bf16[2,72,768]{2,1,0:T(8,128)(2,1)S(1)}, bf16[2,72,768]{2,1,0:T(8,128)(2,1)S(1)}, u32[]{:S(2)}, u32[]{:S(2)}) collective-permute-start(bf16[2,72,768]{2,1,0:T(8,128)(2,1)S(1)} %select_bitcast_fusion.39), channel_id=1, source_target_pairs={{0,1},{1,0},{2,3},{3,2},{4,5},{5,4},{6,7},{7,6},{8,9},{9,8},{10,11... | collective-permute-start | bytes 663560 | tf_op jit(solution)/shard_map/ppermute | solution.py:29
  26.7 19.7 %collective-permute-start.9 = (bf16[2,72,768]{2,1,0:T(8,128)(2,1)S(1)}, bf16[2,72,768]{2,1,0:T(8,128)(2,1)S(1)}, u32[]{:S(2)}, u32[]{:S(2)}) collective-permute-start(bf16[2,72,768]{2,1,0:T(8,128)(2,1)S(1)} %select_bitcast_fusion.38), channel_id=1, source_target_pairs={{0,2},{1,3},{2,0},{3,1},{4,6},{5,7},{6,4},{7,5},{8,10},{9,11},{10,... | collective-permute-start | bytes 663560 | tf_op jit(solution)/shard_map/ppermute | solution.py:29
  76.5 25.9 %collective-permute-start.14 = (bf16[4,216,768]{2,1,0:T(8,128)(2,1)S(1)}, bf16[4,216,768]{2,1,0:T(8,128)(2,1)}, u32[]{:S(2)}, u32[]{:S(2)}) collective-permute-start(bf16[4,216,768]{2,1,0:T(8,128)(2,1)S(1)} %bitcast_dynamic-update-slice_fusion.4), channel_id=1, source_target_pairs={{0,4},{4,0},{8,12},{12,8},{16,20},{20,16},{24,28},{28,24},{1,5},{5... | collective-permute-start | bytes 3981320 | tf_op jit(solution)/shard_map/ppermute | solution.py:82
  145.3 19.8 %collective-permute-start.19 = (bf16[2,256,768]{2,1,0:T(8,128)(2,1)S(1)}, bf16[2,256,768]{2,1,0:T(8,128)(2,1)S(1)}, u32[]{:S(2)}, u32[]{:S(2)}) collective-permute-start(bf16[2,256,768]{2,1,0:T(8,128)(2,1)S(1)} %fusion.60), channel_id=1, source_target_pairs={{0,1},{1,0},{2,3},{3,2},{4,5},{5,4},{6,7},{7,6},{8,9},{9,8},{10,11... | collective-permute-start | bytes 2359304 | tf_op jit(solution)/shard_map/ppermute | solution.py:29
  177.5 41.5 %collective-permute-start.26 = (bf16[4,312,768]{2,1,0:T(8,128)(2,1)S(1)}, bf16[4,312,768]{2,1,0:T(8,128)(2,1)S(1)}, u32[]{:S(2)}, u32[]{:S(2)}) collective-permute-start(bf16[4,312,768]{2,1,0:T(8,128)(2,1)S(1)} %bitcast_dynamic-update-slice_fusion), channel_id=1, source_target_pairs={{0,4},{4,0},{8,12},{12,8},{16,20},{20,16},{24,28},{28,24},{1,5},{5... | collective-permute-start | bytes 5750792 | tf_op jit(solution)/shard_map/ppermute | solution.py:82
  187.7 32.3 %collective-permute-start.22 = (bf16[2,256,768]{2,1,0:T(8,128)(2,1)S(1)}, bf16[2,256,768]{2,1,0:T(8,128)(2,1)S(1)}, u32[]{:S(2)}, u32[]{:S(2)}) collective-permute-start(bf16[2,256,768]{2,1,0:T(8,128)(2,1)S(1)} %pad_maximum_fusion.15), channel_id=1, source_target_pairs={{0,1},{1,0},{2,3},{3,2},{4,5},{5,4},{6,7},{7,6},{8,9},{9,8},{10,11... | collective-permute-start | bytes 2359304 | tf_op jit(solution)/shard_map/ppermute | solution.py:29
  233.2 19.1 %collective-permute-start.33 = (bf16[256,768]{1,0:T(8,128)(2,1)S(1)}, bf16[256,768]{1,0:T(8,128)(2,1)S(1)}, u32[]{:S(2)}, u32[]{:S(2)}) collective-permute-start(bf16[256,768]{1,0:T(8,128)(2,1)S(1)} %fusion.58), channel_id=1, source_target_pairs={{0,2},{1,3},{2,0},{3,1},{4,6},{5,7},{6,4},{7,5},{8,10},{9,11},{10,... | collective-permute-start | bytes 1179656 | tf_op jit(solution)/shard_map/ppermute | solution.py:29
  244.6 15.3 %collective-permute-start.29 = (bf16[256,768]{1,0:T(8,128)(2,1)S(1)}, bf16[256,768]{1,0:T(8,128)(2,1)S(1)}, u32[]{:S(2)}, u32[]{:S(2)}) collective-permute-start(bf16[256,768]{1,0:T(8,128)(2,1)S(1)} %add_convert_fusion), channel_id=1, source_target_pairs={{0,2},{1,3},{2,0},{3,1},{4,6},{5,7},{6,4},{7,5},{8,10},{9,11},{10,... | collective-permute-start | bytes 1179656 | tf_op jit(solution)/shard_map/ppermute | solution.py:29
  274.4 17.9 %collective-permute-start.32 = (bf16[256,768]{1,0:T(8,128)(2,1)S(1)}, bf16[256,768]{1,0:T(8,128)(2,1)S(1)}, u32[]{:S(2)}, u32[]{:S(2)}) collective-permute-start(bf16[256,768]{1,0:T(8,128)(2,1)S(1)} %fusion.85), channel_id=1, source_target_pairs={{0,2},{1,3},{2,0},{3,1},{4,6},{5,7},{6,4},{7,5},{8,10},{9,11},{10,... | collective-permute-start | bytes 1179656 | tf_op jit(solution)/shard_map/ppermute | solution.py:29
  344.7 31.9 %collective-permute-start.71 = (bf16[4,216,768]{2,1,0:T(8,128)(2,1)}, bf16[4,216,768]{2,1,0:T(8,128)(2,1)}, u32[]{:S(2)}, u32[]{:S(2)}) collective-permute-start(bf16[4,216,768]{2,1,0:T(8,128)(2,1)} %fusion.33), channel_id=1, source_target_pairs={{0,4},{4,0},{8,12},{12,8},{16,20},{20,16},{24,28},{28,24},{1,5},{5... | collective-permute-start | bytes 3981320 | tf_op jit(solution)/shard_map/ppermute | solution.py:96
  356.7 35.0 %collective-permute-start.41 = (bf16[256,768]{1,0:T(8,128)(2,1)S(1)}, bf16[256,768]{1,0:T(8,128)(2,1)S(1)}, u32[]{:S(2)}, u32[]{:S(2)}) collective-permute-start(bf16[256,768]{1,0:T(8,128)(2,1)S(1)} %get-tuple-element.45), channel_id=1, source_target_pairs={{0,2},{1,3},{2,0},{3,1},{4,6},{5,7},{6,4},{7,5},{8,10},{9,11},{10,... | collective-permute-start | bytes 1179656 | tf_op jit(solution)/shard_map/ppermute | solution.py:29
  391.9 18.9 %collective-permute-start.42 = (bf16[2,256,768]{2,1,0:T(8,128)(2,1)S(1)}, bf16[2,256,768]{2,1,0:T(8,128)(2,1)S(1)}, u32[]{:S(2)}, u32[]{:S(2)}) collective-permute-start(bf16[2,256,768]{2,1,0:T(8,128)(2,1)S(1)} %pad_maximum_fusion.19), channel_id=1, source_target_pairs={{0,1},{1,0},{2,3},{3,2},{4,5},{5,4},{6,7},{7,6},{8,9},{9,8},{10,11... | collective-permute-start | bytes 2359304 | tf_op jit(solution)/shard_map/ppermute | solution.py:29
  410.8 16.4 %collective-permute-start.78 = (bf16[2,24,768]{2,1,0:T(8,128)(2,1)S(1)}, bf16[2,24,768]{2,1,0:T(8,128)(2,1)S(1)}, u32[]{:S(2)}, u32[]{:S(2)}) collective-permute-start(bf16[2,24,768]{2,1,0:T(8,128)(2,1)S(1)} %fusion.107), channel_id=1, source_target_pairs={{0,1},{1,0},{2,3},{3,2},{4,5},{5,4},{6,7},{7,6},{8,9},{9,8},{10,11... | collective-permute-start | bytes 221192 | tf_op jit(solution)/shard_map/ppermute | solution.py:29
  426.9 40.7 %collective-permute-start.60 = (bf16[4,288,768]{2,1,0:T(8,128)(2,1)}, bf16[4,288,768]{2,1,0:T(8,128)(2,1)}, u32[]{:S(2)}, u32[]{:S(2)}) collective-permute-start(bf16[4,288,768]{2,1,0:T(8,128)(2,1)} %fusion.26), channel_id=1, source_target_pairs={{0,4},{4,0},{8,12},{12,8},{16,20},{20,16},{24,28},{28,24},{1,5},{5... | collective-permute-start | bytes 5308424 | tf_op jit(solution)/shard_map/ppermute | solution.py:96
  450.0 33.5 %collective-permute-start.46 = (bf16[2,256,768]{2,1,0:T(8,128)(2,1)S(1)}, bf16[2,256,768]{2,1,0:T(8,128)(2,1)S(1)}, u32[]{:S(2)}, u32[]{:S(2)}) collective-permute-start(bf16[2,256,768]{2,1,0:T(8,128)(2,1)S(1)} %pad_maximum_fusion.20), channel_id=1, source_target_pairs={{0,1},{1,0},{2,3},{3,2},{4,5},{5,4},{6,7},{7,6},{8,9},{9,8},{10,11... | collective-permute-start | bytes 2359304 | tf_op jit(solution)/shard_map/ppermute | solution.py:29
  483.4 32.9 %collective-permute-start.62 = (bf16[288,768]{1,0:T(8,128)(2,1)}, bf16[288,768]{1,0:T(8,128)(2,1)}, u32[]{:S(2)}, u32[]{:S(2)}) collective-permute-start(bf16[288,768]{1,0:T(8,128)(2,1)} %fusion.46), channel_id=1, source_target_pairs={{0,8},{4,12},{8,24},{12,28},{16,0},{20,4},{24,16},{28,20},{1,9},{5... | collective-permute-start | bytes 1327112 | tf_op jit(solution)/shard_map/ppermute | solution.py:100
  501.3 16.6 %collective-permute-start.54 = (bf16[4,96,576]{2,1,0:T(8,128)(2,1)S(1)}, bf16[4,96,576]{2,1,0:T(8,128)(2,1)S(1)}, u32[]{:S(2)}, u32[]{:S(2)}) collective-permute-start(bf16[4,96,576]{2,1,0:T(8,128)(2,1)S(1)} %fusion.78), channel_id=1, source_target_pairs={{0,4},{4,0},{8,12},{12,8},{16,20},{20,16},{24,28},{28,24},{1,5},{5... | collective-permute-start | bytes 1327112 | tf_op jit(solution)/shard_map/ppermute | solution.py:96
  510.8 34.7 %collective-permute-start.47 = (bf16[2,256,768]{2,1,0:T(8,128)(2,1)S(1)}, bf16[2,256,768]{2,1,0:T(8,128)(2,1)S(1)}, u32[]{:S(2)}, u32[]{:S(2)}) collective-permute-start(bf16[2,256,768]{2,1,0:T(8,128)(2,1)S(1)} %fusion.66), channel_id=1, source_target_pairs={{0,1},{1,0},{2,3},{3,2},{4,5},{5,4},{6,7},{7,6},{8,9},{9,8},{10,11... | collective-permute-start | bytes 2359304 | tf_op jit(solution)/shard_map/ppermute | solution.py:29
  517.4 22.2 %collective-permute-start.63 = (bf16[288,768]{1,0:T(8,128)(2,1)S(1)}, bf16[288,768]{1,0:T(8,128)(2,1)S(1)}, u32[]{:S(2)}, u32[]{:S(2)}) collective-permute-start(bf16[288,768]{1,0:T(8,128)(2,1)S(1)} %fusion.45), channel_id=1, source_target_pairs={{0,8},{4,12},{8,24},{12,28},{16,0},{20,4},{24,16},{28,20},{1,9},{5... | collective-permute-start | bytes 1327112 | tf_op jit(solution)/shard_map/ppermute | solution.py:100
  518.0 15.7 %collective-permute-start.55 = (bf16[96,576]{1,0:T(8,128)(2,1)S(1)}, bf16[96,576]{1,0:T(8,128)(2,1)S(1)}, u32[]{:S(2)}, u32[]{:S(2)}) collective-permute-start(bf16[96,576]{1,0:T(8,128)(2,1)S(1)} %fusion.100), channel_id=1, source_target_pairs={{0,8},{4,12},{8,24},{12,28},{16,0},{20,4},{24,16},{28,20},{1,9},{5... | collective-permute-start | bytes 331784 | tf_op jit(solution)/shard_map/ppermute | solution.py:100
  541.1 31.1 %collective-permute-start.80 = (bf16[96,768]{1,0:T(8,128)(2,1)}, bf16[96,768]{1,0:T(8,128)(2,1)}, u32[]{:S(2)}, u32[]{:S(2)}) collective-permute-start(bf16[96,768]{1,0:T(8,128)(2,1)} %get-tuple-element.102), channel_id=1, source_target_pairs={{0,0},{1,8},{2,16},{3,24},{4,4},{5,12},{6,20},{7,28},{8,1},{9,9},{... | collective-permute-start | bytes 442376 | tf_op jit(solution)/shard_map/ppermute | solution.py:111
  546.5 23.2 %collective-permute-start.48 = (bf16[256,768]{1,0:T(8,128)(2,1)}, bf16[256,768]{1,0:T(8,128)(2,1)}, u32[]{:S(2)}, u32[]{:S(2)}) collective-permute-start(bf16[256,768]{1,0:T(8,128)(2,1)} %fusion.89), channel_id=1, source_target_pairs={{0,2},{1,3},{2,0},{3,1},{4,6},{5,7},{6,4},{7,5},{8,10},{9,11},{10,... | collective-permute-start | bytes 1179656 | tf_op jit(solution)/shard_map/ppermute | solution.py:29
  (166 other events, 1149.3 us)

commit v2 on v1

v2 whole, which is shorter than its diff:
```python
import jax
import jax.numpy as jnp
from jax import lax
from jax.experimental import pallas as pl
from jax.experimental.pallas import tpu as pltpu
from jax.sharding import PartitionSpec as P

H = 12
HD = 64
LAYERS = 2
MAX_DOC = 512

NORM_EPS = 1e-05
BRANCH_SCALE = 0.7071067811865476
MASKED = -1e30
BF = jnp.bfloat16
F32 = jnp.float32
BOTH = ("fsdp", "seq")

RING_NEXT = (1, 3, 0, 2)


def ring_behind(line, steps):
    at = ((line ^ (line >> 1)) - steps) & 3
    return at ^ (at >> 1)


def after(value, *others):
    return lax.optimization_barrier((value,) + others)[0] if others else value


def swap_seq(values, bit):
    return lax.ppermute(values, "seq", [(s, s ^ bit) for s in range(4)])


def by_bit(bit, own, other):
    zero = bit == 0
    return jnp.where(zero, own, other), jnp.where(zero, other, own)


def gather_seq(rows, work=None):
    place = lax.axis_index("seq")
    far = swap_seq(rows, 2)
    if work is not None:
        far = after(far, *work(rows))
    pair = jnp.stack(by_bit(place // 2, rows, far))
    near = swap_seq(pair, 1)
    return jnp.stack(by_bit(place % 2, pair, near), axis=1).reshape(-1, rows.shape[-1])


def scatter_seq(partial, work=None):
    place = lax.axis_index("seq")
    y_bit, c_bit = place // 2, place % 2
    width = partial.shape[-1]
    parts = partial.reshape(2, 2, -1, width)
    sent = lax.dynamic_index_in_dim(parts, 1 - c_bit, 1, keepdims=False).astype(BF)
    kept = lax.dynamic_index_in_dim(parts, c_bit, 1, keepdims=False).astype(F32)
    half = kept + swap_seq(sent, 1).astype(F32)
    sent = lax.dynamic_index_in_dim(half, 1 - y_bit, 0, keepdims=False).astype(BF)
    kept = lax.dynamic_index_in_dim(half, y_bit, 0, keepdims=False)
    got = swap_seq(sent, 2)
    if work is not None:
        got = after(got, *work(sent))
    return kept + got.astype(F32)


def exchange_seq(parts):
    place = lax.axis_index("seq")
    y_bit, c_bit = place // 2, place % 2
    grid = parts.reshape((2, 2) + parts.shape[1:])
    kept, sent = by_bit(c_bit, grid[:, 0], grid[:, 1])
    half = jnp.stack(by_bit(c_bit, kept, swap_seq(sent, 1)), axis=1)
    kept, sent = by_bit(y_bit, half[0], half[1])
    return jnp.stack(by_bit(y_bit, kept, swap_seq(sent, 2))).reshape(parts.shape)


def over_line(block):
    return lax.ppermute(block, "fsdp", [(f, 2 * RING_NEXT[f // 2] + f % 2) for f in range(8)])


def over_side(block):
    return lax.ppermute(block, "fsdp", [(f, f ^ 1) for f in range(8)])


def owner(steps, other=0):
    place = lax.axis_index("fsdp")
    return 2 * ring_behind(place // 2, steps) + (place % 2 ^ other)


class Gather:
    def __init__(self, block):
        self.got = block
        self.step = 0
        self.result = jnp.zeros((8,) + block.shape, block.dtype)

    def put(self, block, place):
        self.result = lax.dynamic_update_index_in_dim(self.result, block, place, 0)

    def advance(self, *gates):
        moved = []
        if self.step > 0:
            self.put(after(self.side, *gates), owner(self.step - 1, 1))
        if self.step < 4:
            block = after(self.got, *gates)
            moved.append(block)
            if self.step < 3:
                self.got = over_line(block)
            self.side = over_side(block)
            self.put(block, owner(self.step))
        self.step += 1
        return moved


class Reduce:
    def __init__(self, blocks):
        self.blocks = blocks
        self.step = 0

    def take(self, place):
        return lax.dynamic_index_in_dim(self.blocks, place, 0, keepdims=False)

    def advance(self, *gates):
        moved = []
        if self.step > 0:
            total = self.take(owner(self.step)).astype(F32) + after(self.side, *gates).astype(F32)
            if self.step > 1:
                total = total + after(self.got, *gates).astype(F32)
            if self.step < 4:
                total = total.astype(BF)
                self.got = over_line(total)
            self.result = total
            moved.append(total)
        if self.step < 4:
            block = self.take(owner(self.step + 1, 1))
            if gates:
                block = after(block, *gates)
            self.side = over_side(block)
            moved.append(block)
        self.step += 1
        return moved


def turn(rows):
    moves = []
    for f in range(8):
        for s in range(4):
            moves.append((f * 4 + s, (2 * s + f % 2) * 4 + f // 2))
    return lax.ppermute(rows, BOTH, moves)


ROWS = 256


def allowed_pairs(first_ref, row_start, key_start, width):
    key_pos = key_start + lax.broadcasted_iota(jnp.int32, (ROWS, width), 1)
    query_pos = row_start + lax.broadcasted_iota(jnp.int32, (ROWS, width), 0)
    first = first_ref[pl.ds(row_start, ROWS), :]
    return (key_pos <= query_pos) & (key_pos >= first)


def key_window(row_start):
    key_start = max(0, row_start - (MAX_DOC + ROWS - 1) // ROWS * ROWS)
    return key_start, row_start + ROWS - key_start


def dot_t(left, right):
    return lax.dot_general(left, right, (((1,), (1,)), ((), ())), preferred_element_type=F32)


def t_dot(left, right):
    return lax.dot_general(left, right, (((0,), (0,)), ((), ())), preferred_element_type=F32)


def attend_kernel(first_ref, mixed_ref, out_ref, total_ref):
    length, group = out_ref.shape
    heads = group // HD
    scale = HD ** (-0.5)
    for row_start in range(0, length, ROWS):
        key_start, width = key_window(row_start)
        allowed = allowed_pairs(first_ref, row_start, key_start, width)
        outs = []
        totals = []
        for head in range(heads):
            at = head * HD
            query = mixed_ref[pl.ds(row_start, ROWS), pl.ds(at, HD)]
            keys = mixed_ref[pl.ds(key_start, width), pl.ds(group + at, HD)]
            values = mixed_ref[pl.ds(key_start, width), pl.ds(2 * group + at, HD)]
            scores = jnp.where(allowed, dot_t(query, keys) * scale, MASKED)
            top = jnp.max(scores, axis=1, keepdims=True)
            weights = jnp.exp(scores - top)
            total = jnp.sum(weights, axis=1, keepdims=True)
            low = (weights * (1.0 / total)).astype(BF)
            outs.append(jnp.dot(low, values, preferred_element_type=F32))
            totals.append(top + jnp.log(total))
        out_ref[pl.ds(row_start, ROWS), :] = jnp.concatenate(outs, axis=1).astype(BF)
        total_ref[pl.ds(row_start, ROWS), :] = jnp.concatenate(totals, axis=1)


def attend(first, mixed):
    length, wide = mixed.shape
    group = wide // 3
    return pl.pallas_call(
        attend_kernel,
        out_shape=(
            jax.ShapeDtypeStruct((length, group), BF),
            jax.ShapeDtypeStruct((length, group // HD), F32),
        ),
        compiler_params=pltpu.CompilerParams(vmem_limit_bytes=48 << 20),
        name="attend",
    )(first, mixed)


def attend_back_kernel(first_ref, mixed_ref, total_ref, cot_ref, out_ref, key_acc, value_acc):
    length, group = cot_ref.shape
    heads = group // HD
    scale = HD ** (-0.5)
    key_acc[...] = jnp.zeros_like(key_acc)
    value_acc[...] = jnp.zeros_like(value_acc)
    for row_start in range(0, length, ROWS):
        key_start, width = key_window(row_start)
        allowed = allowed_pairs(first_ref, row_start, key_start, width)
        query_grads = []
        key_grads = []
        value_grads = []
        for head in range(heads):
            at = head * HD
            query = mixed_ref[pl.ds(row_start, ROWS), pl.ds(at, HD)]
            keys = mixed_ref[pl.ds(key_start, width), pl.ds(group + at, HD)]
            values = mixed_ref[pl.ds(key_start, width), pl.ds(2 * group + at, HD)]
            cot = cot_ref[pl.ds(row_start, ROWS), pl.ds(at, HD)]
            total = total_ref[pl.ds(row_start, ROWS), pl.ds(head, 1)]
            scores = jnp.where(allowed, dot_t(query, keys) * scale - total, MASKED)
            probs = jnp.exp(scores)
            prob_cot = dot_t(cot, values)
            delta = jnp.sum(probs * prob_cot, axis=1, keepdims=True)
            score_cot = (probs * (prob_cot - delta)).astype(BF)
            query_grads.append(jnp.dot(score_cot, keys, preferred_element_type=F32) * scale)
            key_grads.append(t_dot(score_cot, query) * scale)
            value_grads.append(t_dot(probs.astype(BF), cot))
        out_ref[pl.ds(row_start, ROWS), pl.ds(0, group)] = jnp.concatenate(query_grads, axis=1).astype(BF)
        window = pl.ds(key_start, width)
        key_acc[window, :] += jnp.concatenate(key_grads, axis=1)
        value_acc[window, :] += jnp.concatenate(value_grads, axis=1)
    out_ref[:, pl.ds(group, group)] = key_acc[...].astype(BF)
    out_ref[:, pl.ds(2 * group, group)] = value_acc[...].astype(BF)


def attend_back(first, mixed, totals, cot):
    length, wide = mixed.shape
    group = wide // 3
    return pl.pallas_call(
        attend_back_kernel,
        out_shape=jax.ShapeDtypeStruct((length, wide), BF),
        scratch_shapes=[pltpu.VMEM((length, group), F32), pltpu.VMEM((length, group), F32)],
        compiler_params=pltpu.CompilerParams(vmem_limit_bytes=48 << 20),
        name="attend_back",
    )(first, mixed, totals, cot)


def norm_parts(values):
    center = values - jnp.mean(values, axis=-1, keepdims=True)
    inverse = lax.rsqrt(jnp.mean(center * center, axis=-1, keepdims=True) + NORM_EPS)
    return center * inverse, inverse


def norm_back(unit, inverse, gain, cot):
    scaled = cot * gain
    inner = scaled - jnp.mean(scaled, axis=-1, keepdims=True)
    inner = inner - unit * jnp.mean(scaled * unit, axis=-1, keepdims=True)
    return inner * inverse, jnp.sum(cot * unit, axis=0), jnp.sum(cot, axis=0)


def gelu_tanh(values):
    return 0.5 * values * (1.0 + jnp.tanh(0.7978845608028654 * (values + 0.044715 * values * values * values)))


def gelu_slope(values):
    square = values * values
    bent = jnp.tanh(0.7978845608028654 * (values + 0.044715 * values * square))
    inner = 0.7978845608028654 * (1.0 + 3.0 * 0.044715 * square)
    return 0.5 * (1.0 + bent) + 0.5 * values * (1.0 - bent * bent) * inner


def mul(left, right):
    return jnp.dot(left, right, preferred_element_type=F32)


def shards(tokens, norm_gains, norm_shifts, w_qkv, w_out, w_up, w_down, out_grad, doc_lengths):
    tok_rows, width = tokens.shape
    fsdp, seq = lax.axis_size("fsdp"), lax.axis_size("seq")
    ruled = fsdp == 8
    length = tok_rows * seq
    group = (H // seq) * HD
    piece = w_qkv.shape[1]
    inner = w_up.shape[2] // seq
    unit_rows = w_down.shape[1]
    place = lax.axis_index("seq")

    ends = jnp.cumsum(doc_lengths[0])
    starts = ends - doc_lengths[0]
    positions = lax.iota(jnp.int32, length)
    first = jnp.max(jnp.where(positions[:, None] >= starts[None, :], starts[None, :], 0), axis=1, keepdims=True)

    def column_parts(layer):
        qkv = w_qkv[layer].astype(BF).reshape(piece, 3, seq, group).transpose(2, 0, 1, 3)
        up = w_up[layer].astype(BF).reshape(piece, fsdp, seq, unit_rows).transpose(2, 0, 1, 3)
        return qkv.reshape(seq, piece, 3 * group), up.reshape(seq, piece, inner)

    def pad_cols(values, cols):
        return jnp.pad(values, [(0, 0)] * (values.ndim - 1) + [(0, cols - values.shape[-1])])

    def beside(columns, rows):
        rows = rows.reshape(piece, 4, group).transpose(1, 0, 2).reshape(4 * piece, group)
        return jnp.concatenate([columns, rows], axis=1)

    def apart(joined):
        rows = joined[..., 3 * group :].reshape(-1, 4, piece, group)
        return rows.transpose(0, 2, 1, 3).reshape(-1, piece, 4 * group)

    def unturn(gathered):
        rest = gathered.shape[1:]
        return gathered.reshape((4, 2) + rest).transpose((1, 0) + tuple(range(2, 2 + len(rest)))).reshape(-1, rest[-1])

    def rows_quarter(shard, size):
        whole = lax.all_gather(shard.astype(BF), BOTH, axis=0, tiled=True)
        return lax.dynamic_slice_in_dim(whole, place * size, size, 0)

    qkv_low = [None, None]
    out_low = [None, None]
    up_low = [None, None]
    down_low = [None, None]
    norms = jnp.stack([norm_gains, norm_shifts]).astype(BF).reshape(1, 1, 8 * piece)
    qkv_parts = [None, None]
    up_parts = [None, None]
    for layer in range(LAYERS):
        qkv_parts[layer], up_parts[layer] = column_parts(layer)
    sent = jnp.concatenate([qkv_parts[0], jnp.broadcast_to(pad_cols(norms, 3 * group), (seq, 8, 3 * group))], axis=1)
    early = exchange_seq(sent)
    if ruled:
        norm_rows = jnp.pad(pad_cols(early[:, piece], 4 * group), ((0, 4), (0, 0)))
        out_rows = turn(w_out.astype(BF))
        early = beside(early[:, :piece].reshape(seq * piece, 3 * group), out_rows[0])
        early = jnp.concatenate([early, norm_rows])
        attn_gather = [Gather(early), None]
        mark = attn_gather[0].advance()
    else:
        early = lax.all_gather(early, "fsdp", axis=0, tiled=False)
        qkv_low[0] = early[:, :, :piece].reshape(width, 3 * group)
        out_low[0] = rows_quarter(w_out[0], group)
        norm_low = early[:, :, piece, : 8 * piece]
        mark = []
    all_tokens = gather_seq(after(tokens, *mark))
    later = jnp.concatenate([up_parts[0], pad_cols(qkv_parts[1], inner), up_parts[1]], axis=1)
    later = exchange_seq(after(later, *mark))
    up_first = later[:, :piece].reshape(seq * piece, inner)
    qkv_next = later[:, piece : 2 * piece, : 3 * group].reshape(seq * piece, 3 * group)
    up_next = later[:, 2 * piece :].reshape(seq * piece, inner)
    if ruled:
        attn_gather[0].advance()
        mark = attn_gather[0].advance()
        low_down = w_down.astype(BF)
        mlp_gather = [
            Gather(jnp.concatenate([up_first, low_down[0]])),
            Gather(jnp.concatenate([up_next, low_down[1]])),
        ]
        attn_gather[1] = Gather(beside(qkv_next, out_rows[1]))
        mark = attn_gather[0].advance()
        mark = mlp_gather[0].advance(*mark)
        attn_gather[0].advance(*mark)
        early = attn_gather[0].result
        norm_low = early[:, 4 * piece : 4 * piece + 4, : 8 * piece]
    else:
        up_low[0] = lax.all_gather(up_first, "fsdp", axis=0, tiled=True)
        qkv_low[1] = lax.all_gather(qkv_next, "fsdp", axis=0, tiled=True)
        up_low[1] = lax.all_gather(up_next, "fsdp", axis=0, tiled=True)
        down_low[0] = lax.all_gather(w_down[0].astype(BF), "fsdp", axis=0, tiled=True)
        out_low[1] = rows_quarter(w_out[1], group)
        down_low[1] = lax.all_gather(w_down[1].astype(BF), "fsdp", axis=0, tiled=True)

    norm_low = norm_low.reshape(fsdp * seq, 2, LAYERS, 2, piece)
    norm_low = norm_low.transpose(1, 2, 3, 0, 4).reshape(2, LAYERS, 2, width).astype(F32)
    gains, shifts = norm_low[0], norm_low[1]
    def take_attn(layer):
        joined = attn_gather[layer].result[:, : 4 * piece]
        qkv_low[layer] = joined[:, :, : 3 * group].reshape(width, 3 * group)
        out_low[layer] = unturn(apart(joined))

    def take_mlp(layer):
        joined = mlp_gather[layer].result
        up_low[layer] = joined[:, : 4 * piece].reshape(width, inner)
        down_low[layer] = joined[:, 4 * piece :].reshape(inner, width)

    plan = {}
    if ruled:
        plan = {
            ("mixed", 0): [mlp_gather[0]],
            ("attended", 0): [mlp_gather[0]],
            ("scatter_a", 0): [mlp_gather[0], attn_gather[1]],
            ("gather_b", 0): [mlp_gather[0], attn_gather[1]],
            ("normed_b", 0): [attn_gather[1]],
            ("scatter_b", 0): [attn_gather[1], mlp_gather[1]],
            ("gather_a", 1): [attn_gather[1], mlp_gather[1]],
            ("mixed", 1): [mlp_gather[1]],
            ("scatter_a", 1): [mlp_gather[1]],
            ("gather_b", 1): [mlp_gather[1]],
        }

    def steps(what, layer):
        def work(gate):
            return sum([each.advance(gate) for each in plan.get((what, layer), [])], [])

        return work

    def beside_main(value, what, layer):
        moved = steps(what, layer)(value)
        return after(value, *moved)

    hidden = tokens.astype(F32)
    saved = []
    first_cot = None
    for layer in range(LAYERS):
        unit_a, inverse_a = norm_parts(hidden)
        if layer == 0:
            normed_a = (norm_parts(all_tokens.astype(F32))[0] * gains[0, 0] + shifts[0, 0]).astype(BF)
        else:
            normed_a = (unit_a * gains[layer, 0] + shifts[layer, 0]).astype(BF)
            normed_a = gather_seq(normed_a, steps("gather_a", layer))
        normed_a = beside_main(normed_a, "normed_a", layer)
        if ruled:
            take_attn(layer)
        mixed = mul(normed_a, qkv_low[layer]).astype(BF)
        if layer == LAYERS - 1:
            first_cot = gather_seq(after((BRANCH_SCALE * out_grad.astype(F32)).astype(BF), mixed))
        mixed = beside_main(mixed, "mixed", layer)
        attended, totals = attend(first, mixed)
        attended = beside_main(attended, "attended", layer)
        hidden = hidden + BRANCH_SCALE * scatter_seq(mul(attended, out_low[layer]), steps("scatter_a", layer))
        unit_b, inverse_b = norm_parts(hidden)
        normed_b = (unit_b * gains[layer, 1] + shifts[layer, 1]).astype(BF)
        normed_b = gather_seq(normed_b, steps("gather_b", layer))
        if layer == LAYERS - 1:
            normed_b = after(normed_b, first_cot)
        normed_b = beside_main(normed_b, "normed_b", layer)
        if ruled:
            take_mlp(layer)
        upper = mul(normed_b, up_low[layer])
        active = gelu_tanh(upper).astype(BF)
        hidden = hidden + BRANCH_SCALE * scatter_seq(mul(active, down_low[layer]), steps("scatter_b", layer))
        saved.append((unit_a, inverse_a, normed_a, mixed, attended, totals, unit_b, inverse_b, normed_b, upper, active))
    outputs = hidden.astype(BF)

    cot = out_grad.astype(F32)
    norm_sums = []
    column_back = {}
    row_back = {}

    def rows_blocks(grad):
        each = grad.shape[0] // 8
        return grad.reshape(2, 4, each, -1).transpose(1, 0, 2, 3).reshape(8, each, -1)

    def rows_whole(grad):
        spread = jnp.zeros((seq,) + grad.shape, BF)
        spread = lax.dynamic_update_index_in_dim(spread, grad.astype(BF), place, 0).reshape(seq * grad.shape[0], -1)
        return lax.psum_scatter(spread, BOTH, scatter_dimension=0, tiled=True).astype(F32)

    def cols_whole(grad):
        blocks = grad.astype(BF).reshape(fsdp, seq * piece, -1)
        return lax.psum_scatter(blocks, "fsdp", scatter_dimension=0, tiled=False).astype(F32)

    sums_of = {}

    def start_attn(layer, grad_qkv, grad_out):
        if not ruled:
            column_back["qkv", layer], row_back["out", layer] = cols_whole(grad_qkv), rows_whole(grad_out)
            return []
        columns = grad_qkv.astype(BF).reshape(fsdp, seq * piece, -1)
        joined = jax.vmap(beside)(columns, rows_blocks(grad_out.astype(BF)))
        sums_of["attn", layer] = Reduce(joined)
        return [joined]

    def start_mlp(layer, grad_up, grad_down):
        if not ruled:
            column_back["up", layer] = cols_whole(grad_up)
            down = grad_down.astype(BF).reshape(fsdp, unit_rows, -1)
            row_back["down", layer] = lax.psum_scatter(down, "fsdp", scatter_dimension=0, tiled=False).astype(F32)
            return []
        columns = grad_up.astype(BF).reshape(fsdp, seq * piece, -1)
        joined = jnp.concatenate([columns, grad_down.astype(BF).reshape(fsdp, unit_rows, -1)], axis=1)
        sums_of["mlp", layer] = Reduce(joined)
        return [joined]

    def step_sums(gate, *names):
        return sum([sums_of[name].advance(gate) for name in names], []) if ruled else []

    back_plan = {
        ("scatter_b", 1): [("mlp", 1)],
        ("gather_a", 1): [("mlp", 1)],
        ("scatter_a", 1): [("mlp", 1), ("attn", 1)],
        ("gather_b", 0): [("mlp", 1), ("attn", 1)],
        ("scatter_b", 0): [("mlp", 1), ("mlp", 0), ("attn", 1)],
        ("gather_a", 0): [("mlp", 0), ("attn", 1)],
        ("back", 0): [("mlp", 0), ("attn", 1)],
        ("scatter_a", 0): [("attn", 0), ("mlp", 0)],
    }
    for layer in reversed(range(LAYERS)):
        unit_a, inverse_a, normed_a, mixed, attended, totals, unit_b, inverse_b, normed_b, upper, active = saved[layer]
        if layer == LAYERS - 1:
            down_cot = first_cot
        else:
            down_cot = gather_seq(
                (BRANCH_SCALE * cot).astype(BF),
                lambda gate: step_sums(gate, *back_plan.get(("gather_b", layer), [])),
            )
        upper_cot = (gelu_slope(upper) * dot_t(down_cot, down_low[layer])).astype(BF)

        def mlp_work(gate):
            held = after(upper_cot, gate)
            moved = start_mlp(layer, t_dot(normed_b, held), t_dot(active, after(down_cot, gate)))
            return moved + step_sums(gate, *back_plan.get(("scatter_b", layer), []))

        second_cot = scatter_seq(dot_t(upper_cot, up_low[layer]), mlp_work)
        back, gain_sum_b, shift_sum_b = norm_back(unit_b, inverse_b, gains[layer, 1], second_cot)
        cot = cot + back
        attn_cot = gather_seq(
            (BRANCH_SCALE * cot).astype(BF),
            lambda gate: step_sums(gate, *back_plan.get(("gather_a", layer), [])),
        )
        attended_cot = dot_t(attn_cot, out_low[layer]).astype(BF)
        mixed_cot = attend_back(first, mixed, totals, attended_cot)
        moved = step_sums(mixed_cot, *back_plan.get(("back", layer), []))
        if moved:
            mixed_cot = after(mixed_cot, *moved)

        def attn_work(gate):
            held = after(mixed_cot, gate)
            moved = start_attn(layer, t_dot(normed_a, held), t_dot(attended, after(attn_cot, gate)))
            return moved + step_sums(gate, *back_plan.get(("scatter_a", layer), []))

        normed_cot = scatter_seq(dot_t(mixed_cot, qkv_low[layer]), attn_work)
        back, gain_sum_a, shift_sum_a = norm_back(unit_a, inverse_a, gains[layer, 0], normed_cot)
        cot = cot + back
        norm_sums.append(jnp.stack([gain_sum_a, gain_sum_b, shift_sum_a, shift_sum_b]))

    sums = jnp.concatenate(norm_sums[::-1])

    def take(layer):
        joined = sums_of["attn", layer].result
        column_back["qkv", layer], out_t = joined[:, : 3 * group], apart(joined[None])[0]
        joined = sums_of["mlp", layer].result
        column_back["up", layer] = joined[: 4 * piece]
        row_back["out", layer], row_back["down", layer] = turn(out_t.astype(BF)).astype(F32), joined[4 * piece :]

    def home(layer):
        both = jnp.concatenate([column_back["up", layer], column_back["qkv", layer]], axis=1).astype(BF)
        both = exchange_seq(both.reshape(seq, piece, -1)).astype(F32)
        qkv = both[:, :, inner:].reshape(seq, piece, 3, group).transpose(1, 2, 0, 3).reshape(piece, -1)
        up = both[:, :, :inner].reshape(seq, piece, fsdp, unit_rows).transpose(1, 2, 0, 3)
        return up.reshape(piece, -1), qkv

    if ruled:
        mark = sums_of["attn", 0].advance(sums) + sums_of["mlp", 0].advance(sums)
        take(1)
        home_1 = home(1)
        sums = after(sums, *mark)
        for bit in (1, 2):
            sums = sums + swap_seq(sums, bit)
        mark = sums_of["attn", 0].advance(sums)
        sums = after(sums, *mark)
        for bit in (1, 2):
            sums = sums + lax.ppermute(sums, "fsdp", [(f, f ^ bit) for f in range(8)])
        mark = sums_of["attn", 0].advance(sums)
        sums = after(sums, *mark)
        sums = sums + lax.ppermute(sums, "fsdp", [(f, f ^ 4) for f in range(8)])
        sums_of["attn", 0].advance(sums)
        take(0)
        home_0 = home(0)
    else:
        home_0, home_1 = home(0), home(1)
        sums = lax.psum(sums, BOTH)
    up_grads, qkv_grads = zip(home_0, home_1)
    whose = lax.axis_index("fsdp") * seq + place
    sums = lax.dynamic_slice_in_dim(sums, whose * piece, piece, 1).reshape(LAYERS, 4, piece)
    return (
        outputs,
        cot.astype(BF),
        sums[:, :2],
        sums[:, 2],
        sums[:, 3],
        jnp.stack(qkv_grads),
        jnp.stack([row_back["out", layer] for layer in range(LAYERS)]),
        jnp.stack(up_grads),
        jnp.stack([row_back["down", layer] for layer in range(LAYERS)]),
    )


def solution(mesh):
    rows = P(BOTH, None)
    thirds = P(None, None, BOTH)
    middle = P(None, BOTH, None)
    return jax.shard_map(
        shards,
        mesh=mesh,
        in_specs=(rows, thirds, thirds, middle, middle, middle, middle, rows, P("fsdp", None)),
        out_specs=(rows, rows, thirds, P(None, BOTH), P(None, BOTH), middle, middle, middle, middle),
        check_vma=False,
    )
```

time: 598 us -> 464 us (0.78)
  waiting for transfers between devices: 313 us -> 136 us
  starting transfers between devices: 67.6 us -> 107 us
  other arithmetic: 58.4 us -> 67.7 us
  between operations: 11.7 us -> 4.43 us
    ppermute x28 -> x57, waiting for transfers between devices: 199 us -> 68.4 us  [the longest x24 36.3 us: over_line(): lax.ppermute(block, 'fsdp', [(f, 2 * RING_NEXT[f // 2] + f % 2) for f in...]
    ppermute x28 -> x57, starting transfers between devices: 13.8 us -> 58.1 us  [the longest x32 30 us: over_side(): return lax.ppermute(block, 'fsdp', [(f, f ^ 1) for f in range(8)])]
    ppermute x46 -> x42, waiting for transfers between devices: 105 us -> 64 us  [swap_seq(): return lax.ppermute(values, 'seq', [(s, s ^ bit) for s in range(4)])]
    dot_general x6 -> x0, local copies, waits for them, and re-layouts: 13.4 us -> none  [t_dot(): lax.dot_general(left, right, (((0,), (0,)), ((), ())), preferred_element_...]
    dynamic_update_slice x10 -> x31, local copies, waits for them, and re-layouts: 2.25 us -> 8.46 us  [put(): self.result = lax.dynamic_update_index_in_dim(self.result, block, place, 0)]
    convert_element_type x21 -> x26, other arithmetic: 12.8 us -> 18.9 us  [the longest x12 10.9 us: advance(): total = total.astype(BF)]
    unnamed x216 -> x313, local copies, waits for them, and re-layouts: 19.8 us -> 22.6 us
    ppermute x46 -> x42, starting transfers between devices: 43.4 us -> 41.9 us  [swap_seq(): return lax.ppermute(values, 'seq', [(s, s ^ bit) for s in range(4)])]
  transfers between devices with their start and end apart: 81 -> 104, of which waited for: 47 -> 48; matrix products, arithmetic and copies ran while one was open for 20% -> 26% of each run, Pallas kernels for 2% -> 4%
where the time goes in v2:
time: 464 us; the launch traced here: 456 us
  waiting for transfers between devices  136 us (29%)
  starting transfers between devices  107 us (23%)
  local copies, waits for them, and re-layouts  69.6 us (15%)
  other arithmetic  67.7 us (15%)
  matrix products  42.2 us (9%)
  Pallas kernels  29.8 us (6%)
    ppermute x42, waiting for transfers between devices, swap_seq(): return lax.ppermute(values, 'seq', [(s, s ^ bit) for s in range(4)])  64 us
    ppermute x42, starting transfers between devices, swap_seq(): return lax.ppermute(values, 'seq', [(s, s ^ bit) for s in range(4)])  41.9 us
    ppermute x24, waiting for transfers between devices, over_line(): lax.ppermute(block, 'fsdp', [(f, 2 * RING_NEXT[f // 2] + f % 2) for f in...  36.3 us
    ppermute x32, starting transfers between devices, over_side(): return lax.ppermute(block, 'fsdp', [(f, f ^ 1) for f in range(8)])  30 us
    ppermute x32, waiting for transfers between devices, over_side(): return lax.ppermute(block, 'fsdp', [(f, f ^ 1) for f in range(8)])  28.8 us
    ppermute x24, starting transfers between devices, over_line(): lax.ppermute(block, 'fsdp', [(f, 2 * RING_NEXT[f // 2] + f % 2) for f in...  26.2 us
    unnamed x313, local copies, waits for them, and re-layouts  22.6 us
    pallas_call x2, Pallas kernels, attend_back(): pl.pallas_call(attend_back_kernel, out_shape=jax.ShapeDtypeStruct((length...  18.2 us
  transfers between devices with their start and end apart: 104, of which 48 were waited for; matrix products, arithmetic and copies ran while one was open for 26% of the time, Pallas kernels for 4%

profile of v2, /device:TPU:0, one launch (start us, length us, event | category | flops | bytes accessed | tf_op | source)
XLA Modules:
  0.0 456.5 jit_solution(2937166991872846573)
XLA Ops:
  7.4 6.4 %collective-permute-start.1 = (bf16[2,32,576]{2,1,0:T(8,128)(2,1)S(1)}, bf16[2,32,576]{2,1,0:T(8,128)(2,1)S(1)}, u32[]{:S(2)}, u32[]{:S(2)}) collective-permute-start(bf16[2,32,576]{2,1,0:T(8,128)(2,1)S(1)} %fusion.156), channel_id=1, source_target_pairs={{0,2},{1,3},{2,0},{3,1},{4,6},{5,7},{6,4},{7,5},{8,10},{9,11},{10,... | collective-permute-start | bytes 221192 | tf_op jit(solution)/shard_map/ppermute | solution.py:33
  21.7 3.8 collective-permute-done.6
  28.3 3.8 collective-permute-done.8
  40.6 5.0 %collective-permute-done.11 = bf16[104,768]{1,0:T(8,128)(2,1)S(1)} collective-permute-done((bf16[104,768]{1,0:T(8,128)(2,1)S(1)}, bf16[104,768]{1,0:T(8,128)(2,1)S(1)}, u32[]{:S(2)}, u32[]{:S(2)}) %collective-permute-start.11) | collective-permute-done | bytes 159776 | tf_op jit(solution)/shard_map/ppermute | solution.py:82
  59.9 5.8 %attend.2 = (bf16[1024,192]{1,0:T(8,128)(2,1)S(1)}, f32[1024,3]{1,0:T(8,128)S(1)}) custom-call(s32[1024,1]{1,0:T(8,128)S(1)} %copy.422.first_ref, bf16[1024,576]{1,0:T(8,128)(2,1)S(1)} %convolution_convert_fusion.1.mixed_ref), custom_call_target="tpu_custom_call" | custom-call | tf_op jit(solution)/shard_map/attend/pallas_call | solution.py:202
  73.0 6.6 %collective-permute-done.23 = bf16[192,768]{1,0:T(8,128)(2,1)S(1)} collective-permute-done((bf16[192,768]{1,0:T(8,128)(2,1)}, bf16[192,768]{1,0:T(8,128)(2,1)S(1)}, u32[]{:S(2)}, u32[]{:S(2)}) %collective-permute-start.23) | collective-permute-done | bytes 294944 | tf_op jit(solution)/shard_map/ppermute | solution.py:82
  105.6 4.5 collective-permute-done.22
  110.1 3.4 fusion.10
  119.6 4.5 collective-permute-done.33
  127.8 3.9 collective-permute-done.29
  155.6 5.8 %attend.3 = (bf16[1024,192]{1,0:T(8,128)(2,1)S(1)}, f32[1024,3]{1,0:T(8,128)S(1)}) custom-call(s32[1024,1]{1,0:T(8,128)S(1)} %copy.422.first_ref, bf16[1024,576]{1,0:T(8,128)(2,1)S(1)} %convolution_convert_fusion.mixed_ref), custom_call_target="tpu_custom_call" | custom-call | tf_op jit(solution)/shard_map/attend/pallas_call | solution.py:202
  171.8 7.7 %collective-permute-done.43 = bf16[256,768]{1,0:T(8,128)(2,1)S(1)} collective-permute-done((bf16[256,768]{1,0:T(8,128)(2,1)S(1)}, bf16[256,768]{1,0:T(8,128)(2,1)S(1)}, u32[]{:S(2)}, u32[]{:S(2)}) %collective-permute-start.43) | collective-permute-done | bytes 393248 | tf_op jit(solution)/shard_map/ppermute | solution.py:33
  180.7 5.6 %collective-permute-done.39 = bf16[256,768]{1,0:T(8,128)(2,1)S(1)} collective-permute-done((bf16[256,768]{1,0:T(8,128)(2,1)S(1)}, bf16[256,768]{1,0:T(8,128)(2,1)S(1)}, u32[]{:S(2)}, u32[]{:S(2)}) %collective-permute-start.39) | collective-permute-done | bytes 393248 | tf_op jit(solution)/shard_map/ppermute | solution.py:33
  188.9 7.8 %collective-permute-done.41 = bf16[256,768]{1,0:T(8,128)(2,1)S(1)} collective-permute-done((bf16[256,768]{1,0:T(8,128)(2,1)S(1)}, bf16[256,768]{1,0:T(8,128)(2,1)S(1)}, u32[]{:S(2)}, u32[]{:S(2)}) %collective-permute-start.41) | collective-permute-done | bytes 393248 | tf_op jit(solution)/shard_map/ppermute | solution.py:33
  202.8 3.4 multiply_convert_fusion.1
  210.4 3.3 fusion.179
  222.8 5.1 %collective-permute-done.52 = bf16[256,768]{1,0:T(8,128)(2,1)S(1)} collective-permute-done((bf16[256,768]{1,0:T(8,128)(2,1)S(1)}, bf16[256,768]{1,0:T(8,128)(2,1)S(1)}, u32[]{:S(2)}, u32[]{:S(2)}) %collective-permute-start.52) | collective-permute-done | bytes 393248 | tf_op jit(solution)/shard_map/ppermute | solution.py:33
  229.0 6.5 %collective-permute-done.50 = bf16[256,768]{1,0:T(8,128)(2,1)S(1)} collective-permute-done((bf16[256,768]{1,0:T(8,128)(2,1)S(1)}, bf16[256,768]{1,0:T(8,128)(2,1)S(1)}, u32[]{:S(2)}, u32[]{:S(2)}) %collective-permute-start.50) | collective-permute-done | bytes 393248 | tf_op jit(solution)/shard_map/ppermute | solution.py:33
  239.4 7.7 %collective-permute-done.53 = bf16[256,768]{1,0:T(8,128)(2,1)S(1)} collective-permute-done((bf16[256,768]{1,0:T(8,128)(2,1)S(1)}, bf16[256,768]{1,0:T(8,128)(2,1)S(1)}, u32[]{:S(2)}, u32[]{:S(2)}) %collective-permute-start.53) | collective-permute-done | bytes 393248 | tf_op jit(solution)/shard_map/ppermute | solution.py:33
  255.0 9.3 %attend_back.2 = bf16[1024,576]{1,0:T(8,128)(2,1)S(1)} custom-call(s32[1024,1]{1,0:T(8,128)S(1)} %copy.422.first_ref, bf16[1024,576]{1,0:T(8,128)(2,1)S(1)} %convolution_convert_fusion.mixed_ref, f32[1024,3]{1,0:T(8,128)S(1)} %copy-done.10, bf16[1024,192]{1,0:T(8,128)(2,1)S(1)} %copy-done), custom_call_target="tpu_custom_call" | custom-call | tf_op jit(solution)/shard_map/attend_back/pallas_call | solution.py:251
  303.7 3.3 multiply_convert_fusion
  357.9 8.9 %attend_back.3 = bf16[1024,576]{1,0:T(8,128)(2,1)S(1)} custom-call(s32[1024,1]{1,0:T(8,128)S(1)} %copy.422.first_ref, bf16[1024,576]{1,0:T(8,128)(2,1)S(1)} %convolution_convert_fusion.1.mixed_ref, f32[1024,3]{1,0:T(8,128)S(1)} %copy-done.8, bf16[1024,192]{1,0:T(8,128)(2,1)S(1)} %copy.453.cot_ref), custom_call_target="tpu_custom_call" | custom-call | tf_op jit(solution)/shard_map/attend_back/pallas_call | solution.py:251
  439.1 3.3 collective-permute-done.95
  444.6 4.2 collective-permute-start.99
  (832 shorter events, 322.5 us)
Async XLA Ops:
  19.3 14.4 %collective-permute-start.3 = (bf16[256,768]{1,0:T(8,128)(2,1)S(1)}, bf16[256,768]{1,0:T(8,128)(2,1)S(1)}, u32[]{:S(2)}, u32[]{:S(2)}) collective-permute-start(bf16[256,768]{1,0:T(8,128)(2,1)S(1)} %copy-done.39), channel_id=1, source_target_pairs={{0,2},{1,3},{2,0},{3,1},{4,6},{5,7},{6,4},{7,5},{8,10},{9,11},{10,... | collective-permute-start | bytes 1179656 | tf_op jit(solution)/shard_map/ppermute | solution.py:33
  34.7 13.6 %collective-permute-start.4 = (bf16[2,256,768]{2,1,0:T(8,128)(2,1)}, bf16[2,256,768]{2,1,0:T(8,128)(2,1)}, u32[]{:S(2)}, u32[]{:S(2)}) collective-permute-start(bf16[2,256,768]{2,1,0:T(8,128)(2,1)} %pad_maximum_fusion.12), channel_id=1, source_target_pairs={{0,1},{1,0},{2,3},{3,2},{4,5},{5,4},{6,7},{7,6},{8,9},{9,8},{10,11... | collective-permute-start | bytes 2359304 | tf_op jit(solution)/shard_map/ppermute | solution.py:33
  39.8 14.2 %collective-permute-start.14 = (bf16[192,768]{1,0:T(8,128)(2,1)}, bf16[192,768]{1,0:T(8,128)(2,1)}, u32[]{:S(2)}, u32[]{:S(2)}) collective-permute-start(bf16[192,768]{1,0:T(8,128)(2,1)} %pad_maximum_fusion.24), channel_id=1, source_target_pairs={{0,8},{4,12},{8,24},{12,28},{16,0},{20,4},{24,16},{28,20},{1,9},{5... | collective-permute-start | bytes 884744 | tf_op jit(solution)/shard_map/ppermute | solution.py:78
  71.4 14.3 %collective-permute-start.24 = (bf16[192,768]{1,0:T(8,128)(2,1)}, bf16[192,768]{1,0:T(8,128)(2,1)S(1)}, u32[]{:S(2)}, u32[]{:S(2)}) collective-permute-start(bf16[192,768]{1,0:T(8,128)(2,1)} %collective-permute-done.14), channel_id=1, source_target_pairs={{0,4},{4,0},{8,12},{12,8},{16,20},{20,16},{24,28},{28,24},{1,5},{5... | collective-permute-start | bytes 884744 | tf_op jit(solution)/shard_map/ppermute | solution.py:82
  83.7 14.5 %collective-permute-start.25 = (bf16[192,768]{1,0:T(8,128)(2,1)}, bf16[192,768]{1,0:T(8,128)(2,1)S(1)}, u32[]{:S(2)}, u32[]{:S(2)}) collective-permute-start(bf16[192,768]{1,0:T(8,128)(2,1)} %collective-permute-done.15), channel_id=1, source_target_pairs={{0,4},{4,0},{8,12},{12,8},{16,20},{20,16},{24,28},{28,24},{1,5},{5... | collective-permute-start | bytes 884744 | tf_op jit(solution)/shard_map/ppermute | solution.py:82
  135.5 15.2 %collective-permute-start.45 = (bf16[192,768]{1,0:T(8,128)(2,1)}, bf16[192,768]{1,0:T(8,128)(2,1)}, u32[]{:S(2)}, u32[]{:S(2)}) collective-permute-start(bf16[192,768]{1,0:T(8,128)(2,1)} %pad_maximum_fusion.25), channel_id=1, source_target_pairs={{0,4},{4,0},{8,12},{12,8},{16,20},{20,16},{24,28},{28,24},{1,5},{5... | collective-permute-start | bytes 884744 | tf_op jit(solution)/shard_map/ppermute | solution.py:82
  147.8 21.4 %collective-permute-start.46 = (bf16[192,768]{1,0:T(8,128)(2,1)}, bf16[192,768]{1,0:T(8,128)(2,1)}, u32[]{:S(2)}, u32[]{:S(2)}) collective-permute-start(bf16[192,768]{1,0:T(8,128)(2,1)} %collective-permute-done.31), channel_id=1, source_target_pairs={{0,4},{4,0},{8,12},{12,8},{16,20},{20,16},{24,28},{28,24},{1,5},{5... | collective-permute-start | bytes 884744 | tf_op jit(solution)/shard_map/ppermute | solution.py:82
  165.5 14.2 %collective-permute-start.40 = (bf16[192,768]{1,0:T(8,128)(2,1)}, bf16[192,768]{1,0:T(8,128)(2,1)S(1)}, u32[]{:S(2)}, u32[]{:S(2)}) collective-permute-start(bf16[192,768]{1,0:T(8,128)(2,1)} %collective-permute-done.37), channel_id=1, source_target_pairs={{0,8},{4,12},{8,24},{12,28},{16,0},{20,4},{24,16},{28,20},{1,9},{5... | collective-permute-start | bytes 884744 | tf_op jit(solution)/shard_map/ppermute | solution.py:78
  166.3 13.4 %collective-permute-start.47 = (bf16[192,768]{1,0:T(8,128)(2,1)}, bf16[192,768]{1,0:T(8,128)(2,1)S(1)}, u32[]{:S(2)}, u32[]{:S(2)}) collective-permute-start(bf16[192,768]{1,0:T(8,128)(2,1)} %collective-permute-done.37), channel_id=1, source_target_pairs={{0,4},{4,0},{8,12},{12,8},{16,20},{20,16},{24,28},{28,24},{1,5},{5... | collective-permute-start | bytes 884744 | tf_op jit(solution)/shard_map/ppermute | solution.py:82
  171.4 14.9 %collective-permute-start.39 = (bf16[256,768]{1,0:T(8,128)(2,1)S(1)}, bf16[256,768]{1,0:T(8,128)(2,1)S(1)}, u32[]{:S(2)}, u32[]{:S(2)}) collective-permute-start(bf16[256,768]{1,0:T(8,128)(2,1)S(1)} %fusion.67), channel_id=1, source_target_pairs={{0,2},{1,3},{2,0},{3,1},{4,6},{5,7},{6,4},{7,5},{8,10},{9,11},{10,... | collective-permute-start | bytes 1179656 | tf_op jit(solution)/shard_map/ppermute | solution.py:33
  179.6 17.5 %collective-permute-start.44 = (bf16[2,256,768]{2,1,0:T(8,128)(2,1)S(1)}, bf16[2,256,768]{2,1,0:T(8,128)(2,1)S(1)}, u32[]{:S(2)}, u32[]{:S(2)}) collective-permute-start(bf16[2,256,768]{2,1,0:T(8,128)(2,1)S(1)} %pad_maximum_fusion.16), channel_id=1, source_target_pairs={{0,1},{1,0},{2,3},{3,2},{4,5},{5,4},{6,7},{7,6},{8,9},{9,8},{10,11... | collective-permute-start | bytes 2359304 | tf_op jit(solution)/shard_map/ppermute | solution.py:33
  179.7 17.8 %collective-permute-start.48 = (bf16[192,768]{1,0:T(8,128)(2,1)S(1)}, bf16[192,768]{1,0:T(8,128)(2,1)S(1)}, u32[]{:S(2)}, u32[]{:S(2)}) collective-permute-start(bf16[192,768]{1,0:T(8,128)(2,1)S(1)} %collective-permute-done.40), channel_id=1, source_target_pairs={{0,4},{4,0},{8,12},{12,8},{16,20},{20,16},{24,28},{28,24},{1,5},{5... | collective-permute-start | bytes 884744 | tf_op jit(solution)/shard_map/ppermute | solution.py:82
  215.9 12.1 %collective-permute-start.52 = (bf16[256,768]{1,0:T(8,128)(2,1)S(1)}, bf16[256,768]{1,0:T(8,128)(2,1)S(1)}, u32[]{:S(2)}, u32[]{:S(2)}) collective-permute-start(bf16[256,768]{1,0:T(8,128)(2,1)S(1)} %fusion.69), channel_id=1, source_target_pairs={{0,2},{1,3},{2,0},{3,1},{4,6},{5,7},{6,4},{7,5},{8,10},{9,11},{10,... | collective-permute-start | bytes 1179656 | tf_op jit(solution)/shard_map/ppermute | solution.py:33
  221.9 13.5 %collective-permute-start.50 = (bf16[256,768]{1,0:T(8,128)(2,1)S(1)}, bf16[256,768]{1,0:T(8,128)(2,1)S(1)}, u32[]{:S(2)}, u32[]{:S(2)}) collective-permute-start(bf16[256,768]{1,0:T(8,128)(2,1)S(1)} %fusion.68), channel_id=1, source_target_pairs={{0,2},{1,3},{2,0},{3,1},{4,6},{5,7},{6,4},{7,5},{8,10},{9,11},{10,... | collective-permute-start | bytes 1179656 | tf_op jit(solution)/shard_map/ppermute | solution.py:33
  222.3 16.3 %collective-permute-start.54 = (bf16[192,768]{1,0:T(8,128)(2,1)S(1)}, bf16[192,768]{1,0:T(8,128)(2,1)S(1)}, u32[]{:S(2)}, u32[]{:S(2)}) collective-permute-start(bf16[192,768]{1,0:T(8,128)(2,1)S(1)} %get-tuple-element.156), channel_id=1, source_target_pairs={{0,4},{4,0},{8,12},{12,8},{16,20},{20,16},{24,28},{28,24},{1,5},{5... | collective-permute-start | bytes 884744 | tf_op jit(solution)/shard_map/ppermute | solution.py:82
  270.6 15.6 %collective-permute-start.57 = (bf16[256,768]{1,0:T(8,128)(2,1)}, bf16[256,768]{1,0:T(8,128)(2,1)}, u32[]{:S(2)}, u32[]{:S(2)}) collective-permute-start(bf16[256,768]{1,0:T(8,128)(2,1)} %fusion.70), channel_id=1, source_target_pairs={{0,2},{1,3},{2,0},{3,1},{4,6},{5,7},{6,4},{7,5},{8,10},{9,11},{10,... | collective-permute-start | bytes 1179656 | tf_op jit(solution)/shard_map/ppermute | solution.py:33
  347.6 19.2 %collective-permute-start.77 = (bf16[192,768]{1,0:T(8,128)(2,1)}, bf16[192,768]{1,0:T(8,128)(2,1)}, u32[]{:S(2)}, u32[]{:S(2)}) collective-permute-start(bf16[192,768]{1,0:T(8,128)(2,1)} %fusion.56), channel_id=1, source_target_pairs={{0,8},{4,12},{8,24},{12,28},{16,0},{20,4},{24,16},{28,20},{1,9},{5... | collective-permute-start | bytes 884744 | tf_op jit(solution)/shard_map/ppermute | solution.py:78
  349.1 17.7 %collective-permute-start.76 = (bf16[192,768]{1,0:T(8,128)(2,1)}, bf16[192,768]{1,0:T(8,128)(2,1)}, u32[]{:S(2)}, u32[]{:S(2)}) collective-permute-start(bf16[192,768]{1,0:T(8,128)(2,1)} %get-tuple-element.186), channel_id=1, source_target_pairs={{0,4},{4,0},{8,12},{12,8},{16,20},{20,16},{24,28},{28,24},{1,5},{5... | collective-permute-start | bytes 884744 | tf_op jit(solution)/shard_map/ppermute | solution.py:82
  349.7 17.1 %collective-permute-start.79 = (bf16[96,768]{1,0:T(8,128)(2,1)}, bf16[96,768]{1,0:T(8,128)(2,1)}, u32[]{:S(2)}, u32[]{:S(2)}) collective-permute-start(bf16[96,768]{1,0:T(8,128)(2,1)} %fusion.99), channel_id=1, source_target_pairs={{0,8},{4,12},{8,24},{12,28},{16,0},{20,4},{24,16},{28,20},{1,9},{5... | collective-permute-start | bytes 442376 | tf_op jit(solution)/shard_map/ppermute | solution.py:78
  351.0 15.8 %collective-permute-start.78 = (bf16[96,768]{1,0:T(8,128)(2,1)}, bf16[96,768]{1,0:T(8,128)(2,1)}, u32[]{:S(2)}, u32[]{:S(2)}) collective-permute-start(bf16[96,768]{1,0:T(8,128)(2,1)} %get-tuple-element.189), channel_id=1, source_target_pairs={{0,4},{4,0},{8,12},{12,8},{16,20},{20,16},{24,28},{28,24},{1,5},{5... | collective-permute-start | bytes 442376 | tf_op jit(solution)/shard_map/ppermute | solution.py:82
  374.9 19.0 %collective-permute-start.83 = (bf16[192,768]{1,0:T(8,128)(2,1)}, bf16[192,768]{1,0:T(8,128)(2,1)}, u32[]{:S(2)}, u32[]{:S(2)}) collective-permute-start(bf16[192,768]{1,0:T(8,128)(2,1)} %fusion.55), channel_id=1, source_target_pairs={{0,8},{4,12},{8,24},{12,28},{16,0},{20,4},{24,16},{28,20},{1,9},{5... | collective-permute-start | bytes 884744 | tf_op jit(solution)/shard_map/ppermute | solution.py:78
  376.3 17.5 %collective-permute-start.82 = (bf16[192,768]{1,0:T(8,128)(2,1)}, bf16[192,768]{1,0:T(8,128)(2,1)}, u32[]{:S(2)}, u32[]{:S(2)}) collective-permute-start(bf16[192,768]{1,0:T(8,128)(2,1)} %get-tuple-element.193), channel_id=1, source_target_pairs={{0,4},{4,0},{8,12},{12,8},{16,20},{20,16},{24,28},{28,24},{1,5},{5... | collective-permute-start | bytes 884744 | tf_op jit(solution)/shard_map/ppermute | solution.py:82
  377.8 72.3 %collective-permute-start.103 = (bf16[24,768]{1,0:T(8,128)(2,1)}, bf16[24,768]{1,0:T(8,128)(2,1)}, u32[]{:S(2)}, u32[]{:S(2)}) collective-permute-start(bf16[24,768]{1,0:T(8,128)(2,1)} %convert_element_type.738), channel_id=1, source_target_pairs={{0,0},{1,8},{2,16},{3,24},{4,4},{5,12},{6,20},{7,28},{8,1},{9,9},{... | collective-permute-start | bytes 110600 | tf_op jit(solution)/shard_map/ppermute | solution.py:148
  385.6 13.1 %collective-permute-start.81 = (bf16[256,768]{1,0:T(8,128)(2,1)}, bf16[256,768]{1,0:T(8,128)(2,1)}, u32[]{:S(2)}, u32[]{:S(2)}) collective-permute-start(bf16[256,768]{1,0:T(8,128)(2,1)} %fusion.72), channel_id=1, source_target_pairs={{0,2},{1,3},{2,0},{3,1},{4,6},{5,7},{6,4},{7,5},{8,10},{9,11},{10,... | collective-permute-start | bytes 1179656 | tf_op jit(solution)/shard_map/ppermute | solution.py:33
  (235 other events, 1621.4 us)

commit v3 on v2

v3 whole, which is shorter than its diff:
```python
import functools

import jax
import jax.numpy as jnp
from jax import lax
from jax.experimental import pallas as pl
from jax.experimental.pallas import tpu as pltpu
from jax.sharding import PartitionSpec as P

H = 12
HD = 64
LAYERS = 2
MAX_DOC = 512

NORM_EPS = 1e-05
BRANCH_SCALE = 0.7071067811865476
MASKED = -1e30
BF = jnp.bfloat16
F32 = jnp.float32
BOTH = ("fsdp", "seq")

RING_NEXT = (1, 3, 0, 2)


def ring_behind(line, steps):
    at = ((line ^ (line >> 1)) - steps) & 3
    return at ^ (at >> 1)


def after(value, *others):
    return lax.optimization_barrier((value,) + others)[0] if others else value


def swap_seq(values, bit):
    return lax.ppermute(values, "seq", [(s, s ^ bit) for s in range(4)])


def by_bit(bit, own, other):
    zero = bit == 0
    return jnp.where(zero, own, other), jnp.where(zero, other, own)


def gather_seq(rows, work=None):
    far = swap_seq(rows, 2)
    near = swap_seq(rows, 1)
    if work is not None:
        far = after(far, *work(rows))
    return [rows, far, near, swap_seq(far, 1)]


def scatter_seq(sent, kept, work=None):
    half = kept + swap_seq(sent, 1).astype(F32)
    sent = half[1].astype(BF)
    got = swap_seq(sent, 2)
    if work is not None:
        got = after(got, *work(sent))
    return half[0] + got.astype(F32)


def exchange_seq(parts):
    place = lax.axis_index("seq")
    y_bit, c_bit = place // 2, place % 2
    grid = parts.reshape((2, 2) + parts.shape[1:])
    kept, sent = by_bit(c_bit, grid[:, 0], grid[:, 1])
    half = jnp.stack(by_bit(c_bit, kept, swap_seq(sent, 1)), axis=1)
    kept, sent = by_bit(y_bit, half[0], half[1])
    return jnp.stack(by_bit(y_bit, kept, swap_seq(sent, 2))).reshape(parts.shape)


def over_line(block, steps=1):
    moves = []
    for f in range(8):
        line = f // 2
        for _ in range(steps):
            line = RING_NEXT[line]
        moves.append((f, 2 * line + f % 2))
    return lax.ppermute(block, "fsdp", moves)


def over_side(block):
    return lax.ppermute(block, "fsdp", [(f, f ^ 1) for f in range(8)])


def owner(steps, other=0):
    place = lax.axis_index("fsdp")
    return 2 * ring_behind(place // 2, steps) + (place % 2 ^ other)


def owners():
    count = lax.axis_size("fsdp")
    if count != 8:
        return jnp.arange(8, dtype=jnp.int32)
    return jnp.stack([owner(steps, other) for other in (0, 1) for steps in range(4)]).astype(jnp.int32)


class Gather:
    def __init__(self, block):
        self.blocks = [block]
        self.sides = []

    def advance(self, *gates):
        block = after(self.blocks[-1], *gates)
        moved = [over_side(block)]
        self.sides.append(moved[0])
        if len(self.sides) < 4:
            moved.append(over_line(block))
            self.blocks.append(moved[1])
        return moved

    def result(self):
        return self.blocks + self.sides


class Reduce:
    def __init__(self, blocks):
        self.blocks = blocks
        self.step = 0
        self.got = 0.0

    def advance(self, *gates):
        self.step += 1
        moved = [over_side(after(self.blocks[4 + self.step % 4], *gates))]
        if self.step > 1:
            moved.append(over_line(after(self.total.astype(BF), *gates)))
            self.got = moved[1].astype(F32)
        self.total = self.got + moved[0].astype(F32) + self.blocks[self.step % 4].astype(F32)
        return moved


def turn(rows):
    moves = []
    for f in range(8):
        for s in range(4):
            moves.append((f * 4 + s, (2 * s + f % 2) * 4 + f // 2))
    return lax.ppermute(rows, BOTH, moves)


ROWS = 256


def allowed_pairs(first_ref, row_start, key_start, width):
    key_pos = key_start + lax.broadcasted_iota(jnp.int32, (ROWS, width), 1)
    query_pos = row_start + lax.broadcasted_iota(jnp.int32, (ROWS, width), 0)
    first = first_ref[pl.ds(row_start, ROWS), :]
    return (key_pos <= query_pos) & (key_pos >= first)


def key_window(row_start):
    key_start = max(0, row_start - (MAX_DOC + ROWS - 1) // ROWS * ROWS)
    return key_start, row_start + ROWS - key_start


def dot_t(left, right):
    return lax.dot_general(left, right, (((1,), (1,)), ((), ())), preferred_element_type=F32)


def t_dot(left, right):
    return lax.dot_general(left, right, (((0,), (0,)), ((), ())), preferred_element_type=F32)


def parts_of(refs):
    return [ref.at[pl.ds(at, ROWS)] for ref in refs for at in range(0, ref.shape[0], ROWS)]


def row_starts(place_ref):
    return [pl.multiple_of((place_ref[0] ^ bits) * ROWS, ROWS) for bits in (0, 2, 1, 3)]


def put_part(sent_ref, kept_ref, part, values):
    if part < 2:
        kept_ref[part] = values
    else:
        sent_ref[part - 2] = values.astype(BF)


def place_blocks(info_ref, blocks, places):
    for slot, block in enumerate(blocks):
        at = info_ref[1 + slot]
        for target, first_row, rows, cols, turned in places:
            where = (at % 2 * 4 + at // 2) if turned else at
            values = block[pl.ds(first_row, rows), pl.ds(0, cols)].astype(target.dtype)
            target[pl.ds(pl.multiple_of(where * rows, 8 if turned else 32), rows), :] = values


def attend_places(blocks, qkv_weight, out_weight):
    top, each = qkv_weight.shape[0] // 8, out_weight.shape[0] // 8
    width = out_weight.shape[1]
    return [(qkv_weight, 0, top, qkv_weight.shape[1], False), (out_weight, top, each, width, True)]


def feed_places(up_weight, down_weight):
    each, width = up_weight.shape[0] // 8, up_weight.shape[1]
    return [(up_weight, 0, each, width, False), (down_weight, each, each, width, False)]


def attend_kernel(place_ref, first_ref, *refs):
    blocks, parts = refs[:8], parts_of(refs[8:-7])
    mixed_ref, attended_ref, total_ref, sent_ref, kept_ref, qkv_weight, out_weight = refs[-7:]
    length, group = attended_ref.shape
    heads = group // HD
    scale = jnp.asarray(HD ** (-0.5), BF)
    starts = row_starts(place_ref)
    place_blocks(place_ref, blocks, attend_places(blocks, qkv_weight, out_weight))
    weight = qkv_weight[...]
    for part, start in zip(parts, starts):
        mixed_ref[pl.ds(start, ROWS), :] = jnp.dot(part[...], weight, preferred_element_type=F32).astype(BF)
    for row_start in range(0, length, ROWS):
        key_start, width = key_window(row_start)
        allowed = allowed_pairs(first_ref, row_start, key_start, width)
        outs = []
        totals = []
        for head in range(heads):
            at = head * HD
            query = mixed_ref[pl.ds(row_start, ROWS), pl.ds(at, HD)] * scale
            keys = mixed_ref[pl.ds(key_start, width), pl.ds(group + at, HD)]
            values = mixed_ref[pl.ds(key_start, width), pl.ds(2 * group + at, HD)]
            scores = jnp.where(allowed, dot_t(query, keys), MASKED)
            top = jnp.max(scores, axis=1, keepdims=True)
            weights = jnp.exp(scores - top)
            total = jnp.sum(weights, axis=1, keepdims=True)
            low = (weights * (1.0 / total)).astype(BF)
            outs.append(jnp.dot(low, values, preferred_element_type=F32))
            totals.append(top + jnp.log(total))
        attended_ref[pl.ds(row_start, ROWS), :] = jnp.concatenate(outs, axis=1).astype(BF)
        total_ref[pl.ds(row_start, ROWS), :] = jnp.concatenate(totals, axis=1)
    weight = out_weight[...].astype(BF)
    for part, start in enumerate(starts):
        values = jnp.dot(attended_ref[pl.ds(start, ROWS), :], weight, preferred_element_type=F32)
        put_part(sent_ref, kept_ref, part, values)


TAKES = {"attend": 10, "attend_back": 14, "attend_sum": 5, "feed": 5, "feed_back": 8, "feed_sum": 6}


def call(kernel, name, outs, scratch, *args):
    in_specs = [pl.BlockSpec(memory_space=pltpu.SMEM)] + [pl.BlockSpec(memory_space=pltpu.VMEM)] * (len(args) - 1)
    return pl.pallas_call(
        kernel,
        in_specs=in_specs,
        out_shape=tuple(jax.ShapeDtypeStruct(shape, dtype) for shape, dtype in outs),
        scratch_shapes=[pltpu.VMEM(shape, dtype) for shape, dtype in scratch],
        cost_estimate=pl.CostEstimate(flops=TAKES[name] * 10**9, bytes_accessed=TAKES[name] * 3 * 10**6, transcendentals=0),
        compiler_params=pltpu.CompilerParams(vmem_limit_bytes=56 << 20),
        name=name,
    )(*args)


def two_parts(width):
    return [((2, ROWS, width), BF), ((2, ROWS, width), F32)]


def attend(place, first, blocks, parts, group):
    length, width = first.shape[0], blocks[0].shape[1]
    outs = [((length, 3 * group), BF), ((length, group), BF), ((length, group // HD), F32)] + two_parts(width)
    scratch = [((width, 3 * group), BF), ((group, width), F32)]
    return call(attend_kernel, "attend", outs, scratch, place, first, *blocks, *parts)


def attend_back_kernel(place_ref, first_ref, mixed_ref, total_ref, *refs):
    blocks, parts = refs[:8], parts_of(refs[8:-8])
    out_ref, sent_ref, kept_ref, qkv_weight, out_weight, cot_ref, key_acc, value_acc = refs[-8:]
    length, group = key_acc.shape
    heads = group // HD
    scale = jnp.asarray(HD ** (-0.5), BF)
    starts = row_starts(place_ref)
    place_blocks(place_ref, blocks, attend_places(blocks, qkv_weight, out_weight))
    weight = out_weight[...].astype(BF)
    for part, start in zip(parts, starts):
        cot_ref[pl.ds(start, ROWS), :] = dot_t(part[...], weight)
    key_acc[...] = jnp.zeros_like(key_acc)
    value_acc[...] = jnp.zeros_like(value_acc)
    for row_start in range(0, length, ROWS):
        key_start, width = key_window(row_start)
        allowed = allowed_pairs(first_ref, row_start, key_start, width)
        query_grads = []
        key_grads = []
        value_grads = []
        for head in range(heads):
            at = head * HD
            query = mixed_ref[pl.ds(row_start, ROWS), pl.ds(at, HD)] * scale
            keys = mixed_ref[pl.ds(key_start, width), pl.ds(group + at, HD)]
            values = mixed_ref[pl.ds(key_start, width), pl.ds(2 * group + at, HD)]
            cot = cot_ref[pl.ds(row_start, ROWS), pl.ds(at, HD)].astype(BF)
            total = total_ref[pl.ds(row_start, ROWS), pl.ds(head, 1)]
            scores = jnp.where(allowed, dot_t(query, keys) - total, MASKED)
            probs = jnp.exp(scores)
            prob_cot = dot_t(cot, values)
            delta = jnp.sum(probs * prob_cot, axis=1, keepdims=True)
            score_cot = (probs * (prob_cot - delta)).astype(BF)
            query_grads.append(jnp.dot(score_cot, keys, preferred_element_type=F32) * scale)
            key_grads.append(t_dot(score_cot, query))
            value_grads.append(t_dot(probs.astype(BF), cot))
        out_ref[pl.ds(row_start, ROWS), pl.ds(0, group)] = jnp.concatenate(query_grads, axis=1).astype(BF)
        window = pl.ds(key_start, width)
        key_acc[window, :] += jnp.concatenate(key_grads, axis=1)
        value_acc[window, :] += jnp.concatenate(value_grads, axis=1)
    out_ref[:, pl.ds(group, group)] = key_acc[...].astype(BF)
    out_ref[:, pl.ds(2 * group, group)] = value_acc[...].astype(BF)
    weight = qkv_weight[...]
    for part, start in enumerate(starts):
        put_part(sent_ref, kept_ref, part, dot_t(out_ref[pl.ds(start, ROWS), :], weight))


def attend_back(place, first, blocks, mixed, totals, parts):
    length, wide = mixed.shape
    group, width = wide // 3, blocks[0].shape[1]
    outs = [((length, wide), BF)] + two_parts(width)
    scratch = [((width, wide), BF), ((group, width), F32)] + [((length, group), F32)] * 3
    return call(attend_back_kernel, "attend_back", outs, scratch, place, first, mixed, totals, *blocks, *parts)


def joint(parts):
    return jnp.concatenate([part[...] for part in parts], axis=0)


def attend_sum_kernel(count, place_ref, mixed_cot_ref, attended_ref, *refs):
    normed, cots = parts_of(refs[:count]), parts_of(refs[count:-10])
    outs, qkv_grad, out_grad = refs[-10:-2], refs[-2], refs[-1]
    width, wide = qkv_grad.shape
    top, each = width // 8, out_grad.shape[0] // 8
    starts = row_starts(place_ref)
    mixed_cot = jnp.concatenate([mixed_cot_ref[pl.ds(start, ROWS), :] for start in starts], axis=0)
    qkv_grad[...] = t_dot(joint(normed), mixed_cot).astype(BF)
    attended = jnp.concatenate([attended_ref[pl.ds(start, ROWS), :] for start in starts], axis=0)
    out_grad[...] = t_dot(attended, joint(cots))
    for slot, out in enumerate(outs):
        at = place_ref[1 + slot]
        out[pl.ds(0, top), :] = jnp.zeros((top, width), BF)
        out[pl.ds(0, top), pl.ds(0, wide)] = qkv_grad[pl.ds(pl.multiple_of(at * top, 32), top), :]
        turned = pl.multiple_of((at % 2 * 4 + at // 2) * each, 8)
        out[pl.ds(top, each), :] = out_grad[pl.ds(turned, each), :].astype(BF)


def attend_sum(place, mixed_cot, attended, normed, cots):
    width, group = cots[0].shape[1], attended.shape[1]
    kernel = functools.partial(attend_sum_kernel, len(normed))
    outs = [((width // 8 + group // 8, width), BF)] * 8
    scratch = [((width, 3 * group), BF), ((group, width), F32)]
    return call(kernel, "attend_sum", outs, scratch, place, mixed_cot, attended, *normed, *cots)


def gelu_tanh(values):
    return 0.5 * values * (1.0 + jnp.tanh(0.7978845608028654 * (values + 0.044715 * values * values * values)))


def feed_kernel(place_ref, *refs):
    blocks, parts = refs[:8], parts_of(refs[8:-4])
    sent_ref, kept_ref, up, down = refs[-4:]
    place_blocks(place_ref, blocks, feed_places(up, down))
    for at, part in enumerate(parts):
        active = gelu_tanh(jnp.dot(part[...], up[...], preferred_element_type=F32)).astype(BF)
        put_part(sent_ref, kept_ref, at, jnp.dot(active, down[...], preferred_element_type=F32))


def feed_scratch(blocks):
    rows, width = blocks[0].shape
    return [((4 * rows, width), BF)] * 2


def feed(place, blocks, parts):
    return call(feed_kernel, "feed", two_parts(blocks[0].shape[1]), feed_scratch(blocks), place, *blocks, *parts)


def feed_back_kernel(place_ref, *refs):
    blocks, refs, (active_ref, cot_ref, sent_ref, kept_ref, up, down) = refs[:8], refs[8:-6], refs[-6:]
    normed, cots = parts_of(refs[: len(refs) // 2]), parts_of(refs[len(refs) // 2 :])
    place_blocks(place_ref, blocks, feed_places(up, down))
    for at, (part, cot) in enumerate(zip(normed, cots)):
        upper = jnp.dot(part[...], up[...], preferred_element_type=F32)
        square = upper * upper
        bent = jnp.tanh(0.7978845608028654 * (upper + 0.044715 * upper * square))
        inner = 0.7978845608028654 * (1.0 + 3.0 * 0.044715 * square)
        half_up = 0.5 * upper
        rows = pl.ds(at * ROWS, ROWS)
        active_ref[rows, :] = (half_up * (1.0 + bent)).astype(BF)
        slope = 0.5 * (1.0 + bent) + half_up * (1.0 - bent * bent) * inner
        upper_cot = (slope * dot_t(cot[...], down[...])).astype(BF)
        cot_ref[rows, :] = upper_cot
        put_part(sent_ref, kept_ref, at, dot_t(upper_cot, up[...]))


def feed_back(place, blocks, normed, cots):
    rows, width = blocks[0].shape
    outs = [((4 * ROWS, 4 * rows), BF)] * 2 + two_parts(width)
    return call(feed_back_kernel, "feed_back", outs, feed_scratch(blocks), place, *blocks, *normed, *cots)


def feed_sum_kernel(place_ref, active_ref, upper_cot_ref, *refs):
    outs, up_grad, down_grad = refs[-10:-2], refs[-2], refs[-1]
    refs = refs[:-10]
    normed, cots = parts_of(refs[: len(refs) // 2]), parts_of(refs[len(refs) // 2 :])
    each = up_grad.shape[0] // 8
    up_grad[...] = t_dot(joint(normed), upper_cot_ref[...]).astype(BF)
    down_grad[...] = t_dot(active_ref[...], joint(cots)).astype(BF)
    for slot, out in enumerate(outs):
        rows = pl.ds(pl.multiple_of(place_ref[1 + slot] * each, 32), each)
        out[pl.ds(0, each), :] = up_grad[rows, :]
        out[pl.ds(each, each), :] = down_grad[rows, :]


def feed_sum(place, active, upper_cot, normed, cots):
    width, inner = cots[0].shape[1], active.shape[1]
    outs = [((inner // 4, width), BF)] * 8
    scratch = [((width, inner), BF), ((inner, width), BF)]
    return call(feed_sum_kernel, "feed_sum", outs, scratch, place, active, upper_cot, *normed, *cots)


def store_kernel(fsdp, *refs):
    qkv_out, out_out, up_out, down_out = refs[6:]
    for layer in range(LAYERS):
        columns_ref, rows_ref, fed_ref = refs[3 * layer : 3 * layer + 3]
        out_out[layer] = rows_ref[...].astype(F32)
        down_out[layer] = fed_ref[pl.ds(fed_ref.shape[0] - down_out.shape[1], down_out.shape[1]), :]
        seq = columns_ref.shape[0]
        inner, group = up_out.shape[2] // seq, qkv_out.shape[2] // (3 * seq)
        for quarter in range(seq):
            values = columns_ref[quarter].astype(F32)
            each = inner // fsdp
            for part in range(fsdp):
                at = (part * seq + quarter) * each
                up_out[layer, :, pl.ds(at, each)] = values[:, part * each : part * each + each]
            for part in range(3):
                at = (part * seq + quarter) * group
                start = inner + part * group
                qkv_out[layer, :, pl.ds(at, group)] = values[:, start : start + group]


def store(sent_0, sent_1, group, seq, fsdp):
    piece, width = sent_0[1].shape
    inner = sent_0[0].shape[2] - 3 * group
    shapes = [(piece, 3 * group * seq), (piece, width), (piece, inner * seq), (inner * seq // (fsdp * seq), width)]
    outs = [((LAYERS,) + shape, F32) for shape in shapes]
    args = sent_0 + sent_1
    return pl.pallas_call(
        functools.partial(store_kernel, fsdp),
        out_shape=tuple(jax.ShapeDtypeStruct(shape, dtype) for shape, dtype in outs),
        compiler_params=pltpu.CompilerParams(vmem_limit_bytes=56 << 20),
        name="store",
    )(*args)


def norm_parts(values):
    center = values - jnp.mean(values, axis=-1, keepdims=True)
    inverse = lax.rsqrt(jnp.mean(center * center, axis=-1, keepdims=True) + NORM_EPS)
    return center * inverse, inverse


def norm_back(unit, inverse, gain, cot):
    scaled = cot * gain
    inner = scaled - jnp.mean(scaled, axis=-1, keepdims=True)
    inner = inner - unit * jnp.mean(scaled * unit, axis=-1, keepdims=True)
    return inner * inverse, jnp.sum(cot * unit, axis=0), jnp.sum(cot, axis=0)


NORM_AT = 640


def norm_kernel(place_ref, *refs):
    blocks, out_ref, both = refs[:8], refs[8], refs[9]
    each = both.shape[0] // 8
    for slot, block in enumerate(blocks):
        both[pl.ds(pl.multiple_of(place_ref[1 + slot] * each, 32), each), :] = block[...].astype(F32)
    out_ref[...] = both[...].T[:8]


def norms_of(place, blocks):
    width = blocks[0].shape[1]
    part = pl.BlockSpec((width // 8, 128), lambda step: (0, NORM_AT // 128))
    return pl.pallas_call(
        norm_kernel,
        grid=(1,),
        in_specs=[pl.BlockSpec(memory_space=pltpu.SMEM)] + [part] * 8,
        out_shape=jax.ShapeDtypeStruct((8, width), F32),
        scratch_shapes=[pltpu.VMEM((width, 128), F32)],
        name="norms_of",
    )(place, *blocks)


def shards(tokens, norm_gains, norm_shifts, w_qkv, w_out, w_up, w_down, out_grad, doc_lengths):
    tok_rows, width = tokens.shape
    fsdp, seq = lax.axis_size("fsdp"), lax.axis_size("seq")
    ruled = fsdp == 8
    length = tok_rows * seq
    group = (H // seq) * HD
    piece = w_qkv.shape[1]
    inner = w_up.shape[2] // seq
    unit_rows = w_down.shape[1]
    place = lax.axis_index("seq")

    ends = jnp.cumsum(doc_lengths[0])
    starts = ends - doc_lengths[0]
    positions = lax.iota(jnp.int32, length)
    first = jnp.max(jnp.where(positions[:, None] >= starts[None, :], starts[None, :], 0), axis=1, keepdims=True)

    def column_parts(layer):
        qkv = w_qkv[layer].astype(BF).reshape(piece, 3, seq, group).transpose(2, 0, 1, 3)
        up = w_up[layer].astype(BF).reshape(piece, fsdp, seq, unit_rows).transpose(2, 0, 1, 3)
        return qkv.reshape(seq, piece, 3 * group), up.reshape(seq, piece, inner)

    def pad_cols(values, cols):
        return jnp.pad(values, [(0, 0)] * (values.ndim - 1) + [(0, cols - values.shape[-1])])

    place_ref = jnp.concatenate([place.reshape(1).astype(jnp.int32), owners()])
    norms = jnp.stack([norm_gains, norm_shifts]).astype(BF).reshape(8, piece).T
    norms = jnp.pad(norms, ((0, 0), (NORM_AT - 3 * group, width - NORM_AT - 8)))
    qkv_parts = [None, None]
    up_parts = [None, None]
    for layer in range(LAYERS):
        qkv_parts[layer], up_parts[layer] = column_parts(layer)
    early = jnp.concatenate([qkv_parts[0], jnp.broadcast_to(norms[None], (seq,) + norms.shape)], axis=2)
    early = exchange_seq(early).reshape(seq * piece, width)
    attn_low = [None, None]
    feed_low = [None, None]

    def wide_blocks(values):
        return pad_cols(values.reshape(8, -1, values.shape[-1]), width)

    def out_blocks(rows):
        return rows.reshape(2, 4, -1, width).transpose(1, 0, 2, 3).reshape(8, -1, width)

    def out_rows_of(blocks):
        return blocks.reshape(4, 2, -1, width).transpose(1, 0, 2, 3).reshape(-1, width)

    if ruled:
        out_rows = turn(w_out.astype(BF))
        early = jnp.concatenate([early, out_rows[0]])
        mark = [early]
        first_gather = Gather(early)
        first_moved = first_gather.advance()
    else:
        mark = []
        first_steps = []
    all_tokens = gather_seq(after(tokens, *mark))
    later = jnp.concatenate([up_parts[0], pad_cols(qkv_parts[1], inner), up_parts[1]], axis=1)
    later = exchange_seq(after(later, *mark))
    up_first = later[:, :piece].reshape(seq * piece, inner)
    qkv_next = later[:, piece : 2 * piece].reshape(seq * piece, inner)
    up_next = later[:, 2 * piece :].reshape(seq * piece, inner)
    if ruled:
        first_moved = first_gather.advance(*first_moved)
        low_down = w_down.astype(BF)
        feed_gather = [
            Gather(jnp.concatenate([up_first, low_down[0]])),
            Gather(jnp.concatenate([up_next, low_down[1]])),
        ]
        attn_gather = Gather(jnp.concatenate([qkv_next, out_rows[1]]))
        first_gather.advance(feed_gather[0].blocks[0], *first_moved)
        moved = feed_gather[0].advance(*first_moved)
        first_gather.advance(first_gather.sides[2])
        first_steps = feed_gather[0].advance(first_gather.blocks[3], *moved)
        attn_low[0] = first_gather.result()
    else:
        early = lax.all_gather(early, "fsdp", axis=0, tiled=True)

        def gathered(columns):
            return lax.all_gather(columns, "fsdp", axis=0, tiled=True)

        def attn_joined(columns, rows):
            rows = lax.all_gather(rows.astype(BF), BOTH, axis=0, tiled=True)
            rows = lax.dynamic_slice_in_dim(rows, place * group, group, 0)
            return jnp.concatenate([columns.reshape(8, -1, width), out_blocks(rows)], axis=1)

        attn_low = [list(attn_joined(early, w_out[0])), list(attn_joined(gathered(qkv_next), w_out[1]))]
        for layer, columns in enumerate((up_first, up_next)):
            blocks = gathered(columns), gathered(w_down[layer].astype(BF))
            feed_low[layer] = list(jnp.concatenate([wide_blocks(part) for part in blocks], axis=1))

    norm_low = norms_of(place_ref, attn_low[0]).reshape(2, LAYERS, 2, width)
    gains, shifts = norm_low[0], norm_low[1]

    plan = {}
    if ruled:
        plan = {
            ("scatter_a", 0): [feed_gather[0], attn_gather],
            ("gather_b", 0): [feed_gather[0], attn_gather],
            ("scatter_b", 0): [attn_gather, feed_gather[1]],
            ("gather_a", 1): [attn_gather, feed_gather[1]],
            ("scatter_a", 1): [feed_gather[1]],
            ("gather_b", 1): [feed_gather[1]],
        }

    def steps(what, layer):
        def work(gate):
            return sum([each.advance(gate) for each in plan.get((what, layer), [])], [])

        return work

    def beside_main(value, what, layer):
        moved = steps(what, layer)(value)
        return after(value, *moved)

    first_cot = gather_seq(after((BRANCH_SCALE * out_grad.astype(F32)).astype(BF), all_tokens[1]))
    first_steps = first_steps + first_cot[1:]

    hidden = tokens.astype(F32)
    saved = []
    for layer in range(LAYERS):
        unit_a, inverse_a = norm_parts(hidden)
        if layer == 0:
            normed_a = (norm_parts(jnp.concatenate(all_tokens).astype(F32))[0] * gains[0, 0] + shifts[0, 0]).astype(BF)
            normed_a = [after(normed_a, *first_steps)]
        else:
            normed_a = (unit_a * gains[layer, 0] + shifts[layer, 0]).astype(BF)
            normed_a = gather_seq(normed_a, steps("gather_a", layer))
        normed_a[-1] = beside_main(normed_a[-1], "normed_a", layer)
        if ruled and layer > 0:
            attn_low[layer] = attn_gather.result()
        mixed, attended, totals, sent, kept = attend(place_ref, first, attn_low[layer], normed_a, group)
        sent = beside_main(sent, "attended", layer)
        hidden = hidden + BRANCH_SCALE * scatter_seq(sent, kept, steps("scatter_a", layer))
        unit_b, inverse_b = norm_parts(hidden)
        normed_b = (unit_b * gains[layer, 1] + shifts[layer, 1]).astype(BF)
        normed_b = gather_seq(normed_b, steps("gather_b", layer))
        normed_b[-1] = beside_main(normed_b[-1], "normed_b", layer)
        if ruled:
            feed_low[layer] = feed_gather[layer].result()
        if layer < LAYERS - 1:
            sent, kept = feed(place_ref, feed_low[layer], normed_b)
            hidden = hidden + BRANCH_SCALE * scatter_seq(sent, kept, steps("scatter_b", layer))
        saved.append((unit_a, inverse_a, normed_a, mixed, attended, totals, unit_b, inverse_b, normed_b))
    last_feed = []

    cot = out_grad.astype(F32)
    norm_sums = []
    sums_of = {}
    grads_of = {}

    def start_sum(name, blocks):
        if ruled:
            sums_of[name] = Reduce(blocks)
        else:
            grads_of[name] = jnp.stack(blocks)
        return [blocks[0]]

    def step_sums(gate, *names):
        return sum([sums_of[name].advance(gate) for name in names], []) if ruled else []

    back_plan = {
        ("gather_a", 1): [("feed", 1)],
        ("scatter_a", 1): [("feed", 1)],
        ("gather_b", 0): [("feed", 1), ("attn", 1)],
        ("scatter_b", 0): [("feed", 1), ("attn", 1)],
        ("gather_a", 0): [("feed", 0), ("attn", 1)],
        ("scatter_a", 0): [("feed", 0), ("attn", 1)],
        ("after_sum", 0): [("attn", 0)],
    }
    for layer in reversed(range(LAYERS)):
        unit_a, inverse_a, normed_a, mixed, attended, totals, unit_b, inverse_b, normed_b = saved[layer]

        def sum_steps(what):
            return lambda gate: step_sums(gate, *back_plan.get((what, layer), []))

        if layer == LAYERS - 1:
            down_cot = first_cot
        else:
            down_cot = gather_seq((BRANCH_SCALE * cot).astype(BF), sum_steps("gather_b"))
        active, upper_cot, sent, kept = feed_back(place_ref, feed_low[layer], normed_b, down_cot)

        def feed_work(gate):
            moved = start_sum(("feed", layer), feed_sum(place_ref, after(active, gate), upper_cot, normed_b, down_cot))
            return moved + sum_steps("scatter_b")(gate)

        second_cot = scatter_seq(sent, kept, feed_work)
        back, gain_sum_b, shift_sum_b = norm_back(unit_b, inverse_b, gains[layer, 1], second_cot)
        cot = cot + back

        def norm_work(gate):
            if layer == LAYERS - 1:
                parts = [after(normed_b[0], gate)] + normed_b[1:]
                last_feed.extend(feed(place_ref, feed_low[layer], parts))
            return sum_steps("gather_a")(gate) + last_feed[:1]

        attn_cot = gather_seq((BRANCH_SCALE * cot).astype(BF), norm_work)
        mixed_cot, sent, kept = attend_back(place_ref, first, attn_low[layer], mixed, totals, attn_cot)
        sent = after(sent, *sum_steps("back")(mixed_cot))

        def attn_work(gate):
            joined = attend_sum(place_ref, after(mixed_cot, gate), attended, normed_a, attn_cot)
            moved = sum_steps("scatter_a")(gate) + start_sum(("attn", layer), joined)
            return moved + sum_steps("after_sum")(gate)

        normed_cot = scatter_seq(sent, kept, attn_work)
        back, gain_sum_a, shift_sum_a = norm_back(unit_a, inverse_a, gains[layer, 0], normed_cot)
        cot = cot + back
        norm_sums.append(jnp.stack([gain_sum_a, gain_sum_b, shift_sum_a, shift_sum_b]))

    sent, kept = last_feed
    outputs = (hidden + BRANCH_SCALE * scatter_seq(after(sent, cot), kept)).astype(BF)
    sums = jnp.concatenate(norm_sums[::-1])
    column_back = {}
    row_back = {}

    def send_home(layer, *gates):
        attn, fed = sums_of["attn", layer].total, sums_of["feed", layer].total
        columns = jnp.concatenate([fed[: seq * piece], attn[: seq * piece, : 3 * group]], axis=1).astype(BF)
        rows = after(attn[seq * piece :].astype(BF), *gates)
        columns = exchange_seq(after(columns, *gates).reshape(seq, piece, -1))
        return columns, turn(rows), fed

    def take(layer):
        def summed(blocks):
            return lax.psum_scatter(blocks, "fsdp", scatter_dimension=0, tiled=True).astype(F32)

        joined = grads_of["attn", layer]
        column_back["qkv", layer] = summed(joined[:, : width // 8, : 3 * group].reshape(width, 3 * group))
        rows = out_rows_of(joined[:, width // 8 :])
        spread = jnp.zeros((seq,) + rows.shape, BF)
        spread = lax.dynamic_update_index_in_dim(spread, rows, place, 0).reshape(-1, width)
        row_back["out", layer] = lax.psum_scatter(spread, BOTH, scatter_dimension=0, tiled=True).astype(F32)
        joined = grads_of["feed", layer]
        column_back["up", layer] = summed(joined[:, : width // 8].reshape(width, inner))
        row_back["down", layer] = summed(joined[:, width // 8 :].reshape(inner, width))

    def home(layer):
        both = jnp.concatenate([column_back["up", layer], column_back["qkv", layer]], axis=1).astype(BF)
        both = exchange_seq(both.reshape(seq, piece, -1)).astype(F32)
        qkv = both[:, :, inner:].reshape(seq, piece, 3, group).transpose(1, 2, 0, 3).reshape(piece, -1)
        up = both[:, :, :inner].reshape(seq, piece, fsdp, unit_rows).transpose(1, 2, 0, 3)
        return up.reshape(piece, -1), qkv

    if ruled:
        mark = sums_of["attn", 0].advance() + sums_of["feed", 0].advance() + [outputs]
        for bit in (1, 2):
            sums = sums + swap_seq(sums, bit)
        sums = after(sums, *mark)
        mark = step_sums(sums, ("attn", 0), ("feed", 0))
        sent_1 = send_home(1, sums)
        for bit in (1, 2):
            sums = sums + lax.ppermute(sums, "fsdp", [(f, f ^ bit) for f in range(8)])
        sums = after(sums, *mark)
        step_sums(sums, ("attn", 0))
        sums = sums + lax.ppermute(sums, "fsdp", [(f, f ^ 4) for f in range(8)])
        weight_grads = store(send_home(0), sent_1, group, seq, fsdp)
    else:
        take(0)
        take(1)
        home_0, home_1 = home(0), home(1)
        sums = lax.psum(sums, BOTH)
        up_grads, qkv_grads = zip(home_0, home_1)
        out_grads = [row_back["out", layer] for layer in range(LAYERS)]
        down_grads = [row_back["down", layer] for layer in range(LAYERS)]
        weight_grads = [jnp.stack(grads) for grads in (qkv_grads, out_grads, up_grads, down_grads)]
    whose = lax.axis_index("fsdp") * seq + place
    sums = lax.dynamic_slice_in_dim(sums, whose * piece, piece, 1).reshape(LAYERS, 4, piece)
    return (
        outputs,
        cot.astype(BF),
        sums[:, :2],
        sums[:, 2],
        sums[:, 3],
        *weight_grads,
    )


def solution(mesh):
    rows = P(BOTH, None)
    thirds = P(None, None, BOTH)
    middle = P(None, BOTH, None)
    return jax.shard_map(
        shards,
        mesh=mesh,
        in_specs=(rows, thirds, thirds, middle, middle, middle, middle, rows, P("fsdp", None)),
        out_specs=(rows, rows, thirds, P(None, BOTH), P(None, BOTH), middle, middle, middle, middle),
        check_vma=False,
    )
```

time: 464 us -> 434 us (0.935)
  Pallas kernels: 29.8 us -> 110 us
  local copies, waits for them, and re-layouts: 69.6 us -> 19.3 us
  matrix products: 42.2 us -> 0 us
  other arithmetic: 67.7 us -> 34.4 us
  waiting for transfers between devices: 136 us -> 161 us
  starting transfers between devices: 107 us -> 102 us
    pallas_call x4 -> x14, Pallas kernels: 29.8 us -> 110 us  [the longest x12 105 us: call(): pl.pallas_call(kernel, in_specs=in_specs, out_shape=tuple((jax.ShapeDtype...]
    dot_general x24 -> x0, matrix products: 42.2 us -> none  [the longest x8 16.2 us: dot_t(): lax.dot_general(left, right, (((1,), (1,)), ((), ())), preferred_element_...]
    ppermute x32, waiting for transfers between devices: 28.8 us -> 55.6 us  [over_side(): return lax.ppermute(block, 'fsdp', [(f, f ^ 1) for f in range(8)])]
    another operation x41 -> x7, other arithmetic: 16.6 us -> 2.18 us  [the longest x15 5.38 us: gather_seq(): jnp.stack(by_bit(place % 2, pair, near), axis=1).reshape(-1, rows.shape[-1])]
    unnamed x313 -> x218, local copies, waits for them, and re-layouts: 22.6 us -> 8.48 us
    convert_element_type x28 -> x9, local copies, waits for them, and re-layouts: 12.7 us -> 0.42 us  [the longest x8 0.33 us: scatter_seq(): sent = half[1].astype(BF)]
    ppermute x24, waiting for transfers between devices: 36.3 us -> 47.3 us  [over_line(): return lax.ppermute(block, 'fsdp', moves)]
    ppermute x42 -> x50, waiting for transfers between devices: 64 us -> 54.6 us  [swap_seq(): return lax.ppermute(values, 'seq', [(s, s ^ bit) for s in range(4)])]
  transfers between devices with their start and end apart: 104 -> 112, of which waited for: 48 -> 49; matrix products, arithmetic and copies ran while one was open for 26% -> 7% of each run, Pallas kernels for 4% -> 7%
where the time goes in v3:
time: 434 us; the launch traced here: 429 us
  waiting for transfers between devices  161 us (37%)
  Pallas kernels  110 us (25%)
  starting transfers between devices  102 us (24%)
  other arithmetic  34.4 us (8%)
  local copies, waits for them, and re-layouts  19.3 us (4%)
    pallas_call x12, Pallas kernels, call(): pl.pallas_call(kernel, in_specs=in_specs, out_shape=tuple((jax.ShapeDtype...  105 us
    ppermute x32, waiting for transfers between devices, over_side(): return lax.ppermute(block, 'fsdp', [(f, f ^ 1) for f in range(8)])  55.6 us
    ppermute x50, waiting for transfers between devices, swap_seq(): return lax.ppermute(values, 'seq', [(s, s ^ bit) for s in range(4)])  54.6 us
    ppermute x24, waiting for transfers between devices, over_line(): return lax.ppermute(block, 'fsdp', moves)  47.3 us
    ppermute x50, starting transfers between devices, swap_seq(): return lax.ppermute(values, 'seq', [(s, s ^ bit) for s in range(4)])  37.5 us
    ppermute x32, starting transfers between devices, over_side(): return lax.ppermute(block, 'fsdp', [(f, f ^ 1) for f in range(8)])  34.5 us
    ppermute x24, starting transfers between devices, over_line(): return lax.ppermute(block, 'fsdp', moves)  25.1 us
    add x8, other arithmetic, scatter_seq(): half = kept + swap_seq(sent, 1).astype(F32)  10.8 us
  transfers between devices with their start and end apart: 112, of which 49 were waited for; matrix products, arithmetic and copies ran while one was open for 7% of the time, Pallas kernels for 7%

profile of v3, /device:TPU:0, one launch (start us, length us, event | category | flops | bytes accessed | tf_op | source)
XLA Modules:
  0.0 428.7 jit_solution(2791660239524083901)
XLA Ops:
  4.8 4.5 %collective-permute-start = (bf16[2,24,768]{2,1,0:T(8,128)(2,1)S(1)}, bf16[2,24,768]{2,1,0:T(8,128)(2,1)S(1)}, u32[]{:S(2)}, u32[]{:S(2)}) collective-permute-start(bf16[2,24,768]{2,1,0:T(8,128)(2,1)S(1)} %fusion.64), channel_id=1, source_target_pairs={{0,1},{1,0},{2,3},{3,2},{4,5},{5,4},{6,7},{7,6},{8,9},{9,8},{10,11... | collective-permute-start | bytes 221192 | tf_op jit(solution)/shard_map/ppermute | solution.py:35
  64.4 11.2 %attend.2 = (bf16[1024,576]{1,0:T(8,128)(2,1)}, bf16[1024,192]{1,0:T(8,128)(2,1)}, f32[1024,3]{1,0:T(8,128)}, bf16[2,256,768]{2,1,0:T(8,128)(2,1)}, f32[2,256,768]{2,1,0:T(8,128)}) custom-call(s32[9]{0:T(128)} %concatenate.43.place_ref, s32[1024,1]{1,0:T(8,128)} %copy.89.first_ref, bf16[120,768]{1,0:T(8,128)(2,1)} %copy-done.7, bf16[120,768]{1,0:T(8,128)(2,1)} %copy-done.36, ...), custom_call_target="tpu_custom_call" | custom-call | flops 10000000000 | bytes 30000000 | tf_op jit(solution)/shard_map/attend/pallas_call | solution.py:237
  85.9 9.4 %collective-permute-done.27.refs_1_ = bf16[120,768]{1,0:T(8,128)(2,1)S(1)} collective-permute-done((bf16[120,768]{1,0:T(8,128)(2,1)S(1)}, bf16[120,768]{1,0:T(8,128)(2,1)S(1)}, u32[]{:S(2)}, u32[]{:S(2)}) %collective-permute-start.27) | collective-permute-done | bytes 184352 | tf_op jit(solution)/shard_map/ppermute | solution.py:77
  104.6 4.3 %collective-permute-done.30.refs_5_ = bf16[120,768]{1,0:T(8,128)(2,1)S(1)} collective-permute-done((bf16[120,768]{1,0:T(8,128)(2,1)S(1)}, bf16[120,768]{1,0:T(8,128)(2,1)S(1)}, u32[]{:S(2)}, u32[]{:S(2)}) %collective-permute-start.30) | collective-permute-done | bytes 184352 | tf_op jit(solution)/shard_map/ppermute | solution.py:81
  111.5 5.9 %feed.2 = (bf16[2,256,768]{2,1,0:T(8,128)(2,1)}, f32[2,256,768]{2,1,0:T(8,128)}) custom-call(s32[9]{0:T(128)} %concatenate.43.place_ref, bf16[192,768]{1,0:T(8,128)(2,1)} %copy-done.19, bf16[192,768]{1,0:T(8,128)(2,1)} %collective-permute-done.15.refs_1_, bf16[192,768]{1,0:T(8,128)(2,1)} %collective-permute-done.18.refs_2_, bf16[192,768]{1,0:T(8,128)(2,1)} %copy-done.78, ...), custom_call_target="tpu_custom_call" | custom-call | flops 5000000000 | bytes 15000000 | tf_op jit(solution)/shard_map/feed/pallas_call | solution.py:237
  127.9 9.1 %collective-permute-done.37.refs_3_ = bf16[120,768]{1,0:T(8,128)(2,1)S(1)} collective-permute-done((bf16[120,768]{1,0:T(8,128)(2,1)S(1)}, bf16[120,768]{1,0:T(8,128)(2,1)S(1)}, u32[]{:S(2)}, u32[]{:S(2)}) %collective-permute-start.37) | collective-permute-done | bytes 184352 | tf_op jit(solution)/shard_map/ppermute | solution.py:77
  142.2 9.0 %collective-permute-done.40.refs_7_ = bf16[120,768]{1,0:T(8,128)(2,1)S(1)} collective-permute-done((bf16[120,768]{1,0:T(8,128)(2,1)S(1)}, bf16[120,768]{1,0:T(8,128)(2,1)S(1)}, u32[]{:S(2)}, u32[]{:S(2)}) %collective-permute-start.40) | collective-permute-done | bytes 184352 | tf_op jit(solution)/shard_map/ppermute | solution.py:81
  154.5 11.1 %attend.3 = (bf16[1024,576]{1,0:T(8,128)(2,1)}, bf16[1024,192]{1,0:T(8,128)(2,1)}, f32[1024,3]{1,0:T(8,128)}, bf16[2,256,768]{2,1,0:T(8,128)(2,1)}, f32[2,256,768]{2,1,0:T(8,128)}) custom-call(s32[9]{0:T(128)} %concatenate.43.place_ref, s32[1024,1]{1,0:T(8,128)} %copy.89.first_ref, bf16[120,768]{1,0:T(8,128)(2,1)} %copy-done.41, ...), custom_call_target="tpu_custom_call" | custom-call | flops 10000000000 | bytes 30000000 | tf_op jit(solution)/shard_map/attend/pallas_call | solution.py:237
  173.9 7.7 %collective-permute-done.49.refs_3_ = bf16[192,768]{1,0:T(8,128)(2,1)S(1)} collective-permute-done((bf16[192,768]{1,0:T(8,128)(2,1)S(1)}, bf16[192,768]{1,0:T(8,128)(2,1)S(1)}, u32[]{:S(2)}, u32[]{:S(2)}) %collective-permute-start.49) | collective-permute-done | bytes 294944 | tf_op jit(solution)/shard_map/ppermute | solution.py:77
  183.9 7.4 %collective-permute-done.50.refs_7_ = bf16[192,768]{1,0:T(8,128)(2,1)S(1)} collective-permute-done((bf16[192,768]{1,0:T(8,128)(2,1)S(1)}, bf16[192,768]{1,0:T(8,128)(2,1)S(1)}, u32[]{:S(2)}, u32[]{:S(2)}) %collective-permute-start.50) | collective-permute-done | bytes 294944 | tf_op jit(solution)/shard_map/ppermute | solution.py:81
  195.1 8.7 %feed_back.2 = (bf16[1024,768]{1,0:T(8,128)(2,1)}, bf16[1024,768]{1,0:T(8,128)(2,1)}, bf16[2,256,768]{2,1,0:T(8,128)(2,1)}, f32[2,256,768]{2,1,0:T(8,128)}) custom-call(s32[9]{0:T(128)} %concatenate.43.place_ref, bf16[192,768]{1,0:T(8,128)(2,1)} %copy-done.20, bf16[192,768]{1,0:T(8,128)(2,1)} %copy-done.83, bf16[192,768]{1,0:T(8,128)(2,1)} %copy-done.87, ...), custom_call_target="tpu_custom_call" | custom-call | flops 8000000000 | bytes 24000000 | tf_op jit(solution)/shard_map/feed_back/pallas_call | solution.py:237
  209.1 6.9 %feed_sum.2 = (bf16[192,768]{1,0:T(8,128)(2,1)}, bf16[192,768]{1,0:T(8,128)(2,1)}, bf16[192,768]{1,0:T(8,128)(2,1)}, bf16[192,768]{1,0:T(8,128)(2,1)}, bf16[192,...) custom-call(s32[9]{0:T(128)} %concatenate.43.place_ref, ...), custom_call_target="tpu_custom_call" | custom-call | flops 6000000000 | bytes 18000000 | tf_op jit(solution)/shard_map/feed_sum/pallas_call | solution.py:237
  221.8 5.9 %feed.3 = (bf16[2,256,768]{2,1,0:T(8,128)(2,1)}, f32[2,256,768]{2,1,0:T(8,128)}) custom-call(s32[9]{0:T(128)} %concatenate.43.place_ref, bf16[192,768]{1,0:T(8,128)(2,1)} %copy-done.20, bf16[192,768]{1,0:T(8,128)(2,1)} %copy-done.83, bf16[192,768]{1,0:T(8,128)(2,1)} %copy-done.87, bf16[192,768]{1,0:T(8,128)(2,1)} %copy-done.90, bf16[192,768]{1,0:T(8,128)(2,1)} %copy-done.84, ...), custom_call_target="tpu_custom_call" | custom-call | flops 5000000000 | bytes 15000000 | tf_op jit(solution)/shard_map/feed/pallas_call | solution.py:237
  234.2 14.8 %attend_back.2 = (bf16[1024,576]{1,0:T(8,128)(2,1)}, bf16[2,256,768]{2,1,0:T(8,128)(2,1)}, f32[2,256,768]{2,1,0:T(8,128)}) custom-call(s32[9]{0:T(128)} %concatenate.43.place_ref, s32[1024,1]{1,0:T(8,128)} %copy.89.first_ref, bf16[1024,576]{1,0:T(8,128)(2,1)} %get-tuple-element.180.mixed_ref, f32[1024,3]{1,0:T(8,128)} %get-tuple-element.181.total_ref, ...), custom_call_target="tpu_custom_call" | custom-call | flops 14000000000 | bytes 42000000 | tf_op jit(solution)/shard_map/attend_back/pallas_call | solution.py:237
  256.5 5.3 %attend_sum.2 = (bf16[120,768]{1,0:T(8,128)(2,1)}, bf16[120,768]{1,0:T(8,128)(2,1)}, bf16[120,768]{1,0:T(8,128)(2,1)}, bf16[120,768]{1,0:T(8,128)(2,1)}, bf16[12...) custom-call(s32[9]{0:T(128)} %concatenate.43.place_ref, ...), custom_call_target="tpu_custom_call" | custom-call | flops 5000000000 | bytes 15000000 | tf_op jit(solution)/shard_map/attend_sum/pallas_call | solution.py:237
  270.5 8.4 %collective-permute-done.67 = bf16[120,768]{1,0:T(8,128)(2,1)S(1)} collective-permute-done((bf16[120,768]{1,0:T(8,128)(2,1)S(1)}, bf16[120,768]{1,0:T(8,128)(2,1)S(1)}, u32[]{:S(2)}, u32[]{:S(2)}) %collective-permute-start.67) | collective-permute-done | bytes 184352 | tf_op jit(solution)/shard_map/ppermute | solution.py:81
  281.5 8.7 %feed_back.3 = (bf16[1024,768]{1,0:T(8,128)(2,1)}, bf16[1024,768]{1,0:T(8,128)(2,1)}, bf16[2,256,768]{2,1,0:T(8,128)(2,1)}, f32[2,256,768]{2,1,0:T(8,128)}) custom-call(s32[9]{0:T(128)} %concatenate.43.place_ref, bf16[192,768]{1,0:T(8,128)(2,1)} %copy-done.19, bf16[192,768]{1,0:T(8,128)(2,1)} %collective-permute-done.15.refs_1_, ...), custom_call_target="tpu_custom_call" | custom-call | flops 8000000000 | bytes 24000000 | tf_op jit(solution)/shard_map/feed_back/pallas_call | solution.py:237
  298.5 6.9 %feed_sum.3 = (bf16[192,768]{1,0:T(8,128)(2,1)}, bf16[192,768]{1,0:T(8,128)(2,1)}, bf16[192,768]{1,0:T(8,128)(2,1)}, bf16[192,768]{1,0:T(8,128)(2,1)}, bf16[192,...) custom-call(s32[9]{0:T(128)} %concatenate.43.place_ref, ...), custom_call_target="tpu_custom_call" | custom-call | flops 6000000000 | bytes 18000000 | tf_op jit(solution)/shard_map/feed_sum/pallas_call | solution.py:237
  313.6 8.5 %collective-permute-done.78 = bf16[120,768]{1,0:T(8,128)(2,1)S(1)} collective-permute-done((bf16[120,768]{1,0:T(8,128)(2,1)S(1)}, bf16[120,768]{1,0:T(8,128)(2,1)S(1)}, u32[]{:S(2)}, u32[]{:S(2)}) %collective-permute-start.78) | collective-permute-done | bytes 184352 | tf_op jit(solution)/shard_map/ppermute | solution.py:81
  324.7 14.6 %attend_back.3 = (bf16[1024,576]{1,0:T(8,128)(2,1)}, bf16[2,256,768]{2,1,0:T(8,128)(2,1)}, f32[2,256,768]{2,1,0:T(8,128)}) custom-call(s32[9]{0:T(128)} %concatenate.43.place_ref, s32[1024,1]{1,0:T(8,128)} %copy.89.first_ref, bf16[1024,576]{1,0:T(8,128)(2,1)} %get-tuple-element.218.mixed_ref, f32[1024,3]{1,0:T(8,128)} %get-tuple-element.219.total_ref, ...), custom_call_target="tpu_custom_call" | custom-call | flops 14000000000 | bytes 42000000 | tf_op jit(solution)/shard_map/attend_back/pallas_call | solution.py:237
  346.9 5.3 %attend_sum.3 = (bf16[120,768]{1,0:T(8,128)(2,1)}, bf16[120,768]{1,0:T(8,128)(2,1)}, bf16[120,768]{1,0:T(8,128)(2,1)}, bf16[120,768]{1,0:T(8,128)(2,1)}, bf16[12...) custom-call(s32[9]{0:T(128)} %concatenate.43.place_ref, ...), custom_call_target="tpu_custom_call" | custom-call | flops 5000000000 | bytes 15000000 | tf_op jit(solution)/shard_map/attend_sum/pallas_call | solution.py:237
  376.8 7.5 %collective-permute-done.92 = f32[8,768]{1,0:T(8,128)S(1)} collective-permute-done((f32[8,768]{1,0:T(8,128)S(1)}, f32[8,768]{1,0:T(8,128)S(1)}, u32[]{:S(2)}, u32[]{:S(2)}) %collective-permute-start.92) | collective-permute-done | bytes 24608 | tf_op jit(solution)/shard_map/ppermute | solution.py:35
  397.5 5.2 %collective-permute-start.110 = (bf16[2,24,1344]{2,1,0:T(8,128)(2,1)S(1)}, bf16[2,24,1344]{2,1,0:T(8,128)(2,1)S(1)}, u32[]{:S(2)}, u32[]{:S(2)}) collective-permute-start(bf16[2,24,1344]{2,1,0:T(8,128)(2,1)S(1)} %fusion.52), channel_id=1, source_target_pairs={{0,2},{1,3},{2,0},{3,1},{4,6},{5,7},{6,4},{7,5},{8,10},{9,11},{10,... | collective-permute-start | bytes 387080 | tf_op jit(solution)/shard_map/ppermute | solution.py:35
  410.3 4.9 %collective-permute-done.104 = bf16[120,768]{1,0:T(8,128)(2,1)S(1)} collective-permute-done((bf16[120,768]{1,0:T(8,128)(2,1)S(1)}, bf16[120,768]{1,0:T(8,128)(2,1)S(1)}, u32[]{:S(2)}, u32[]{:S(2)}) %collective-permute-start.104) | collective-permute-done | bytes 184352 | tf_op jit(solution)/shard_map/ppermute | solution.py:77
  (589 shorter events, 234.9 us)
Async XLA Ops:
  1.6 12.8 %collective-permute-start.2 = (bf16[2,24,768]{2,1,0:T(8,128)(2,1)S(1)}, bf16[2,24,768]{2,1,0:T(8,128)(2,1)S(1)}, u32[]{:S(2)}, u32[]{:S(2)}) collective-permute-start(bf16[2,24,768]{2,1,0:T(8,128)(2,1)S(1)} %convert_element_type.331), channel_id=1, source_target_pairs={{0,0},{1,8},{2,16},{3,24},{4,4},{5,12},{6,20},{7,28},{8,1},{9,9},{... | collective-permute-start | bytes 221192 | tf_op jit(solution)/shard_map/ppermute | solution.py:135
  20.6 14.1 %collective-permute-start.7 = (bf16[2,72,768]{2,1,0:T(8,128)(2,1)S(1)}, bf16[2,72,768]{2,1,0:T(8,128)(2,1)S(1)}, u32[]{:S(2)}, u32[]{:S(2)}) collective-permute-start(bf16[2,72,768]{2,1,0:T(8,128)(2,1)S(1)} %fusion.47), channel_id=1, source_target_pairs={{0,2},{1,3},{2,0},{3,1},{4,6},{5,7},{6,4},{7,5},{8,10},{9,11},{10,... | collective-permute-start | bytes 663560 | tf_op jit(solution)/shard_map/ppermute | solution.py:35
  20.8 30.8 %collective-permute-start.13 = (bf16[256,768]{1,0:T(8,128)(2,1)S(1)}, bf16[256,768]{1,0:T(8,128)(2,1)S(1)}, u32[]{:S(2)}, u32[]{:S(2)}) collective-permute-start(bf16[256,768]{1,0:T(8,128)(2,1)S(1)} %copy-done), channel_id=1, source_target_pairs={{0,1},{1,0},{2,3},{3,2},{4,5},{5,4},{6,7},{7,6},{8,9},{9,8},{10,11... | collective-permute-start | bytes 1179656 | tf_op jit(solution)/shard_map/ppermute | solution.py:35
  30.6 21.7 %collective-permute-start.14 = (bf16[256,768]{1,0:T(8,128)(2,1)S(1)}, bf16[256,768]{1,0:T(8,128)(2,1)S(1)}, u32[]{:S(2)}, u32[]{:S(2)}) collective-permute-start(bf16[256,768]{1,0:T(8,128)(2,1)S(1)} %collective-permute-done.12), channel_id=1, source_target_pairs={{0,1},{1,0},{2,3},{3,2},{4,5},{5,4},{6,7},{7,6},{8,9},{9,8},{10,11... | collective-permute-start | bytes 1179656 | tf_op jit(solution)/shard_map/ppermute | solution.py:35
  48.4 16.0 %collective-permute-start.20 = (bf16[256,768]{1,0:T(8,128)(2,1)S(1)}, bf16[256,768]{1,0:T(8,128)(2,1)}, u32[]{:S(2)}, u32[]{:S(2)}) collective-permute-start(bf16[256,768]{1,0:T(8,128)(2,1)S(1)} %fusion.19.refs_12_.refs_4_), channel_id=1, source_target_pairs={{0,1},{1,0},{2,3},{3,2},{4,5},{5,4},{6,7},{7,6},{8,9},{9,8},{10,11... | collective-permute-start | bytes 1179656 | tf_op jit(solution)/shard_map/ppermute | solution.py:35
  51.7 12.7 %collective-permute-start.18 = (bf16[192,768]{1,0:T(8,128)(2,1)}, bf16[192,768]{1,0:T(8,128)(2,1)}, u32[]{:S(2)}, u32[]{:S(2)}) collective-permute-start(bf16[192,768]{1,0:T(8,128)(2,1)} %collective-permute-done.15.refs_1_), channel_id=1, source_target_pairs={{0,8},{4,12},{8,24},{12,28},{16,0},{20,4},{24,16},{28,20},{1,9},{5... | collective-permute-start | bytes 884744 | tf_op jit(solution)/shard_map/ppermute | solution.py:77
  79.7 15.7 %collective-permute-start.23 = (bf16[256,768]{1,0:T(8,128)(2,1)S(1)}, bf16[256,768]{1,0:T(8,128)(2,1)S(1)}, u32[]{:S(2)}, u32[]{:S(2)}) collective-permute-start(bf16[256,768]{1,0:T(8,128)(2,1)S(1)} %fusion.38), channel_id=1, source_target_pairs={{0,2},{1,3},{2,0},{3,1},{4,6},{5,7},{6,4},{7,5},{8,10},{9,11},{10,... | collective-permute-start | bytes 1179656 | tf_op jit(solution)/shard_map/ppermute | solution.py:35
  81.5 13.9 %collective-permute-start.25 = (bf16[192,768]{1,0:T(8,128)(2,1)}, bf16[192,768]{1,0:T(8,128)(2,1)S(1)}, u32[]{:S(2)}, u32[]{:S(2)}) collective-permute-start(bf16[192,768]{1,0:T(8,128)(2,1)} %collective-permute-done.18.refs_2_), channel_id=1, source_target_pairs={{0,8},{4,12},{8,24},{12,28},{16,0},{20,4},{24,16},{28,20},{1,9},{5... | collective-permute-start | bytes 884744 | tf_op jit(solution)/shard_map/ppermute | solution.py:77
  81.6 13.8 %collective-permute-start.24 = (bf16[192,768]{1,0:T(8,128)(2,1)}, bf16[192,768]{1,0:T(8,128)(2,1)S(1)}, u32[]{:S(2)}, u32[]{:S(2)}) collective-permute-start(bf16[192,768]{1,0:T(8,128)(2,1)} %collective-permute-done.18.refs_2_), channel_id=1, source_target_pairs={{0,4},{4,0},{8,12},{12,8},{16,20},{20,16},{24,28},{28,24},{1,5},{5... | collective-permute-start | bytes 884744 | tf_op jit(solution)/shard_map/ppermute | solution.py:81
  82.3 13.1 %collective-permute-start.27 = (bf16[120,768]{1,0:T(8,128)(2,1)S(1)}, bf16[120,768]{1,0:T(8,128)(2,1)S(1)}, u32[]{:S(2)}, u32[]{:S(2)}) collective-permute-start(bf16[120,768]{1,0:T(8,128)(2,1)S(1)} %pad_maximum_fusion.9.refs_0_), channel_id=1, source_target_pairs={{0,8},{4,12},{8,24},{12,28},{16,0},{20,4},{24,16},{28,20},{1,9},{5... | collective-permute-start | bytes 552968 | tf_op jit(solution)/shard_map/ppermute | solution.py:77
  121.6 16.2 %collective-permute-start.35 = (bf16[256,768]{1,0:T(8,128)(2,1)S(1)}, bf16[256,768]{1,0:T(8,128)(2,1)S(1)}, u32[]{:S(2)}, u32[]{:S(2)}) collective-permute-start(bf16[256,768]{1,0:T(8,128)(2,1)S(1)} %fusion.39), channel_id=1, source_target_pairs={{0,2},{1,3},{2,0},{3,1},{4,6},{5,7},{6,4},{7,5},{8,10},{9,11},{10,... | collective-permute-start | bytes 1179656 | tf_op jit(solution)/shard_map/ppermute | solution.py:35
  123.3 13.7 %collective-permute-start.39 = (bf16[192,768]{1,0:T(8,128)(2,1)S(1)}, bf16[192,768]{1,0:T(8,128)(2,1)S(1)}, u32[]{:S(2)}, u32[]{:S(2)}) collective-permute-start(bf16[192,768]{1,0:T(8,128)(2,1)S(1)} %pad_maximum_fusion.3.refs_0_), channel_id=1, source_target_pairs={{0,8},{4,12},{8,24},{12,28},{16,0},{20,4},{24,16},{28,20},{1,9},{5... | collective-permute-start | bytes 884744 | tf_op jit(solution)/shard_map/ppermute | solution.py:77
  124.1 12.8 %collective-permute-start.38 = (bf16[192,768]{1,0:T(8,128)(2,1)S(1)}, bf16[192,768]{1,0:T(8,128)(2,1)S(1)}, u32[]{:S(2)}, u32[]{:S(2)}) collective-permute-start(bf16[192,768]{1,0:T(8,128)(2,1)S(1)} %pad_maximum_fusion.3.refs_0_), channel_id=1, source_target_pairs={{0,4},{4,0},{8,12},{12,8},{16,20},{20,16},{24,28},{28,24},{1,5},{5... | collective-permute-start | bytes 884744 | tf_op jit(solution)/shard_map/ppermute | solution.py:81
  138.4 13.5 %collective-permute-start.41 = (bf16[256,768]{1,0:T(8,128)(2,1)S(1)}, bf16[256,768]{1,0:T(8,128)(2,1)S(1)}, u32[]{:S(2)}, u32[]{:S(2)}) collective-permute-start(bf16[256,768]{1,0:T(8,128)(2,1)S(1)} %add_convert_fusion.1.refs_8_.refs_0_), channel_id=1, source_target_pairs={{0,2},{1,3},{2,0},{3,1},{4,6},{5,7},{6,4},{7,5},{8,10},{9,11},{10,... | collective-permute-start | bytes 1179656 | tf_op jit(solution)/shard_map/ppermute | solution.py:35
  265.7 13.2 %collective-permute-start.64 = (bf16[256,768]{1,0:T(8,128)(2,1)S(1)}, bf16[256,768]{1,0:T(8,128)(2,1)S(1)}, u32[]{:S(2)}, u32[]{:S(2)}) collective-permute-start(bf16[256,768]{1,0:T(8,128)(2,1)S(1)} %get-tuple-element.295.refs_12_.refs_4_), channel_id=1, source_target_pairs={{0,2},{1,3},{2,0},{3,1},{4,6},{5,7},{6,4},{7,5},{8,10},{9,11},{10,... | collective-permute-start | bytes 1179656 | tf_op jit(solution)/shard_map/ppermute | solution.py:35
  293.0 15.3 %collective-permute-start.71 = (bf16[256,768]{1,0:T(8,128)(2,1)S(1)}, bf16[256,768]{1,0:T(8,128)(2,1)S(1)}, u32[]{:S(2)}, u32[]{:S(2)}) collective-permute-start(bf16[256,768]{1,0:T(8,128)(2,1)S(1)} %fusion.43), channel_id=1, source_target_pairs={{0,2},{1,3},{2,0},{3,1},{4,6},{5,7},{6,4},{7,5},{8,10},{9,11},{10,... | collective-permute-start | bytes 1179656 | tf_op jit(solution)/shard_map/ppermute | solution.py:35
  309.7 12.4 %collective-permute-start.76 = (bf16[256,768]{1,0:T(8,128)(2,1)S(1)}, bf16[256,768]{1,0:T(8,128)(2,1)S(1)}, u32[]{:S(2)}, u32[]{:S(2)}) collective-permute-start(bf16[256,768]{1,0:T(8,128)(2,1)S(1)} %get-tuple-element.293.refs_8_.refs_1_), channel_id=1, source_target_pairs={{0,2},{1,3},{2,0},{3,1},{4,6},{5,7},{6,4},{7,5},{8,10},{9,11},{10,... | collective-permute-start | bytes 1179656 | tf_op jit(solution)/shard_map/ppermute | solution.py:35
  343.3 17.9 %collective-permute-start.83 = (bf16[256,768]{1,0:T(8,128)(2,1)S(1)}, bf16[256,768]{1,0:T(8,128)(2,1)S(1)}, u32[]{:S(2)}, u32[]{:S(2)}) collective-permute-start(bf16[256,768]{1,0:T(8,128)(2,1)S(1)} %fusion.44), channel_id=1, source_target_pairs={{0,2},{1,3},{2,0},{3,1},{4,6},{5,7},{6,4},{7,5},{8,10},{9,11},{10,... | collective-permute-start | bytes 1179656 | tf_op jit(solution)/shard_map/ppermute | solution.py:35
  345.5 15.7 %collective-permute-start.84 = (bf16[192,768]{1,0:T(8,128)(2,1)S(1)}, bf16[192,768]{1,0:T(8,128)(2,1)S(1)}, u32[]{:S(2)}, u32[]{:S(2)}) collective-permute-start(bf16[192,768]{1,0:T(8,128)(2,1)S(1)} %copy-done.85), channel_id=1, source_target_pairs={{0,4},{4,0},{8,12},{12,8},{16,20},{20,16},{24,28},{28,24},{1,5},{5... | collective-permute-start | bytes 884744 | tf_op jit(solution)/shard_map/ppermute | solution.py:81
  346.5 14.8 %collective-permute-start.85 = (bf16[192,768]{1,0:T(8,128)(2,1)S(1)}, bf16[192,768]{1,0:T(8,128)(2,1)S(1)}, u32[]{:S(2)}, u32[]{:S(2)}) collective-permute-start(bf16[192,768]{1,0:T(8,128)(2,1)S(1)} %add_convert_fusion.5), channel_id=1, source_target_pairs={{0,8},{4,12},{8,24},{12,28},{16,0},{20,4},{24,16},{28,20},{1,9},{5... | collective-permute-start | bytes 884744 | tf_op jit(solution)/shard_map/ppermute | solution.py:77
  359.8 25.4 %collective-permute-start.95 = (bf16[192,768]{1,0:T(8,128)(2,1)}, bf16[192,768]{1,0:T(8,128)(2,1)S(1)}, u32[]{:S(2)}, u32[]{:S(2)}) collective-permute-start(bf16[192,768]{1,0:T(8,128)(2,1)} %get-tuple-element.247), channel_id=1, source_target_pairs={{0,4},{4,0},{8,12},{12,8},{16,20},{20,16},{24,28},{28,24},{1,5},{5... | collective-permute-start | bytes 884744 | tf_op jit(solution)/shard_map/ppermute | solution.py:81
  390.4 34.7 %collective-permute-start.111 = (bf16[24,768]{1,0:T(8,128)(2,1)S(1)}, bf16[24,768]{1,0:T(8,128)(2,1)S(1)}, u32[]{:S(2)}, u32[]{:S(2)}) collective-permute-start(bf16[24,768]{1,0:T(8,128)(2,1)S(1)} %copy-done.52), channel_id=1, source_target_pairs={{0,0},{1,8},{2,16},{3,24},{4,4},{5,12},{6,20},{7,28},{8,1},{9,9},{... | collective-permute-start | bytes 110600 | tf_op jit(solution)/shard_map/ppermute | solution.py:135
  393.6 12.7 %collective-permute-start.101 = (bf16[192,768]{1,0:T(8,128)(2,1)S(1)}, bf16[192,768]{1,0:T(8,128)(2,1)S(1)}, u32[]{:S(2)}, u32[]{:S(2)}) collective-permute-start(bf16[192,768]{1,0:T(8,128)(2,1)S(1)} %copy-done.81), channel_id=1, source_target_pairs={{0,4},{4,0},{8,12},{12,8},{16,20},{20,16},{24,28},{28,24},{1,5},{5... | collective-permute-start | bytes 884744 | tf_op jit(solution)/shard_map/ppermute | solution.py:81
  395.4 12.3 %collective-permute-start.102 = (bf16[192,768]{1,0:T(8,128)(2,1)S(1)}, bf16[192,768]{1,0:T(8,128)(2,1)S(1)}, u32[]{:S(2)}, u32[]{:S(2)}) collective-permute-start(bf16[192,768]{1,0:T(8,128)(2,1)S(1)} %add_convert_fusion.3), channel_id=1, source_target_pairs={{0,8},{4,12},{8,24},{12,28},{16,0},{20,4},{24,16},{28,20},{1,9},{5... | collective-permute-start | bytes 884744 | tf_op jit(solution)/shard_map/ppermute | solution.py:77
  (197 other events, 1411.8 us)

commit v4 on v3

--- a/solution.py
+++ b/solution.py
@@ -49,7 +49,7 @@
 
 
 def scatter_seq(sent, kept, work=None):
-    half = kept + swap_seq(sent, 1).astype(F32)
+    half = kept.astype(F32) + swap_seq(sent, 1).astype(F32)
     sent = half[1].astype(BF)
     got = swap_seq(sent, 2)
     if work is not None:
@@ -59,12 +59,13 @@
 
 def exchange_seq(parts):
     place = lax.axis_index("seq")
-    y_bit, c_bit = place // 2, place % 2
-    grid = parts.reshape((2, 2) + parts.shape[1:])
-    kept, sent = by_bit(c_bit, grid[:, 0], grid[:, 1])
-    half = jnp.stack(by_bit(c_bit, kept, swap_seq(sent, 1)), axis=1)
-    kept, sent = by_bit(y_bit, half[0], half[1])
-    return jnp.stack(by_bit(y_bit, kept, swap_seq(sent, 2))).reshape(parts.shape)
+    own = [lax.dynamic_index_in_dim(parts, place ^ bits, 0, keepdims=False) for bits in range(4)]
+    got = own[:1] + [swap_seq(own[bits], bits) for bits in (1, 2, 3)]
+    core = place % 2 == 0
+    pairs = [(jnp.where(core, got[at], got[at + 1]), jnp.where(core, got[at + 1], got[at])) for at in (0, 2)]
+    here = place // 2 == 0
+    ends = [jnp.where(here, pairs[0][at], pairs[1][at]) for at in (0, 1)]
+    return jnp.stack(ends + [jnp.where(here, pairs[1][at], pairs[0][at]) for at in (0, 1)])
 
 
 def over_line(block, steps=1):
@@ -168,7 +169,7 @@
 
 def put_part(sent_ref, kept_ref, part, values):
     if part < 2:
-        kept_ref[part] = values
+        kept_ref[part] = values.astype(BF)
     else:
         sent_ref[part - 2] = values.astype(BF)
 
@@ -246,7 +247,7 @@
 
 
 def two_parts(width):
-    return [((2, ROWS, width), BF), ((2, ROWS, width), F32)]
+    return [((2, ROWS, width), BF)] * 2
 
 
 def attend(place, first, blocks, parts, group):
@@ -682,10 +683,9 @@
         normed_cot = scatter_seq(sent, kept, attn_work)
         back, gain_sum_a, shift_sum_a = norm_back(unit_a, inverse_a, gains[layer, 0], normed_cot)
         cot = cot + back
-        norm_sums.append(jnp.stack([gain_sum_a, gain_sum_b, shift_sum_a, shift_sum_b]))
+        norm_sums.append(jnp.concatenate([gain_sum_a, gain_sum_b, shift_sum_a, shift_sum_b]))
 
     sent, kept = last_feed
-    outputs = (hidden + BRANCH_SCALE * scatter_seq(after(sent, cot), kept)).astype(BF)
     sums = jnp.concatenate(norm_sums[::-1])
     column_back = {}
     row_back = {}
@@ -719,21 +719,24 @@
         return up.reshape(piece, -1), qkv
 
     if ruled:
-        mark = sums_of["attn", 0].advance() + sums_of["feed", 0].advance() + [outputs]
-        for bit in (1, 2):
-            sums = sums + swap_seq(sums, bit)
-        sums = after(sums, *mark)
+        mark = sums_of["attn", 0].advance() + sums_of["feed", 0].advance()
+        near = swap_seq(after(sent, cot), 1)
+        sums = after(sums + swap_seq(sums, 1), *mark, near)
+        half = kept.astype(F32) + near.astype(F32)
         mark = step_sums(sums, ("attn", 0), ("feed", 0))
+        got = swap_seq(after(half[1].astype(BF), sums), 2)
+        sums = after(sums + swap_seq(sums, 2), *mark, got)
+        mark = step_sums(sums, ("attn", 0))
+        sums = after(sums + lax.ppermute(sums, "fsdp", [(f, f ^ 1) for f in range(8)]), *mark)
+        outputs = hidden + BRANCH_SCALE * (half[0] + got.astype(F32))
         sent_1 = send_home(1, sums)
-        for bit in (1, 2):
+        for bit in (2, 4):
             sums = sums + lax.ppermute(sums, "fsdp", [(f, f ^ bit) for f in range(8)])
-        sums = after(sums, *mark)
-        step_sums(sums, ("attn", 0))
-        sums = sums + lax.ppermute(sums, "fsdp", [(f, f ^ 4) for f in range(8)])
         weight_grads = store(send_home(0), sent_1, group, seq, fsdp)
     else:
         take(0)
         take(1)
+        outputs = hidden + BRANCH_SCALE * scatter_seq(sent, kept)
         home_0, home_1 = home(0), home(1)
         sums = lax.psum(sums, BOTH)
         up_grads, qkv_grads = zip(home_0, home_1)
@@ -741,9 +744,9 @@
         down_grads = [row_back["down", layer] for layer in range(LAYERS)]
         weight_grads = [jnp.stack(grads) for grads in (qkv_grads, out_grads, up_grads, down_grads)]
     whose = lax.axis_index("fsdp") * seq + place
-    sums = lax.dynamic_slice_in_dim(sums, whose * piece, piece, 1).reshape(LAYERS, 4, piece)
+    sums = lax.dynamic_slice_in_dim(sums.reshape(-1, width), whose * piece, piece, 1).reshape(LAYERS, 4, piece)
     return (
-        outputs,
+        outputs.astype(BF),
         cot.astype(BF),
         sums[:, :2],
         sums[:, 2],

time: 434 us -> 423 us (0.975)
  other arithmetic: 34.4 us -> 25.5 us
  local copies, waits for them, and re-layouts: 19.3 us -> 12.6 us
    ppermute x32, waiting for transfers between devices: 55.6 us -> 81.9 us  [over_side(): return lax.ppermute(block, 'fsdp', [(f, f ^ 1) for f in range(8)])]
    ppermute x50 -> x54, waiting for transfers between devices: 54.6 us -> 37.7 us  [swap_seq(): return lax.ppermute(values, 'seq', [(s, s ^ bit) for s in range(4)])]
    ppermute x24, waiting for transfers between devices: 47.3 us -> 37.9 us  [over_line(): return lax.ppermute(block, 'fsdp', moves)]
    ppermute x50 -> x54, starting transfers between devices: 37.5 us -> 41.1 us  [swap_seq(): return lax.ppermute(values, 'seq', [(s, s ^ bit) for s in range(4)])]
  transfers between devices with their start and end apart: 112 -> 116, of which waited for: 49 -> 58; matrix products, arithmetic and copies ran while one was open for 7% -> 4% of each run, Pallas kernels for 7% -> 8%
where the time goes in v4:
time: 423 us; the launch traced here: 416 us
  waiting for transfers between devices  160 us (38%)
  Pallas kernels  109 us (26%)
  starting transfers between devices  105 us (25%)
  other arithmetic  25.5 us (6%)
  local copies, waits for them, and re-layouts  12.6 us (3%)
    pallas_call x12, Pallas kernels, call(): pl.pallas_call(kernel, in_specs=in_specs, out_shape=tuple((jax.ShapeDtype...  105 us
    ppermute x32, waiting for transfers between devices, over_side(): return lax.ppermute(block, 'fsdp', [(f, f ^ 1) for f in range(8)])  81.9 us
    ppermute x54, starting transfers between devices, swap_seq(): return lax.ppermute(values, 'seq', [(s, s ^ bit) for s in range(4)])  41.1 us
    ppermute x24, waiting for transfers between devices, over_line(): return lax.ppermute(block, 'fsdp', moves)  37.9 us
    ppermute x54, waiting for transfers between devices, swap_seq(): return lax.ppermute(values, 'seq', [(s, s ^ bit) for s in range(4)])  37.7 us
    ppermute x32, starting transfers between devices, over_side(): return lax.ppermute(block, 'fsdp', [(f, f ^ 1) for f in range(8)])  33 us
    ppermute x24, starting transfers between devices, over_line(): return lax.ppermute(block, 'fsdp', moves)  25.8 us
  transfers between devices with their start and end apart: 116, of which 58 were waited for; matrix products, arithmetic and copies ran while one was open for 4% of the time, Pallas kernels for 8%

profile of v4, /device:TPU:0, one launch (start us, length us, event | category | flops | bytes accessed | tf_op | source)
XLA Modules:
  0.0 415.7 jit_solution(15542246901103357790)
XLA Ops:
  11.8 5.9 %collective-permute-start.8 = (bf16[72,768]{1,0:T(8,128)(2,1)S(1)}, bf16[72,768]{1,0:T(8,128)(2,1)S(1)}, u32[]{:S(2)}, u32[]{:S(2)}) collective-permute-start(bf16[72,768]{1,0:T(8,128)(2,1)S(1)} %get-tuple-element.324), channel_id=1, source_target_pairs={{0,2},{1,3},{2,0},{3,1},{4,6},{5,7},{6,4},{7,5},{8,10},{9,11},{10,... | collective-permute-start | bytes 331784 | tf_op jit(solution)/shard_map/ppermute | solution.py:35
  63.6 11.2 %attend.2 = (bf16[1024,576]{1,0:T(8,128)(2,1)}, bf16[1024,192]{1,0:T(8,128)(2,1)}, f32[1024,3]{1,0:T(8,128)}, bf16[2,256,768]{2,1,0:T(8,128)(2,1)}, bf16[2,256,768]{2,1,0:T(8,128)(2,1)}) custom-call(s32[9]{0:T(128)} %concatenate.40.place_ref, s32[1024,1]{1,0:T(8,128)} %copy.33.first_ref, bf16[120,768]{1,0:T(8,128)(2,1)} %copy-done.7, ...), custom_call_target="tpu_custom_call" | custom-call | flops 10000000000 | bytes 30000000 | tf_op jit(solution)/shard_map/attend/pallas_call | solution.py:238
  83.9 8.0 %collective-permute-done.28.refs_4_ = bf16[120,768]{1,0:T(8,128)(2,1)S(1)} collective-permute-done((bf16[120,768]{1,0:T(8,128)(2,1)S(1)}, bf16[120,768]{1,0:T(8,128)(2,1)S(1)}, u32[]{:S(2)}, u32[]{:S(2)}) %collective-permute-start.28) | collective-permute-done | bytes 184352 | tf_op jit(solution)/shard_map/ppermute | solution.py:82
  99.5 8.9 %collective-permute-done.32.refs_5_ = bf16[120,768]{1,0:T(8,128)(2,1)S(1)} collective-permute-done((bf16[120,768]{1,0:T(8,128)(2,1)S(1)}, bf16[120,768]{1,0:T(8,128)(2,1)S(1)}, u32[]{:S(2)}, u32[]{:S(2)}) %collective-permute-start.32) | collective-permute-done | bytes 184352 | tf_op jit(solution)/shard_map/ppermute | solution.py:82
  111.0 5.9 %feed.2 = (bf16[2,256,768]{2,1,0:T(8,128)(2,1)}, bf16[2,256,768]{2,1,0:T(8,128)(2,1)}) custom-call(s32[9]{0:T(128)} %concatenate.40.place_ref, bf16[192,768]{1,0:T(8,128)(2,1)} %copy-done.19, bf16[192,768]{1,0:T(8,128)(2,1)} %collective-permute-done.17.refs_1_, bf16[192,768]{1,0:T(8,128)(2,1)} %copy-done.76, bf16[192,768]{1,0:T(8,128)(2,1)} %copy-done.78, ...), custom_call_target="tpu_custom_call" | custom-call | flops 5000000000 | bytes 15000000 | tf_op jit(solution)/shard_map/feed/pallas_call | solution.py:238
  125.7 8.6 %collective-permute-done.38.refs_6_ = bf16[120,768]{1,0:T(8,128)(2,1)S(1)} collective-permute-done((bf16[120,768]{1,0:T(8,128)(2,1)S(1)}, bf16[120,768]{1,0:T(8,128)(2,1)S(1)}, u32[]{:S(2)}, u32[]{:S(2)}) %collective-permute-start.38) | collective-permute-done | bytes 184352 | tf_op jit(solution)/shard_map/ppermute | solution.py:82
  140.2 9.2 %collective-permute-done.42.refs_7_ = bf16[120,768]{1,0:T(8,128)(2,1)S(1)} collective-permute-done((bf16[120,768]{1,0:T(8,128)(2,1)S(1)}, bf16[120,768]{1,0:T(8,128)(2,1)S(1)}, u32[]{:S(2)}, u32[]{:S(2)}) %collective-permute-start.42) | collective-permute-done | bytes 184352 | tf_op jit(solution)/shard_map/ppermute | solution.py:82
  152.0 10.9 %attend.3 = (bf16[1024,576]{1,0:T(8,128)(2,1)}, bf16[1024,192]{1,0:T(8,128)(2,1)}, f32[1024,3]{1,0:T(8,128)}, bf16[2,256,768]{2,1,0:T(8,128)(2,1)}, bf16[2,256,768]{2,1,0:T(8,128)(2,1)}) custom-call(s32[9]{0:T(128)} %concatenate.40.place_ref, s32[1024,1]{1,0:T(8,128)} %copy.33.first_ref, bf16[120,768]{1,0:T(8,128)(2,1)} %copy-done.36, ...), custom_call_target="tpu_custom_call" | custom-call | flops 10000000000 | bytes 30000000 | tf_op jit(solution)/shard_map/attend/pallas_call | solution.py:238
  169.2 7.0 %collective-permute-done.50.refs_6_ = bf16[192,768]{1,0:T(8,128)(2,1)S(1)} collective-permute-done((bf16[192,768]{1,0:T(8,128)(2,1)S(1)}, bf16[192,768]{1,0:T(8,128)(2,1)S(1)}, u32[]{:S(2)}, u32[]{:S(2)}) %collective-permute-start.50) | collective-permute-done | bytes 294944 | tf_op jit(solution)/shard_map/ppermute | solution.py:82
  181.5 6.7 %collective-permute-done.52.refs_7_ = bf16[192,768]{1,0:T(8,128)(2,1)S(1)} collective-permute-done((bf16[192,768]{1,0:T(8,128)(2,1)S(1)}, bf16[192,768]{1,0:T(8,128)(2,1)S(1)}, u32[]{:S(2)}, u32[]{:S(2)}) %collective-permute-start.52) | collective-permute-done | bytes 294944 | tf_op jit(solution)/shard_map/ppermute | solution.py:82
  191.6 8.8 %feed_back.2 = (bf16[1024,768]{1,0:T(8,128)(2,1)}, bf16[1024,768]{1,0:T(8,128)(2,1)}, bf16[2,256,768]{2,1,0:T(8,128)(2,1)}, bf16[2,256,768]{2,1,0:T(8,128)(2,1)}) custom-call(s32[9]{0:T(128)} %concatenate.40.place_ref, bf16[192,768]{1,0:T(8,128)(2,1)} %copy-done.20, bf16[192,768]{1,0:T(8,128)(2,1)} %copy-done.84, bf16[192,768]{1,0:T(8,128)(2,1)} %copy-done.87, ...), custom_call_target="tpu_custom_call" | custom-call | flops 8000000000 | bytes 24000000 | tf_op jit(solution)/shard_map/feed_back/pallas_call | solution.py:238
  205.7 6.8 %feed_sum.2 = (bf16[192,768]{1,0:T(8,128)(2,1)}, bf16[192,768]{1,0:T(8,128)(2,1)}, bf16[192,768]{1,0:T(8,128)(2,1)}, bf16[192,768]{1,0:T(8,128)(2,1)}, bf16[192,...) custom-call(s32[9]{0:T(128)} %concatenate.40.place_ref, ...), custom_call_target="tpu_custom_call" | custom-call | flops 6000000000 | bytes 18000000 | tf_op jit(solution)/shard_map/feed_sum/pallas_call | solution.py:238
  218.5 5.9 %feed.3 = (bf16[2,256,768]{2,1,0:T(8,128)(2,1)}, bf16[2,256,768]{2,1,0:T(8,128)(2,1)}) custom-call(s32[9]{0:T(128)} %concatenate.40.place_ref, bf16[192,768]{1,0:T(8,128)(2,1)} %copy-done.20, bf16[192,768]{1,0:T(8,128)(2,1)} %copy-done.84, bf16[192,768]{1,0:T(8,128)(2,1)} %copy-done.87, bf16[192,768]{1,0:T(8,128)(2,1)} %copy-done.90, ...), custom_call_target="tpu_custom_call" | custom-call | flops 5000000000 | bytes 15000000 | tf_op jit(solution)/shard_map/feed/pallas_call | solution.py:238
  229.7 14.5 %attend_back.2 = (bf16[1024,576]{1,0:T(8,128)(2,1)}, bf16[2,256,768]{2,1,0:T(8,128)(2,1)}, bf16[2,256,768]{2,1,0:T(8,128)(2,1)}) custom-call(s32[9]{0:T(128)} %concatenate.40.place_ref, s32[1024,1]{1,0:T(8,128)} %copy.33.first_ref, bf16[1024,576]{1,0:T(8,128)(2,1)} %get-tuple-element.182.mixed_ref, f32[1024,3]{1,0:T(8,128)} %get-tuple-element.183.total_ref, ...), custom_call_target="tpu_custom_call" | custom-call | flops 14000000000 | bytes 42000000 | tf_op jit(solution)/shard_map/attend_back/pallas_call | solution.py:238
  250.4 5.3 %attend_sum.2 = (bf16[120,768]{1,0:T(8,128)(2,1)}, bf16[120,768]{1,0:T(8,128)(2,1)}, bf16[120,768]{1,0:T(8,128)(2,1)}, bf16[120,768]{1,0:T(8,128)(2,1)}, bf16[12...) custom-call(s32[9]{0:T(128)} %concatenate.40.place_ref, ...), custom_call_target="tpu_custom_call" | custom-call | flops 5000000000 | bytes 15000000 | tf_op jit(solution)/shard_map/attend_sum/pallas_call | solution.py:238
  264.8 9.0 %collective-permute-done.69 = bf16[120,768]{1,0:T(8,128)(2,1)S(1)} collective-permute-done((bf16[120,768]{1,0:T(8,128)(2,1)S(1)}, bf16[120,768]{1,0:T(8,128)(2,1)S(1)}, u32[]{:S(2)}, u32[]{:S(2)}) %collective-permute-start.69) | collective-permute-done | bytes 184352 | tf_op jit(solution)/shard_map/ppermute | solution.py:82
  276.4 8.8 %feed_back.3 = (bf16[1024,768]{1,0:T(8,128)(2,1)}, bf16[1024,768]{1,0:T(8,128)(2,1)}, bf16[2,256,768]{2,1,0:T(8,128)(2,1)}, bf16[2,256,768]{2,1,0:T(8,128)(2,1)}) custom-call(s32[9]{0:T(128)} %concatenate.40.place_ref, bf16[192,768]{1,0:T(8,128)(2,1)} %copy-done.19, bf16[192,768]{1,0:T(8,128)(2,1)} %collective-permute-done.17.refs_1_, ...), custom_call_target="tpu_custom_call" | custom-call | flops 8000000000 | bytes 24000000 | tf_op jit(solution)/shard_map/feed_back/pallas_call | solution.py:238
  293.6 6.8 %feed_sum.3 = (bf16[192,768]{1,0:T(8,128)(2,1)}, bf16[192,768]{1,0:T(8,128)(2,1)}, bf16[192,768]{1,0:T(8,128)(2,1)}, bf16[192,768]{1,0:T(8,128)(2,1)}, bf16[192,...) custom-call(s32[9]{0:T(128)} %concatenate.40.place_ref, ...), custom_call_target="tpu_custom_call" | custom-call | flops 6000000000 | bytes 18000000 | tf_op jit(solution)/shard_map/feed_sum/pallas_call | solution.py:238
  309.2 4.7 %collective-permute-done.81 = bf16[120,768]{1,0:T(8,128)(2,1)S(1)} collective-permute-done((bf16[120,768]{1,0:T(8,128)(2,1)S(1)}, bf16[120,768]{1,0:T(8,128)(2,1)S(1)}, u32[]{:S(2)}, u32[]{:S(2)}) %collective-permute-start.81) | collective-permute-done | bytes 184352 | tf_op jit(solution)/shard_map/ppermute | solution.py:78
  319.2 14.4 %attend_back.3 = (bf16[1024,576]{1,0:T(8,128)(2,1)}, bf16[2,256,768]{2,1,0:T(8,128)(2,1)}, bf16[2,256,768]{2,1,0:T(8,128)(2,1)}) custom-call(s32[9]{0:T(128)} %concatenate.40.place_ref, s32[1024,1]{1,0:T(8,128)} %copy.33.first_ref, bf16[1024,576]{1,0:T(8,128)(2,1)} %get-tuple-element.220.mixed_ref, f32[1024,3]{1,0:T(8,128)} %get-tuple-element.221.total_ref, ...), custom_call_target="tpu_custom_call" | custom-call | flops 14000000000 | bytes 42000000 | tf_op jit(solution)/shard_map/attend_back/pallas_call | solution.py:238
  339.4 5.3 %attend_sum.3 = (bf16[120,768]{1,0:T(8,128)(2,1)}, bf16[120,768]{1,0:T(8,128)(2,1)}, bf16[120,768]{1,0:T(8,128)(2,1)}, bf16[120,768]{1,0:T(8,128)(2,1)}, bf16[12...) custom-call(s32[9]{0:T(128)} %concatenate.40.place_ref, ...), custom_call_target="tpu_custom_call" | custom-call | flops 5000000000 | bytes 15000000 | tf_op jit(solution)/shard_map/attend_sum/pallas_call | solution.py:238
  348.7 3.7 collective-permute-done.90
  356.7 4.9 %collective-permute-done.86 = bf16[192,768]{1,0:T(8,128)(2,1)S(1)} collective-permute-done((bf16[192,768]{1,0:T(8,128)(2,1)S(1)}, bf16[192,768]{1,0:T(8,128)(2,1)S(1)}, u32[]{:S(2)}, u32[]{:S(2)}) %collective-permute-start.86) | collective-permute-done | bytes 294944 | tf_op jit(solution)/shard_map/ppermute | solution.py:82
  398.8 3.8 collective-permute-start.109
  (590 shorter events, 228.0 us)
Async XLA Ops:
  19.5 23.6 %collective-permute-start.14 = (bf16[256,768]{1,0:T(8,128)(2,1)S(1)}, bf16[256,768]{1,0:T(8,128)(2,1)S(1)}, u32[]{:S(2)}, u32[]{:S(2)}) collective-permute-start(bf16[256,768]{1,0:T(8,128)(2,1)S(1)} %copy-done), channel_id=1, source_target_pairs={{0,2},{1,3},{2,0},{3,1},{4,6},{5,7},{6,4},{7,5},{8,10},{9,11},{10,... | collective-permute-start | bytes 1179656 | tf_op jit(solution)/shard_map/ppermute | solution.py:35
  43.1 11.9 %collective-permute-start.15 = (bf16[256,768]{1,0:T(8,128)(2,1)S(1)}, bf16[256,768]{1,0:T(8,128)(2,1)S(1)}, u32[]{:S(2)}, u32[]{:S(2)}) collective-permute-start(bf16[256,768]{1,0:T(8,128)(2,1)S(1)} %copy-done), channel_id=1, source_target_pairs={{0,1},{1,0},{2,3},{3,2},{4,5},{5,4},{6,7},{7,6},{8,9},{9,8},{10,11... | collective-permute-start | bytes 1179656 | tf_op jit(solution)/shard_map/ppermute | solution.py:35
  43.2 14.8 %collective-permute-start.21 = (bf16[256,768]{1,0:T(8,128)(2,1)S(1)}, bf16[256,768]{1,0:T(8,128)(2,1)}, u32[]{:S(2)}, u32[]{:S(2)}) collective-permute-start(bf16[256,768]{1,0:T(8,128)(2,1)S(1)} %fusion.19.refs_12_.refs_4_), channel_id=1, source_target_pairs={{0,2},{1,3},{2,0},{3,1},{4,6},{5,7},{6,4},{7,5},{8,10},{9,11},{10,... | collective-permute-start | bytes 1179656 | tf_op jit(solution)/shard_map/ppermute | solution.py:35
  45.7 15.5 %collective-permute-start.22 = (bf16[256,768]{1,0:T(8,128)(2,1)S(1)}, bf16[256,768]{1,0:T(8,128)(2,1)}, u32[]{:S(2)}, u32[]{:S(2)}) collective-permute-start(bf16[256,768]{1,0:T(8,128)(2,1)S(1)} %fusion.19.refs_12_.refs_4_), channel_id=1, source_target_pairs={{0,1},{1,0},{2,3},{3,2},{4,5},{5,4},{6,7},{7,6},{8,9},{9,8},{10,11... | collective-permute-start | bytes 1179656 | tf_op jit(solution)/shard_map/ppermute | solution.py:35
  78.6 15.3 %collective-permute-start.25 = (bf16[256,768]{1,0:T(8,128)(2,1)S(1)}, bf16[256,768]{1,0:T(8,128)(2,1)S(1)}, u32[]{:S(2)}, u32[]{:S(2)}) collective-permute-start(bf16[256,768]{1,0:T(8,128)(2,1)S(1)} %fusion.38), channel_id=1, source_target_pairs={{0,2},{1,3},{2,0},{3,1},{4,6},{5,7},{6,4},{7,5},{8,10},{9,11},{10,... | collective-permute-start | bytes 1179656 | tf_op jit(solution)/shard_map/ppermute | solution.py:35
  78.8 15.0 %collective-permute-start.26 = (bf16[192,768]{1,0:T(8,128)(2,1)S(1)}, bf16[192,768]{1,0:T(8,128)(2,1)S(1)}, u32[]{:S(2)}, u32[]{:S(2)}) collective-permute-start(bf16[192,768]{1,0:T(8,128)(2,1)S(1)} %collective-permute-done.20.refs_2_), channel_id=1, source_target_pairs={{0,4},{4,0},{8,12},{12,8},{16,20},{20,16},{24,28},{28,24},{1,5},{5... | collective-permute-start | bytes 884744 | tf_op jit(solution)/shard_map/ppermute | solution.py:82
  80.2 13.6 %collective-permute-start.27 = (bf16[192,768]{1,0:T(8,128)(2,1)S(1)}, bf16[192,768]{1,0:T(8,128)(2,1)S(1)}, u32[]{:S(2)}, u32[]{:S(2)}) collective-permute-start(bf16[192,768]{1,0:T(8,128)(2,1)S(1)} %collective-permute-done.20.refs_2_), channel_id=1, source_target_pairs={{0,8},{4,12},{8,24},{12,28},{16,0},{20,4},{24,16},{28,20},{1,9},{5... | collective-permute-start | bytes 884744 | tf_op jit(solution)/shard_map/ppermute | solution.py:78
  82.0 11.9 %collective-permute-start.29 = (bf16[120,768]{1,0:T(8,128)(2,1)S(1)}, bf16[120,768]{1,0:T(8,128)(2,1)S(1)}, u32[]{:S(2)}, u32[]{:S(2)}) collective-permute-start(bf16[120,768]{1,0:T(8,128)(2,1)S(1)} %pad_maximum_fusion.8.refs_0_), channel_id=1, source_target_pairs={{0,8},{4,12},{8,24},{12,28},{16,0},{20,4},{24,16},{28,20},{1,9},{5... | collective-permute-start | bytes 552968 | tf_op jit(solution)/shard_map/ppermute | solution.py:78
  95.3 13.1 %collective-permute-start.31 = (bf16[256,768]{1,0:T(8,128)(2,1)S(1)}, bf16[256,768]{1,0:T(8,128)(2,1)S(1)}, u32[]{:S(2)}, u32[]{:S(2)}) collective-permute-start(bf16[256,768]{1,0:T(8,128)(2,1)S(1)} %add_convert_fusion.2.refs_8_.refs_0_), channel_id=1, source_target_pairs={{0,2},{1,3},{2,0},{3,1},{4,6},{5,7},{6,4},{7,5},{8,10},{9,11},{10,... | collective-permute-start | bytes 1179656 | tf_op jit(solution)/shard_map/ppermute | solution.py:35
  120.8 14.8 %collective-permute-start.37 = (bf16[256,768]{1,0:T(8,128)(2,1)S(1)}, bf16[256,768]{1,0:T(8,128)(2,1)S(1)}, u32[]{:S(2)}, u32[]{:S(2)}) collective-permute-start(bf16[256,768]{1,0:T(8,128)(2,1)S(1)} %fusion.39), channel_id=1, source_target_pairs={{0,2},{1,3},{2,0},{3,1},{4,6},{5,7},{6,4},{7,5},{8,10},{9,11},{10,... | collective-permute-start | bytes 1179656 | tf_op jit(solution)/shard_map/ppermute | solution.py:35
  121.5 14.1 %collective-permute-start.40 = (bf16[192,768]{1,0:T(8,128)(2,1)S(1)}, bf16[192,768]{1,0:T(8,128)(2,1)S(1)}, u32[]{:S(2)}, u32[]{:S(2)}) collective-permute-start(bf16[192,768]{1,0:T(8,128)(2,1)S(1)} %pad_maximum_fusion.3.refs_0_), channel_id=1, source_target_pairs={{0,4},{4,0},{8,12},{12,8},{16,20},{20,16},{24,28},{28,24},{1,5},{5... | collective-permute-start | bytes 884744 | tf_op jit(solution)/shard_map/ppermute | solution.py:82
  122.3 13.3 %collective-permute-start.41 = (bf16[192,768]{1,0:T(8,128)(2,1)S(1)}, bf16[192,768]{1,0:T(8,128)(2,1)S(1)}, u32[]{:S(2)}, u32[]{:S(2)}) collective-permute-start(bf16[192,768]{1,0:T(8,128)(2,1)S(1)} %pad_maximum_fusion.3.refs_0_), channel_id=1, source_target_pairs={{0,8},{4,12},{8,24},{12,28},{16,0},{20,4},{24,16},{28,20},{1,9},{5... | collective-permute-start | bytes 884744 | tf_op jit(solution)/shard_map/ppermute | solution.py:78
  122.4 11.9 %collective-permute-start.38 = (bf16[120,768]{1,0:T(8,128)(2,1)S(1)}, bf16[120,768]{1,0:T(8,128)(2,1)S(1)}, u32[]{:S(2)}, u32[]{:S(2)}) collective-permute-start(bf16[120,768]{1,0:T(8,128)(2,1)S(1)} %collective-permute-done.33.refs_2_), channel_id=1, source_target_pairs={{0,4},{4,0},{8,12},{12,8},{16,20},{20,16},{24,28},{28,24},{1,5},{5... | collective-permute-start | bytes 552968 | tf_op jit(solution)/shard_map/ppermute | solution.py:82
  123.8 11.8 %collective-permute-start.39 = (bf16[120,768]{1,0:T(8,128)(2,1)S(1)}, bf16[120,768]{1,0:T(8,128)(2,1)S(1)}, u32[]{:S(2)}, u32[]{:S(2)}) collective-permute-start(bf16[120,768]{1,0:T(8,128)(2,1)S(1)} %collective-permute-done.33.refs_2_), channel_id=1, source_target_pairs={{0,8},{4,12},{8,24},{12,28},{16,0},{20,4},{24,16},{28,20},{1,9},{5... | collective-permute-start | bytes 552968 | tf_op jit(solution)/shard_map/ppermute | solution.py:78
  136.6 12.8 %collective-permute-start.43 = (bf16[256,768]{1,0:T(8,128)(2,1)S(1)}, bf16[256,768]{1,0:T(8,128)(2,1)S(1)}, u32[]{:S(2)}, u32[]{:S(2)}) collective-permute-start(bf16[256,768]{1,0:T(8,128)(2,1)S(1)} %add_convert_fusion.1.refs_8_.refs_0_), channel_id=1, source_target_pairs={{0,2},{1,3},{2,0},{3,1},{4,6},{5,7},{6,4},{7,5},{8,10},{9,11},{10,... | collective-permute-start | bytes 1179656 | tf_op jit(solution)/shard_map/ppermute | solution.py:35
  166.8 11.8 %collective-permute-start.49 = (bf16[256,768]{1,0:T(8,128)(2,1)S(1)}, bf16[256,768]{1,0:T(8,128)(2,1)S(1)}, u32[]{:S(2)}, u32[]{:S(2)}) collective-permute-start(bf16[256,768]{1,0:T(8,128)(2,1)S(1)} %fusion.40), channel_id=1, source_target_pairs={{0,2},{1,3},{2,0},{3,1},{4,6},{5,7},{6,4},{7,5},{8,10},{9,11},{10,... | collective-permute-start | bytes 1179656 | tf_op jit(solution)/shard_map/ppermute | solution.py:35
  260.7 13.1 %collective-permute-start.66 = (bf16[256,768]{1,0:T(8,128)(2,1)S(1)}, bf16[256,768]{1,0:T(8,128)(2,1)S(1)}, u32[]{:S(2)}, u32[]{:S(2)}) collective-permute-start(bf16[256,768]{1,0:T(8,128)(2,1)S(1)} %get-tuple-element.301.refs_12_.refs_4_), channel_id=1, source_target_pairs={{0,2},{1,3},{2,0},{3,1},{4,6},{5,7},{6,4},{7,5},{8,10},{9,11},{10,... | collective-permute-start | bytes 1179656 | tf_op jit(solution)/shard_map/ppermute | solution.py:35
  261.7 12.1 %collective-permute-start.68 = (bf16[192,768]{1,0:T(8,128)(2,1)S(1)}, bf16[192,768]{1,0:T(8,128)(2,1)S(1)}, u32[]{:S(2)}, u32[]{:S(2)}) collective-permute-start(bf16[192,768]{1,0:T(8,128)(2,1)S(1)} %add_convert_fusion.7), channel_id=1, source_target_pairs={{0,8},{4,12},{8,24},{12,28},{16,0},{20,4},{24,16},{28,20},{1,9},{5... | collective-permute-start | bytes 884744 | tf_op jit(solution)/shard_map/ppermute | solution.py:78
  288.0 15.5 %collective-permute-start.73 = (bf16[256,768]{1,0:T(8,128)(2,1)S(1)}, bf16[256,768]{1,0:T(8,128)(2,1)S(1)}, u32[]{:S(2)}, u32[]{:S(2)}) collective-permute-start(bf16[256,768]{1,0:T(8,128)(2,1)S(1)} %fusion.43), channel_id=1, source_target_pairs={{0,2},{1,3},{2,0},{3,1},{4,6},{5,7},{6,4},{7,5},{8,10},{9,11},{10,... | collective-permute-start | bytes 1179656 | tf_op jit(solution)/shard_map/ppermute | solution.py:35
  304.8 12.2 %collective-permute-start.78 = (bf16[256,768]{1,0:T(8,128)(2,1)S(1)}, bf16[256,768]{1,0:T(8,128)(2,1)}, u32[]{:S(2)}, u32[]{:S(2)}) collective-permute-start(bf16[256,768]{1,0:T(8,128)(2,1)S(1)} %get-tuple-element.299.refs_8_.refs_1_), channel_id=1, source_target_pairs={{0,2},{1,3},{2,0},{3,1},{4,6},{5,7},{6,4},{7,5},{8,10},{9,11},{10,... | collective-permute-start | bytes 1179656 | tf_op jit(solution)/shard_map/ppermute | solution.py:35
  333.9 33.3 %collective-permute-start.95 = (bf16[192,768]{1,0:T(8,128)(2,1)}, bf16[192,768]{1,0:T(8,128)(2,1)S(1)}, u32[]{:S(2)}, u32[]{:S(2)}) collective-permute-start(bf16[192,768]{1,0:T(8,128)(2,1)} %get-tuple-element.249), channel_id=1, source_target_pairs={{0,4},{4,0},{8,12},{12,8},{16,20},{20,16},{24,28},{28,24},{1,5},{5... | collective-permute-start | bytes 884744 | tf_op jit(solution)/shard_map/ppermute | solution.py:82
  336.5 26.7 %collective-permute-start.85 = (bf16[256,768]{1,0:T(8,128)(2,1)S(1)}, bf16[256,768]{1,0:T(8,128)(2,1)S(1)}, u32[]{:S(2)}, u32[]{:S(2)}) collective-permute-start(bf16[256,768]{1,0:T(8,128)(2,1)S(1)} %fusion.44), channel_id=1, source_target_pairs={{0,2},{1,3},{2,0},{3,1},{4,6},{5,7},{6,4},{7,5},{8,10},{9,11},{10,... | collective-permute-start | bytes 1179656 | tf_op jit(solution)/shard_map/ppermute | solution.py:35
  345.8 19.3 %collective-permute-start.93 = (bf16[120,768]{1,0:T(8,128)(2,1)}, bf16[120,768]{1,0:T(8,128)(2,1)S(1)}, u32[]{:S(2)}, u32[]{:S(2)}) collective-permute-start(bf16[120,768]{1,0:T(8,128)(2,1)} %get-tuple-element.247), channel_id=1, source_target_pairs={{0,4},{4,0},{8,12},{12,8},{16,20},{20,16},{24,28},{28,24},{1,5},{5... | collective-permute-start | bytes 552968 | tf_op jit(solution)/shard_map/ppermute | solution.py:82
  398.1 13.3 %collective-permute-start.115 = (bf16[24,768]{1,0:T(8,128)(2,1)S(1)}, bf16[24,768]{1,0:T(8,128)(2,1)S(1)}, u32[]{:S(2)}, u32[]{:S(2)}) collective-permute-start(bf16[24,768]{1,0:T(8,128)(2,1)S(1)} %slice.253), channel_id=1, source_target_pairs={{0,0},{1,8},{2,16},{3,24},{4,4},{5,12},{6,20},{7,28},{8,1},{9,9},{... | collective-permute-start | bytes 110600 | tf_op jit(solution)/shard_map/ppermute | solution.py:136
  (200 other events, 1431.0 us)

commit v5 on v4

--- a/solution.py
+++ b/solution.py
@@ -730,9 +730,11 @@
         sums = after(sums + lax.ppermute(sums, "fsdp", [(f, f ^ 1) for f in range(8)]), *mark)
         outputs = hidden + BRANCH_SCALE * (half[0] + got.astype(F32))
         sent_1 = send_home(1, sums)
-        for bit in (2, 4):
-            sums = sums + lax.ppermute(sums, "fsdp", [(f, f ^ bit) for f in range(8)])
-        weight_grads = store(send_home(0), sent_1, group, seq, fsdp)
+        sums = sums + lax.ppermute(sums, "fsdp", [(f, f ^ 2) for f in range(8)])
+        sent_0 = send_home(0)
+        sums = after(sums, *sent_0[:2], *sent_1[:2])
+        sums = sums + lax.ppermute(sums, "fsdp", [(f, f ^ 4) for f in range(8)])
+        weight_grads = store(sent_0, sent_1, group, seq, fsdp)
     else:
         take(0)
         take(1)

time: 423 us -> 420 us (level)
  starting transfers between devices: 105 us -> 113 us
  waiting for transfers between devices: 160 us -> 153 us
  transfers between devices with their start and end apart: 116 -> 116, of which waited for: 58 -> 59; matrix products, arithmetic and copies ran while one was open for 4% -> 4% of each run, Pallas kernels for 8% -> 8%
where the time goes in v5:
time: 420 us; the launch traced here: 414 us
  waiting for transfers between devices  153 us (36%)
  starting transfers between devices  113 us (27%)
  Pallas kernels  109 us (26%)
  other arithmetic  23.9 us (6%)
  local copies, waits for them, and re-layouts  12.4 us (3%)
    pallas_call x12, Pallas kernels, call(): pl.pallas_call(kernel, in_specs=in_specs, out_shape=tuple((jax.ShapeDtype...  105 us
    ppermute x32, waiting for transfers between devices, over_side(): return lax.ppermute(block, 'fsdp', [(f, f ^ 1) for f in range(8)])  78.2 us
    ppermute x54, starting transfers between devices, swap_seq(): return lax.ppermute(values, 'seq', [(s, s ^ bit) for s in range(4)])  42.2 us
    ppermute x54, waiting for transfers between devices, swap_seq(): return lax.ppermute(values, 'seq', [(s, s ^ bit) for s in range(4)])  38.8 us
    ppermute x24, waiting for transfers between devices, over_line(): return lax.ppermute(block, 'fsdp', moves)  35.2 us
    ppermute x32, starting transfers between devices, over_side(): return lax.ppermute(block, 'fsdp', [(f, f ^ 1) for f in range(8)])  32.1 us
    ppermute x24, starting transfers between devices, over_line(): return lax.ppermute(block, 'fsdp', moves)  29.1 us
  transfers between devices with their start and end apart: 116, of which 59 were waited for; matrix products, arithmetic and copies ran while one was open for 4% of the time, Pallas kernels for 8%

profile of v5, /device:TPU:0, one launch (start us, length us, event | category | flops | bytes accessed | tf_op | source)
XLA Modules:
  0.0 414.4 jit_solution(17523092581013366072)
XLA Ops:
  11.8 5.9 %collective-permute-start.8 = (bf16[72,768]{1,0:T(8,128)(2,1)S(1)}, bf16[72,768]{1,0:T(8,128)(2,1)S(1)}, u32[]{:S(2)}, u32[]{:S(2)}) collective-permute-start(bf16[72,768]{1,0:T(8,128)(2,1)S(1)} %get-tuple-element.326), channel_id=1, source_target_pairs={{0,2},{1,3},{2,0},{3,1},{4,6},{5,7},{6,4},{7,5},{8,10},{9,11},{10,... | collective-permute-start | bytes 331784 | tf_op jit(solution)/shard_map/ppermute | solution.py:35
  63.6 11.1 %attend.2 = (bf16[1024,576]{1,0:T(8,128)(2,1)}, bf16[1024,192]{1,0:T(8,128)(2,1)}, f32[1024,3]{1,0:T(8,128)}, bf16[2,256,768]{2,1,0:T(8,128)(2,1)}, bf16[2,256,768]{2,1,0:T(8,128)(2,1)}) custom-call(s32[9]{0:T(128)} %concatenate.40.place_ref, s32[1024,1]{1,0:T(8,128)} %copy.33.first_ref, bf16[120,768]{1,0:T(8,128)(2,1)} %copy-done.7, ...), custom_call_target="tpu_custom_call" | custom-call | flops 10000000000 | bytes 30000000 | tf_op jit(solution)/shard_map/attend/pallas_call | solution.py:238
  83.8 8.0 %collective-permute-done.28.refs_4_ = bf16[120,768]{1,0:T(8,128)(2,1)S(1)} collective-permute-done((bf16[120,768]{1,0:T(8,128)(2,1)S(1)}, bf16[120,768]{1,0:T(8,128)(2,1)S(1)}, u32[]{:S(2)}, u32[]{:S(2)}) %collective-permute-start.28) | collective-permute-done | bytes 184352 | tf_op jit(solution)/shard_map/ppermute | solution.py:82
  99.0 8.9 %collective-permute-done.32.refs_5_ = bf16[120,768]{1,0:T(8,128)(2,1)S(1)} collective-permute-done((bf16[120,768]{1,0:T(8,128)(2,1)S(1)}, bf16[120,768]{1,0:T(8,128)(2,1)S(1)}, u32[]{:S(2)}, u32[]{:S(2)}) %collective-permute-start.32) | collective-permute-done | bytes 184352 | tf_op jit(solution)/shard_map/ppermute | solution.py:82
  110.5 5.9 %feed.2 = (bf16[2,256,768]{2,1,0:T(8,128)(2,1)}, bf16[2,256,768]{2,1,0:T(8,128)(2,1)}) custom-call(s32[9]{0:T(128)} %concatenate.40.place_ref, bf16[192,768]{1,0:T(8,128)(2,1)} %copy-done.19, bf16[192,768]{1,0:T(8,128)(2,1)} %collective-permute-done.17.refs_1_, bf16[192,768]{1,0:T(8,128)(2,1)} %copy-done.66, bf16[192,768]{1,0:T(8,128)(2,1)} %copy-done.68, ...), custom_call_target="tpu_custom_call" | custom-call | flops 5000000000 | bytes 15000000 | tf_op jit(solution)/shard_map/feed/pallas_call | solution.py:238
  125.2 8.6 %collective-permute-done.38.refs_6_ = bf16[120,768]{1,0:T(8,128)(2,1)S(1)} collective-permute-done((bf16[120,768]{1,0:T(8,128)(2,1)S(1)}, bf16[120,768]{1,0:T(8,128)(2,1)S(1)}, u32[]{:S(2)}, u32[]{:S(2)}) %collective-permute-start.38) | collective-permute-done | bytes 184352 | tf_op jit(solution)/shard_map/ppermute | solution.py:82
  140.1 9.3 %collective-permute-done.42.refs_7_ = bf16[120,768]{1,0:T(8,128)(2,1)S(1)} collective-permute-done((bf16[120,768]{1,0:T(8,128)(2,1)S(1)}, bf16[120,768]{1,0:T(8,128)(2,1)S(1)}, u32[]{:S(2)}, u32[]{:S(2)}) %collective-permute-start.42) | collective-permute-done | bytes 184352 | tf_op jit(solution)/shard_map/ppermute | solution.py:82
  152.0 11.0 %attend.3 = (bf16[1024,576]{1,0:T(8,128)(2,1)}, bf16[1024,192]{1,0:T(8,128)(2,1)}, f32[1024,3]{1,0:T(8,128)}, bf16[2,256,768]{2,1,0:T(8,128)(2,1)}, bf16[2,256,768]{2,1,0:T(8,128)(2,1)}) custom-call(s32[9]{0:T(128)} %concatenate.40.place_ref, s32[1024,1]{1,0:T(8,128)} %copy.33.first_ref, bf16[120,768]{1,0:T(8,128)(2,1)} %copy-done.34, ...), custom_call_target="tpu_custom_call" | custom-call | flops 10000000000 | bytes 30000000 | tf_op jit(solution)/shard_map/attend/pallas_call | solution.py:238
  169.2 7.1 %collective-permute-done.50.refs_6_ = bf16[192,768]{1,0:T(8,128)(2,1)S(1)} collective-permute-done((bf16[192,768]{1,0:T(8,128)(2,1)S(1)}, bf16[192,768]{1,0:T(8,128)(2,1)S(1)}, u32[]{:S(2)}, u32[]{:S(2)}) %collective-permute-start.50) | collective-permute-done | bytes 294944 | tf_op jit(solution)/shard_map/ppermute | solution.py:82
  181.5 6.6 %collective-permute-done.52.refs_7_ = bf16[192,768]{1,0:T(8,128)(2,1)S(1)} collective-permute-done((bf16[192,768]{1,0:T(8,128)(2,1)S(1)}, bf16[192,768]{1,0:T(8,128)(2,1)S(1)}, u32[]{:S(2)}, u32[]{:S(2)}) %collective-permute-start.52) | collective-permute-done | bytes 294944 | tf_op jit(solution)/shard_map/ppermute | solution.py:82
  191.6 8.8 %feed_back.2 = (bf16[1024,768]{1,0:T(8,128)(2,1)}, bf16[1024,768]{1,0:T(8,128)(2,1)}, bf16[2,256,768]{2,1,0:T(8,128)(2,1)}, bf16[2,256,768]{2,1,0:T(8,128)(2,1)}) custom-call(s32[9]{0:T(128)} %concatenate.40.place_ref, bf16[192,768]{1,0:T(8,128)(2,1)} %copy-done.20, bf16[192,768]{1,0:T(8,128)(2,1)} %copy-done.74, bf16[192,768]{1,0:T(8,128)(2,1)} %copy-done.77, ...), custom_call_target="tpu_custom_call" | custom-call | flops 8000000000 | bytes 24000000 | tf_op jit(solution)/shard_map/feed_back/pallas_call | solution.py:238
  205.7 6.8 %feed_sum.2 = (bf16[192,768]{1,0:T(8,128)(2,1)}, bf16[192,768]{1,0:T(8,128)(2,1)}, bf16[192,768]{1,0:T(8,128)(2,1)}, bf16[192,768]{1,0:T(8,128)(2,1)}, bf16[192,...) custom-call(s32[9]{0:T(128)} %concatenate.40.place_ref, ...), custom_call_target="tpu_custom_call" | custom-call | flops 6000000000 | bytes 18000000 | tf_op jit(solution)/shard_map/feed_sum/pallas_call | solution.py:238
  218.5 5.9 %feed.3 = (bf16[2,256,768]{2,1,0:T(8,128)(2,1)}, bf16[2,256,768]{2,1,0:T(8,128)(2,1)}) custom-call(s32[9]{0:T(128)} %concatenate.40.place_ref, bf16[192,768]{1,0:T(8,128)(2,1)} %copy-done.20, bf16[192,768]{1,0:T(8,128)(2,1)} %copy-done.74, bf16[192,768]{1,0:T(8,128)(2,1)} %copy-done.77, bf16[192,768]{1,0:T(8,128)(2,1)} %copy-done.80, ...), custom_call_target="tpu_custom_call" | custom-call | flops 5000000000 | bytes 15000000 | tf_op jit(solution)/shard_map/feed/pallas_call | solution.py:238
  229.7 14.6 %attend_back.2 = (bf16[1024,576]{1,0:T(8,128)(2,1)}, bf16[2,256,768]{2,1,0:T(8,128)(2,1)}, bf16[2,256,768]{2,1,0:T(8,128)(2,1)}) custom-call(s32[9]{0:T(128)} %concatenate.40.place_ref, s32[1024,1]{1,0:T(8,128)} %copy.33.first_ref, bf16[1024,576]{1,0:T(8,128)(2,1)} %get-tuple-element.183.mixed_ref, f32[1024,3]{1,0:T(8,128)} %get-tuple-element.184.total_ref, ...), custom_call_target="tpu_custom_call" | custom-call | flops 14000000000 | bytes 42000000 | tf_op jit(solution)/shard_map/attend_back/pallas_call | solution.py:238
  250.2 5.3 %attend_sum.2 = (bf16[120,768]{1,0:T(8,128)(2,1)}, bf16[120,768]{1,0:T(8,128)(2,1)}, bf16[120,768]{1,0:T(8,128)(2,1)}, bf16[120,768]{1,0:T(8,128)(2,1)}, bf16[12...) custom-call(s32[9]{0:T(128)} %concatenate.40.place_ref, ...), custom_call_target="tpu_custom_call" | custom-call | flops 5000000000 | bytes 15000000 | tf_op jit(solution)/shard_map/attend_sum/pallas_call | solution.py:238
  264.4 9.1 %collective-permute-done.69 = bf16[120,768]{1,0:T(8,128)(2,1)S(1)} collective-permute-done((bf16[120,768]{1,0:T(8,128)(2,1)S(1)}, bf16[120,768]{1,0:T(8,128)(2,1)S(1)}, u32[]{:S(2)}, u32[]{:S(2)}) %collective-permute-start.69) | collective-permute-done | bytes 184352 | tf_op jit(solution)/shard_map/ppermute | solution.py:82
  276.1 8.9 %feed_back.3 = (bf16[1024,768]{1,0:T(8,128)(2,1)}, bf16[1024,768]{1,0:T(8,128)(2,1)}, bf16[2,256,768]{2,1,0:T(8,128)(2,1)}, bf16[2,256,768]{2,1,0:T(8,128)(2,1)}) custom-call(s32[9]{0:T(128)} %concatenate.40.place_ref, bf16[192,768]{1,0:T(8,128)(2,1)} %copy-done.19, bf16[192,768]{1,0:T(8,128)(2,1)} %collective-permute-done.17.refs_1_, ...), custom_call_target="tpu_custom_call" | custom-call | flops 8000000000 | bytes 24000000 | tf_op jit(solution)/shard_map/feed_back/pallas_call | solution.py:238
  293.3 6.8 %feed_sum.3 = (bf16[192,768]{1,0:T(8,128)(2,1)}, bf16[192,768]{1,0:T(8,128)(2,1)}, bf16[192,768]{1,0:T(8,128)(2,1)}, bf16[192,768]{1,0:T(8,128)(2,1)}, bf16[192,...) custom-call(s32[9]{0:T(128)} %concatenate.40.place_ref, ...), custom_call_target="tpu_custom_call" | custom-call | flops 6000000000 | bytes 18000000 | tf_op jit(solution)/shard_map/feed_sum/pallas_call | solution.py:238
  308.3 4.9 %collective-permute-done.81 = bf16[120,768]{1,0:T(8,128)(2,1)S(1)} collective-permute-done((bf16[120,768]{1,0:T(8,128)(2,1)S(1)}, bf16[120,768]{1,0:T(8,128)(2,1)S(1)}, u32[]{:S(2)}, u32[]{:S(2)}) %collective-permute-start.81) | collective-permute-done | bytes 184352 | tf_op jit(solution)/shard_map/ppermute | solution.py:78
  319.2 14.3 %attend_back.3 = (bf16[1024,576]{1,0:T(8,128)(2,1)}, bf16[2,256,768]{2,1,0:T(8,128)(2,1)}, bf16[2,256,768]{2,1,0:T(8,128)(2,1)}) custom-call(s32[9]{0:T(128)} %concatenate.40.place_ref, s32[1024,1]{1,0:T(8,128)} %copy.33.first_ref, bf16[1024,576]{1,0:T(8,128)(2,1)} %get-tuple-element.221.mixed_ref, f32[1024,3]{1,0:T(8,128)} %get-tuple-element.222.total_ref, ...), custom_call_target="tpu_custom_call" | custom-call | flops 14000000000 | bytes 42000000 | tf_op jit(solution)/shard_map/attend_back/pallas_call | solution.py:238
  339.3 5.3 %attend_sum.3 = (bf16[120,768]{1,0:T(8,128)(2,1)}, bf16[120,768]{1,0:T(8,128)(2,1)}, bf16[120,768]{1,0:T(8,128)(2,1)}, bf16[120,768]{1,0:T(8,128)(2,1)}, bf16[12...) custom-call(s32[9]{0:T(128)} %concatenate.40.place_ref, ...), custom_call_target="tpu_custom_call" | custom-call | flops 5000000000 | bytes 15000000 | tf_op jit(solution)/shard_map/attend_sum/pallas_call | solution.py:238
  348.9 3.5 collective-permute-done.90
  384.9 3.7 collective-permute-done.105
  404.1 5.2 %collective-permute-start.115 = (f32[6144]{0:T(1024)S(1)}, f32[6144]{0:T(1024)S(1)}, u32[]{:S(2)}, u32[]{:S(2)}) collective-permute-start(f32[6144]{0:T(1024)S(1)} %add.416), channel_id=1, source_target_pairs={{0,16},{4,20},{8,24},{12,28},{16,0},{20,4},{24,8},{28,12},{1,17},{... | collective-permute-start | bytes 73736 | tf_op jit(solution)/shard_map/ppermute | solution.py:736
  (570 shorter events, 226.3 us)
Async XLA Ops:
  19.5 23.6 %collective-permute-start.14 = (bf16[256,768]{1,0:T(8,128)(2,1)S(1)}, bf16[256,768]{1,0:T(8,128)(2,1)S(1)}, u32[]{:S(2)}, u32[]{:S(2)}) collective-permute-start(bf16[256,768]{1,0:T(8,128)(2,1)S(1)} %copy-done), channel_id=1, source_target_pairs={{0,2},{1,3},{2,0},{3,1},{4,6},{5,7},{6,4},{7,5},{8,10},{9,11},{10,... | collective-permute-start | bytes 1179656 | tf_op jit(solution)/shard_map/ppermute | solution.py:35
  43.1 11.9 %collective-permute-start.15 = (bf16[256,768]{1,0:T(8,128)(2,1)S(1)}, bf16[256,768]{1,0:T(8,128)(2,1)S(1)}, u32[]{:S(2)}, u32[]{:S(2)}) collective-permute-start(bf16[256,768]{1,0:T(8,128)(2,1)S(1)} %copy-done), channel_id=1, source_target_pairs={{0,1},{1,0},{2,3},{3,2},{4,5},{5,4},{6,7},{7,6},{8,9},{9,8},{10,11... | collective-permute-start | bytes 1179656 | tf_op jit(solution)/shard_map/ppermute | solution.py:35
  43.2 14.8 %collective-permute-start.21 = (bf16[256,768]{1,0:T(8,128)(2,1)S(1)}, bf16[256,768]{1,0:T(8,128)(2,1)}, u32[]{:S(2)}, u32[]{:S(2)}) collective-permute-start(bf16[256,768]{1,0:T(8,128)(2,1)S(1)} %fusion.19.refs_12_.refs_4_), channel_id=1, source_target_pairs={{0,2},{1,3},{2,0},{3,1},{4,6},{5,7},{6,4},{7,5},{8,10},{9,11},{10,... | collective-permute-start | bytes 1179656 | tf_op jit(solution)/shard_map/ppermute | solution.py:35
  45.7 15.4 %collective-permute-start.22 = (bf16[256,768]{1,0:T(8,128)(2,1)S(1)}, bf16[256,768]{1,0:T(8,128)(2,1)}, u32[]{:S(2)}, u32[]{:S(2)}) collective-permute-start(bf16[256,768]{1,0:T(8,128)(2,1)S(1)} %fusion.19.refs_12_.refs_4_), channel_id=1, source_target_pairs={{0,1},{1,0},{2,3},{3,2},{4,5},{5,4},{6,7},{7,6},{8,9},{9,8},{10,11... | collective-permute-start | bytes 1179656 | tf_op jit(solution)/shard_map/ppermute | solution.py:35
  78.6 15.2 %collective-permute-start.25 = (bf16[256,768]{1,0:T(8,128)(2,1)S(1)}, bf16[256,768]{1,0:T(8,128)(2,1)S(1)}, u32[]{:S(2)}, u32[]{:S(2)}) collective-permute-start(bf16[256,768]{1,0:T(8,128)(2,1)S(1)} %fusion.38), channel_id=1, source_target_pairs={{0,2},{1,3},{2,0},{3,1},{4,6},{5,7},{6,4},{7,5},{8,10},{9,11},{10,... | collective-permute-start | bytes 1179656 | tf_op jit(solution)/shard_map/ppermute | solution.py:35
  78.8 15.0 %collective-permute-start.26 = (bf16[192,768]{1,0:T(8,128)(2,1)S(1)}, bf16[192,768]{1,0:T(8,128)(2,1)S(1)}, u32[]{:S(2)}, u32[]{:S(2)}) collective-permute-start(bf16[192,768]{1,0:T(8,128)(2,1)S(1)} %collective-permute-done.20.refs_2_), channel_id=1, source_target_pairs={{0,4},{4,0},{8,12},{12,8},{16,20},{20,16},{24,28},{28,24},{1,5},{5... | collective-permute-start | bytes 884744 | tf_op jit(solution)/shard_map/ppermute | solution.py:82
  80.2 13.6 %collective-permute-start.27 = (bf16[192,768]{1,0:T(8,128)(2,1)S(1)}, bf16[192,768]{1,0:T(8,128)(2,1)S(1)}, u32[]{:S(2)}, u32[]{:S(2)}) collective-permute-start(bf16[192,768]{1,0:T(8,128)(2,1)S(1)} %collective-permute-done.20.refs_2_), channel_id=1, source_target_pairs={{0,8},{4,12},{8,24},{12,28},{16,0},{20,4},{24,16},{28,20},{1,9},{5... | collective-permute-start | bytes 884744 | tf_op jit(solution)/shard_map/ppermute | solution.py:78
  81.9 11.9 %collective-permute-start.29 = (bf16[120,768]{1,0:T(8,128)(2,1)S(1)}, bf16[120,768]{1,0:T(8,128)(2,1)S(1)}, u32[]{:S(2)}, u32[]{:S(2)}) collective-permute-start(bf16[120,768]{1,0:T(8,128)(2,1)S(1)} %pad_maximum_fusion.8.refs_0_), channel_id=1, source_target_pairs={{0,8},{4,12},{8,24},{12,28},{16,0},{20,4},{24,16},{28,20},{1,9},{5... | collective-permute-start | bytes 552968 | tf_op jit(solution)/shard_map/ppermute | solution.py:78
  94.8 13.1 %collective-permute-start.31 = (bf16[256,768]{1,0:T(8,128)(2,1)S(1)}, bf16[256,768]{1,0:T(8,128)(2,1)S(1)}, u32[]{:S(2)}, u32[]{:S(2)}) collective-permute-start(bf16[256,768]{1,0:T(8,128)(2,1)S(1)} %add_convert_fusion.2.refs_8_.refs_0_), channel_id=1, source_target_pairs={{0,2},{1,3},{2,0},{3,1},{4,6},{5,7},{6,4},{7,5},{8,10},{9,11},{10,... | collective-permute-start | bytes 1179656 | tf_op jit(solution)/shard_map/ppermute | solution.py:35
  96.6 11.3 %collective-permute-start.30 = (bf16[192,768]{1,0:T(8,128)(2,1)S(1)}, bf16[192,768]{1,0:T(8,128)(2,1)S(1)}, u32[]{:S(2)}, u32[]{:S(2)}) collective-permute-start(bf16[192,768]{1,0:T(8,128)(2,1)S(1)} %collective-permute-done.27.refs_3_), channel_id=1, source_target_pairs={{0,4},{4,0},{8,12},{12,8},{16,20},{20,16},{24,28},{28,24},{1,5},{5... | collective-permute-start | bytes 884744 | tf_op jit(solution)/shard_map/ppermute | solution.py:82
  120.3 15.5 %collective-permute-start.37 = (bf16[256,768]{1,0:T(8,128)(2,1)S(1)}, bf16[256,768]{1,0:T(8,128)(2,1)S(1)}, u32[]{:S(2)}, u32[]{:S(2)}) collective-permute-start(bf16[256,768]{1,0:T(8,128)(2,1)S(1)} %fusion.39), channel_id=1, source_target_pairs={{0,2},{1,3},{2,0},{3,1},{4,6},{5,7},{6,4},{7,5},{8,10},{9,11},{10,... | collective-permute-start | bytes 1179656 | tf_op jit(solution)/shard_map/ppermute | solution.py:35
  121.0 14.1 %collective-permute-start.40 = (bf16[192,768]{1,0:T(8,128)(2,1)S(1)}, bf16[192,768]{1,0:T(8,128)(2,1)S(1)}, u32[]{:S(2)}, u32[]{:S(2)}) collective-permute-start(bf16[192,768]{1,0:T(8,128)(2,1)S(1)} %pad_maximum_fusion.3.refs_0_), channel_id=1, source_target_pairs={{0,4},{4,0},{8,12},{12,8},{16,20},{20,16},{24,28},{28,24},{1,5},{5... | collective-permute-start | bytes 884744 | tf_op jit(solution)/shard_map/ppermute | solution.py:82
  121.8 13.3 %collective-permute-start.41 = (bf16[192,768]{1,0:T(8,128)(2,1)S(1)}, bf16[192,768]{1,0:T(8,128)(2,1)S(1)}, u32[]{:S(2)}, u32[]{:S(2)}) collective-permute-start(bf16[192,768]{1,0:T(8,128)(2,1)S(1)} %pad_maximum_fusion.3.refs_0_), channel_id=1, source_target_pairs={{0,8},{4,12},{8,24},{12,28},{16,0},{20,4},{24,16},{28,20},{1,9},{5... | collective-permute-start | bytes 884744 | tf_op jit(solution)/shard_map/ppermute | solution.py:78
  122.0 11.8 %collective-permute-start.38 = (bf16[120,768]{1,0:T(8,128)(2,1)S(1)}, bf16[120,768]{1,0:T(8,128)(2,1)S(1)}, u32[]{:S(2)}, u32[]{:S(2)}) collective-permute-start(bf16[120,768]{1,0:T(8,128)(2,1)S(1)} %collective-permute-done.33.refs_2_), channel_id=1, source_target_pairs={{0,4},{4,0},{8,12},{12,8},{16,20},{20,16},{24,28},{28,24},{1,5},{5... | collective-permute-start | bytes 552968 | tf_op jit(solution)/shard_map/ppermute | solution.py:82
  123.3 11.8 %collective-permute-start.39 = (bf16[120,768]{1,0:T(8,128)(2,1)S(1)}, bf16[120,768]{1,0:T(8,128)(2,1)S(1)}, u32[]{:S(2)}, u32[]{:S(2)}) collective-permute-start(bf16[120,768]{1,0:T(8,128)(2,1)S(1)} %collective-permute-done.33.refs_2_), channel_id=1, source_target_pairs={{0,8},{4,12},{8,24},{12,28},{16,0},{20,4},{24,16},{28,20},{1,9},{5... | collective-permute-start | bytes 552968 | tf_op jit(solution)/shard_map/ppermute | solution.py:78
  136.5 12.8 %collective-permute-start.43 = (bf16[256,768]{1,0:T(8,128)(2,1)S(1)}, bf16[256,768]{1,0:T(8,128)(2,1)S(1)}, u32[]{:S(2)}, u32[]{:S(2)}) collective-permute-start(bf16[256,768]{1,0:T(8,128)(2,1)S(1)} %add_convert_fusion.1.refs_8_.refs_0_), channel_id=1, source_target_pairs={{0,2},{1,3},{2,0},{3,1},{4,6},{5,7},{6,4},{7,5},{8,10},{9,11},{10,... | collective-permute-start | bytes 1179656 | tf_op jit(solution)/shard_map/ppermute | solution.py:35
  166.9 11.7 %collective-permute-start.49 = (bf16[256,768]{1,0:T(8,128)(2,1)S(1)}, bf16[256,768]{1,0:T(8,128)(2,1)S(1)}, u32[]{:S(2)}, u32[]{:S(2)}) collective-permute-start(bf16[256,768]{1,0:T(8,128)(2,1)S(1)} %fusion.40), channel_id=1, source_target_pairs={{0,2},{1,3},{2,0},{3,1},{4,6},{5,7},{6,4},{7,5},{8,10},{9,11},{10,... | collective-permute-start | bytes 1179656 | tf_op jit(solution)/shard_map/ppermute | solution.py:35
  260.2 13.3 %collective-permute-start.66 = (bf16[256,768]{1,0:T(8,128)(2,1)S(1)}, bf16[256,768]{1,0:T(8,128)(2,1)S(1)}, u32[]{:S(2)}, u32[]{:S(2)}) collective-permute-start(bf16[256,768]{1,0:T(8,128)(2,1)S(1)} %get-tuple-element.303.refs_12_.refs_4_), channel_id=1, source_target_pairs={{0,2},{1,3},{2,0},{3,1},{4,6},{5,7},{6,4},{7,5},{8,10},{9,11},{10,... | collective-permute-start | bytes 1179656 | tf_op jit(solution)/shard_map/ppermute | solution.py:35
  261.3 12.2 %collective-permute-start.68 = (bf16[192,768]{1,0:T(8,128)(2,1)S(1)}, bf16[192,768]{1,0:T(8,128)(2,1)S(1)}, u32[]{:S(2)}, u32[]{:S(2)}) collective-permute-start(bf16[192,768]{1,0:T(8,128)(2,1)S(1)} %add_convert_fusion.7), channel_id=1, source_target_pairs={{0,8},{4,12},{8,24},{12,28},{16,0},{20,4},{24,16},{28,20},{1,9},{5... | collective-permute-start | bytes 884744 | tf_op jit(solution)/shard_map/ppermute | solution.py:78
  287.8 15.6 %collective-permute-start.73 = (bf16[256,768]{1,0:T(8,128)(2,1)S(1)}, bf16[256,768]{1,0:T(8,128)(2,1)S(1)}, u32[]{:S(2)}, u32[]{:S(2)}) collective-permute-start(bf16[256,768]{1,0:T(8,128)(2,1)S(1)} %fusion.43), channel_id=1, source_target_pairs={{0,2},{1,3},{2,0},{3,1},{4,6},{5,7},{6,4},{7,5},{8,10},{9,11},{10,... | collective-permute-start | bytes 1179656 | tf_op jit(solution)/shard_map/ppermute | solution.py:35
  304.2 12.2 %collective-permute-start.78 = (bf16[256,768]{1,0:T(8,128)(2,1)S(1)}, bf16[256,768]{1,0:T(8,128)(2,1)}, u32[]{:S(2)}, u32[]{:S(2)}) collective-permute-start(bf16[256,768]{1,0:T(8,128)(2,1)S(1)} %get-tuple-element.301.refs_8_.refs_1_), channel_id=1, source_target_pairs={{0,2},{1,3},{2,0},{3,1},{4,6},{5,7},{6,4},{7,5},{8,10},{9,11},{10,... | collective-permute-start | bytes 1179656 | tf_op jit(solution)/shard_map/ppermute | solution.py:35
  333.8 31.0 %collective-permute-start.95 = (bf16[192,768]{1,0:T(8,128)(2,1)}, bf16[192,768]{1,0:T(8,128)(2,1)S(1)}, u32[]{:S(2)}, u32[]{:S(2)}) collective-permute-start(bf16[192,768]{1,0:T(8,128)(2,1)} %get-tuple-element.250), channel_id=1, source_target_pairs={{0,4},{4,0},{8,12},{12,8},{16,20},{20,16},{24,28},{28,24},{1,5},{5... | collective-permute-start | bytes 884744 | tf_op jit(solution)/shard_map/ppermute | solution.py:82
  336.4 24.4 %collective-permute-start.85 = (bf16[256,768]{1,0:T(8,128)(2,1)S(1)}, bf16[256,768]{1,0:T(8,128)(2,1)S(1)}, u32[]{:S(2)}, u32[]{:S(2)}) collective-permute-start(bf16[256,768]{1,0:T(8,128)(2,1)S(1)} %fusion.44), channel_id=1, source_target_pairs={{0,2},{1,3},{2,0},{3,1},{4,6},{5,7},{6,4},{7,5},{8,10},{9,11},{10,... | collective-permute-start | bytes 1179656 | tf_op jit(solution)/shard_map/ppermute | solution.py:35
  390.2 13.9 %collective-permute-start.114 = (bf16[24,768]{1,0:T(8,128)(2,1)S(1)}, bf16[24,768]{1,0:T(8,128)(2,1)S(1)}, u32[]{:S(2)}, u32[]{:S(2)}) collective-permute-start(bf16[24,768]{1,0:T(8,128)(2,1)S(1)} %slice.250), channel_id=1, source_target_pairs={{0,0},{1,8},{2,16},{3,24},{4,4},{5,12},{6,20},{7,28},{8,1},{9,9},{... | collective-permute-start | bytes 110600 | tf_op jit(solution)/shard_map/ppermute | solution.py:136
  (190 other events, 1397.9 us)
